TPU v7x, 32 devices: a whole 2x2x4 slice. The times are simulated.
32 devices in a mesh: seq: 4 (over y, x), fsdp: 8 (over z, core).
Axes of the slice: x: 2, y: 2, z: 4, core: 2. Of those that a mesh axis runs over, the one named last changes fastest.
Arguments:
- block_input: bfloat16 [8, 2048, 1024], P('fsdp', 'seq'), may hold values from -6 to 6
- norm_gain_a: float32 [1024], P('fsdp'), may hold values from 0.1 to 1.9
- weight_qkv: float32 [1024, 3072], P('fsdp'), may hold values from -0.1875 to 0.1875
- weight_out: float32 [1024, 1024], P('fsdp'), may hold values from -3 to 3
- norm_gain_b: float32 [1024], P('fsdp'), may hold values from 0.1 to 1.9
- weight_gate_up: float32 [1024, 8192], P('fsdp'), may hold values from -0.1875 to 0.1875
- weight_down: float32 [1024, 4096], P('fsdp'), may hold values from -0.09375 to 0.09375
- cotangent: bfloat16 [8, 2048, 1024], P('fsdp', 'seq'), may hold values from -6 to 6
- permutation: int32 [8, 2048], P('fsdp'), may hold values from 0 to 2047, each once within a row
- lengths: int32 [8, 3], P('fsdp'), may hold values from 256 to 1024, as said below
- offsets: int32 [8, 3], P('fsdp'), may hold values from 0 to 1792, as said below
Outputs:
- block_output: bfloat16 [8, 2048, 1024], P('fsdp', 'seq')
- grad_input: bfloat16 [8, 2048, 1024], P('fsdp', 'seq')
- grad_gain_a: float32 [1024], P('fsdp')
- grad_qkv: float32 [1024, 3072], P('fsdp')
- grad_out: float32 [1024, 1024], P('fsdp')
- grad_gain_b: float32 [1024], P('fsdp')
- grad_gate_up: float32 [1024, 8192], P('fsdp')
- grad_down: float32 [1024, 4096], P('fsdp')
Inputs may be any that keep to these rules, and one draw needn't show every extreme that they name: A group's 3 lengths sum to 2048, and its longest is exactly 1024. offsets[g, k] is the sum of lengths[g, i] over i < k, so that a group's sequences tile its positions.
All inputs are finite; a program needn't handle non-finite values.
Results may differ from a plain program's by a relative error of at most 0.02.
Values may be sent and summed in bfloat16 or wider, within the bound.
A program may use at most 256 MiB of HBM per device.

v0:
```python
import jax
import jax.numpy as jnp
from jax import lax
from jax.sharding import PartitionSpec as P

HEADS = 16
HEAD_DIM = 64


epsilon = 1e-05


def rms_scale(values):
    return lax.rsqrt(jnp.mean(values * values, axis=-1, keepdims=True) + epsilon)


def norm_backward(values, inv_scale, grad_normed, gain):
    scaled = grad_normed * gain
    gain_grad = jnp.sum(grad_normed * values * inv_scale, axis=0)
    input_grad = inv_scale * scaled - values * inv_scale**3 * jnp.mean(
        values * scaled, axis=-1, keepdims=True
    )
    return (input_grad, gain_grad)


def block_mask(seg_query, pos_query, segment, position):
    return (seg_query[:, None] == segment[None, :]) & (position[None, :] <= pos_query[:, None])


def on_device(
    block_input,
    norm_gain_a,
    weight_qkv,
    weight_out,
    norm_gain_b,
    weight_gate_up,
    weight_down,
    cotangent,
    permutation,
    lengths,
    offsets,
):
    seq_count = lax.axis_size("seq")
    row_count = block_input.shape[1]
    model_width = block_input.shape[2]
    group_len = row_count * seq_count
    head_local = HEADS // seq_count
    score_scale = HEAD_DIM ** (-0.5)
    blk_rows = min(512, group_len)
    block_count = group_len // blk_rows
    inputs = block_input[0].astype(jnp.float32)
    gain_a, full_qkv, full_out = (
        lax.all_gather(norm_gain_a.astype(jnp.bfloat16), "fsdp", axis=0, tiled=True),
        lax.all_gather(weight_qkv.astype(jnp.bfloat16), "fsdp", axis=0, tiled=True),
        lax.all_gather(weight_out.astype(jnp.bfloat16), "fsdp", axis=0, tiled=True),
    )
    inv_first = rms_scale(inputs)
    normed_a = (inputs * inv_first * gain_a.astype(jnp.float32)).astype(jnp.bfloat16)
    qkv_rows = jnp.dot(normed_a, full_qkv, preferred_element_type=jnp.float32).astype(jnp.bfloat16)
    head_rows = lax.all_to_all(
        qkv_rows.reshape(row_count, 3, seq_count, -1),
        "seq",
        split_axis=2,
        concat_axis=0,
        tiled=True,
    )
    head_rows = head_rows.reshape(group_len, 3, head_local, HEAD_DIM)
    position = jnp.arange(group_len, dtype=jnp.int32)
    dealt_pos = permutation[0]
    inverse = jnp.zeros((group_len,), jnp.int32).at[dealt_pos].set(position)
    ordered = head_rows[inverse]
    seq_starts = offsets[0]
    seq_lengths = lengths[0]
    inside = (position[:, None] >= seq_starts[None, :]) & (
        position[:, None] < seq_starts[None, :] + seq_lengths[None, :]
    )
    segment = jnp.sum(
        inside.astype(jnp.int32) * jnp.arange(seq_lengths.shape[0], dtype=jnp.int32)[None, :],
        axis=1,
    )
    queries = ordered[:, 0]
    key_rows = ordered[:, 1]
    values = ordered[:, 2]

    def forward_block(block_item):
        query_blk, seg_blk, pos_blk = block_item
        scores = (
            jnp.einsum("qhd,khd->hqk", query_blk, key_rows, preferred_element_type=jnp.float32)
            * score_scale
        )
        allowed = block_mask(seg_blk, pos_blk, segment, position)
        scores = jnp.where(allowed[None], scores, -1e30)
        row_top = jnp.max(scores, axis=-1, keepdims=True)
        exponent = jnp.exp(scores - row_top)
        row_total = jnp.sum(exponent, axis=-1, keepdims=True)
        weights_low = (exponent / row_total).astype(jnp.bfloat16)
        attended = jnp.einsum(
            "hqk,khd->qhd", weights_low, values, preferred_element_type=jnp.float32
        )
        return (attended.astype(jnp.bfloat16), (row_top + jnp.log(row_total))[:, :, 0])

    query_blocks = queries.reshape(block_count, blk_rows, head_local, HEAD_DIM)
    seg_blocks = segment.reshape(block_count, blk_rows)
    pos_blocks = position.reshape(block_count, blk_rows)
    attended, log_total = lax.map(forward_block, (query_blocks, seg_blocks, pos_blocks))
    dealt_out = attended.reshape(group_len, -1)[dealt_pos]
    mixed = lax.all_to_all(
        dealt_out.reshape(group_len, 1, -1), "seq", split_axis=0, concat_axis=1, tiled=True
    ).reshape(row_count, model_width)
    hidden = inputs + jnp.dot(mixed, full_out, preferred_element_type=jnp.float32)
    gain_b, full_gate_up, full_down = (
        lax.all_gather(norm_gain_b.astype(jnp.bfloat16), "fsdp", axis=0, tiled=True),
        lax.all_gather(weight_gate_up.astype(jnp.bfloat16), "fsdp", axis=0, tiled=True),
        lax.all_gather(weight_down.astype(jnp.bfloat16), "fsdp", axis=0, tiled=True),
    )
    inv_second = rms_scale(hidden)
    normed_b = (hidden * inv_second * gain_b.astype(jnp.float32)).astype(jnp.bfloat16)
    gate_up = jnp.dot(normed_b, full_gate_up, preferred_element_type=jnp.float32)
    hidden_units = full_gate_up.shape[1] // 2
    gate_part = gate_up[:, :hidden_units]
    up_part = gate_up[:, hidden_units:]
    gate_sigmoid = jax.nn.sigmoid(gate_part)
    gate_silu = gate_part * gate_sigmoid
    activation = (gate_silu * up_part).astype(jnp.bfloat16)
    branch_out = jnp.einsum("rf,df->rd", activation, full_down, preferred_element_type=jnp.float32)
    result_rows = (hidden + branch_out).astype(jnp.bfloat16)
    gain_b, full_gate_up, full_down = (
        lax.all_gather(norm_gain_b.astype(jnp.bfloat16), "fsdp", axis=0, tiled=True),
        lax.all_gather(weight_gate_up.astype(jnp.bfloat16), "fsdp", axis=0, tiled=True),
        lax.all_gather(weight_down.astype(jnp.bfloat16), "fsdp", axis=0, tiled=True),
    )
    out_grad = cotangent[0].astype(jnp.float32)
    out_grad_low = out_grad.astype(jnp.bfloat16)
    grad_down_term = jnp.einsum(
        "rd,rf->df", out_grad_low, activation, preferred_element_type=jnp.float32
    )
    grad_activation = jnp.dot(out_grad_low, full_down, preferred_element_type=jnp.float32)
    grad_gate = grad_activation * up_part * gate_sigmoid * (1.0 + gate_part * (1.0 - gate_sigmoid))
    grad_up = grad_activation * gate_silu
    grad_gate_up = jnp.concatenate([grad_gate, grad_up], axis=1).astype(jnp.bfloat16)
    grad_gate_up_term = jnp.einsum(
        "rd,rf->df", normed_b, grad_gate_up, preferred_element_type=jnp.float32
    )
    grad_normed_b = jnp.einsum(
        "rf,df->rd", grad_gate_up, full_gate_up, preferred_element_type=jnp.float32
    )
    hidden_back, grad_gain_b_term = norm_backward(
        hidden, inv_second, grad_normed_b, gain_b.astype(jnp.float32)
    )
    grad_hidden = out_grad + hidden_back
    gain_a, full_qkv, full_out = (
        lax.all_gather(norm_gain_a.astype(jnp.bfloat16), "fsdp", axis=0, tiled=True),
        lax.all_gather(weight_qkv.astype(jnp.bfloat16), "fsdp", axis=0, tiled=True),
        lax.all_gather(weight_out.astype(jnp.bfloat16), "fsdp", axis=0, tiled=True),
    )
    grad_branch = grad_hidden.astype(jnp.bfloat16)
    grad_out_term = jnp.einsum("rd,re->de", mixed, grad_branch, preferred_element_type=jnp.float32)
    grad_mixed = jnp.einsum(
        "re,de->rd", grad_branch, full_out, preferred_element_type=jnp.float32
    ).astype(jnp.bfloat16)
    grad_heads = lax.all_to_all(
        grad_mixed.reshape(row_count, seq_count, -1), "seq", split_axis=1, concat_axis=0, tiled=True
    )
    grad_ordered = grad_heads.reshape(group_len, head_local, HEAD_DIM)[inverse]
    grad_blocks = grad_ordered.reshape(block_count, blk_rows, head_local, HEAD_DIM)

    def backward_block(carry, block_item):
        key_acc, value_acc = carry
        query_blk, grad_blk, log_blk, seg_blk, pos_blk = block_item
        scores = (
            jnp.einsum("qhd,khd->hqk", query_blk, key_rows, preferred_element_type=jnp.float32)
            * score_scale
        )
        allowed = block_mask(seg_blk, pos_blk, segment, position)
        scores = jnp.where(allowed[None], scores, -1e30)
        probability = jnp.exp(scores - log_blk[:, :, None])
        grad_prob = jnp.einsum("qhd,khd->hqk", grad_blk, values, preferred_element_type=jnp.float32)
        row_delta = jnp.sum(probability * grad_prob, axis=-1, keepdims=True)
        grad_score = (probability * (grad_prob - row_delta)).astype(jnp.bfloat16)
        grad_query = (
            jnp.einsum("hqk,khd->qhd", grad_score, key_rows, preferred_element_type=jnp.float32)
            * score_scale
        )
        key_acc = (
            key_acc
            + jnp.einsum("hqk,qhd->khd", grad_score, query_blk, preferred_element_type=jnp.float32)
            * score_scale
        )
        value_acc = value_acc + jnp.einsum(
            "hqk,qhd->khd",
            probability.astype(jnp.bfloat16),
            grad_blk,
            preferred_element_type=jnp.float32,
        )
        return ((key_acc, value_acc), grad_query.astype(jnp.bfloat16))

    zero_acc = jnp.zeros((group_len, head_local, HEAD_DIM), jnp.float32)
    accumulated, query_grad = lax.scan(
        backward_block,
        (zero_acc, zero_acc),
        (query_blocks, grad_blocks, log_total, seg_blocks, pos_blocks),
    )
    qkv_grad = jnp.stack(
        [
            query_grad.reshape(group_len, -1),
            accumulated[0].reshape(group_len, -1).astype(jnp.bfloat16),
            accumulated[1].reshape(group_len, -1).astype(jnp.bfloat16),
        ],
        axis=1,
    )
    dealt_grad = qkv_grad[dealt_pos]
    rows_grad = lax.all_to_all(
        dealt_grad.reshape(group_len, 3, 1, -1), "seq", split_axis=0, concat_axis=2, tiled=True
    ).reshape(row_count, -1)
    grad_qkv_term = jnp.einsum("rd,re->de", normed_a, rows_grad, preferred_element_type=jnp.float32)
    grad_normed_a = jnp.einsum("re,de->rd", rows_grad, full_qkv, preferred_element_type=jnp.float32)
    input_back, grad_gain_a_term = norm_backward(
        inputs, inv_first, grad_normed_a, gain_a.astype(jnp.float32)
    )
    input_grad = (grad_hidden + input_back).astype(jnp.bfloat16)
    attn_shards = (
        lax.psum_scatter(
            grad_gain_a_term.astype(jnp.bfloat16), "fsdp", scatter_dimension=0, tiled=True
        ).astype(jnp.float32),
        lax.psum_scatter(
            grad_qkv_term.astype(jnp.bfloat16), "fsdp", scatter_dimension=0, tiled=True
        ).astype(jnp.float32),
        lax.psum_scatter(
            grad_out_term.astype(jnp.bfloat16), "fsdp", scatter_dimension=0, tiled=True
        ).astype(jnp.float32),
    )
    mlp_shards = (
        lax.psum_scatter(
            grad_gain_b_term.astype(jnp.bfloat16), "fsdp", scatter_dimension=0, tiled=True
        ).astype(jnp.float32),
        lax.psum_scatter(
            grad_gate_up_term.astype(jnp.bfloat16), "fsdp", scatter_dimension=0, tiled=True
        ).astype(jnp.float32),
        lax.psum_scatter(
            grad_down_term.astype(jnp.bfloat16), "fsdp", scatter_dimension=0, tiled=True
        ).astype(jnp.float32),
    )
    totals = (
        lax.psum(attn_shards[0].astype(jnp.bfloat16), "seq").astype(jnp.float32),
        lax.psum(attn_shards[1].astype(jnp.bfloat16), "seq").astype(jnp.float32),
        lax.psum(attn_shards[2].astype(jnp.bfloat16), "seq").astype(jnp.float32),
        lax.psum(mlp_shards[0].astype(jnp.bfloat16), "seq").astype(jnp.float32),
        lax.psum(mlp_shards[1].astype(jnp.bfloat16), "seq").astype(jnp.float32),
        lax.psum(mlp_shards[2].astype(jnp.bfloat16), "seq").astype(jnp.float32),
    )
    return (
        result_rows[None],
        input_grad[None],
        totals[0],
        totals[1],
        totals[2],
        totals[3],
        totals[4],
        totals[5],
    )


def solution(mesh):
    placed = (
        P("fsdp", "seq", None),
        P("fsdp"),
        P("fsdp", None),
        P("fsdp", None),
        P("fsdp"),
        P("fsdp", None),
        P("fsdp", None),
        P("fsdp", "seq", None),
        P("fsdp", None),
        P("fsdp", None),
        P("fsdp", None),
    )
    return jax.shard_map(
        on_device,
        mesh=mesh,
        in_specs=placed,
        out_specs=(
            P("fsdp", "seq", None),
            P("fsdp", "seq", None),
            P("fsdp"),
            P("fsdp", None),
            P("fsdp", None),
            P("fsdp"),
            P("fsdp", None),
            P("fsdp", None),
        ),
        check_vma=False,
    )
```

profile of v0, /device:TPU:0, one launch (start us, length us, event | category | flops | bytes accessed | tf_op | source)
XLA Modules:
  0.0 1127.4 jit_solution(276207675843231154)
XLA Ops:
  15.4 13.5 %all-gather = bf16[8,1,128]{2,1,0:T(2,128)(2,1)S(1)} all-gather(bf16[1,1,128]{2,1,0:T(2,128)(2,1)S(1)} %convert_bitcast_fusion.3), channel_id=1, replica_groups=mesh['seq'=4,'fsdp'=8] {'fsdp'}, dimensions={0}, use_global_device_ids=true | all-gather | bytes 2304 | tf_op jit(solution)/shard_map/all_gather | solution.py:53
  29.8 47.9 %all-gather.7.cloned.1.call-done = bf16[1024,3072]{1,0:T(8,128)(2,1)} async-done(((bf16[128,3072]{1,0:T(8,128)(2,1)}), bf16[1024,3072]{1,0:T(8,128)(2,1)}) %all-gather.7.cloned.1.call-update) | async-done | bytes 6291472 | tf_op jit(solution)/shard_map/all_gather | solution.py:54
  77.7 7.7 convolution_convert_fusion.2
  102.6 8.2 scatter_custom_fusion
  112.1 23.7 %all-to-all-done = bf16[512,3,4,256]{0,3,1,2:T(8,128)(2,1)S(1)} async-done(((bf16[512,3,4,256]{0,3,1,2:T(8,128)(2,1)}), bf16[512,3,4,256]{0,3,1,2:T(8,128)(2,1)S(1)}, u32[]{:S(2)}, u32[]{:S(2)}) %all-to-all-start) | async-done | bytes 3145760 | tf_op jit(solution)/shard_map/all_to_all | solution.py:60
  140.4 13.1 %reshape.380 = bf16[2048,3,4,64]{3,2,1,0:T(4,128)(2,1)} reshape(bf16[4,512,3,1,256]{4,2,1,0,3:T(4,128)(2,1)} %copy.141) | data formatting | bytes 6291456 | tf_op jit(solution)/shard_map/reshape | solution.py:67
  153.6 23.0 %gather_fusion = bf16[2048,3,4,64]{3,2,1,0:T(4,128)(2,1)} fusion(bf16[2048,3,4,64]{3,2,1,0:T(4,128)(2,1)} %reshape.380, s32[2048]{0:T(1024)S(1)} %fusion.84), kind=kCustom, calls=%fused_computation | custom fusion | bytes 6299648 | tf_op jit(solution)/shard_map/gather | solution.py:71
  191.8 64.2 %while.28 = (s32[]{:T(128)}, bf16[4,512,4,64]{1,3,2,0:T(8,128)(2,1)}, f32[4,4,512]{2,1,0:T(4,128)}, s32[4,512]{1,0:T(4,128)}, s32[2048]{0:T(1024)S(1)}, /*index=...) while((s32[]{:T(128)}, ...), condition=%wide.region_6.7_spmd.clone, body=%wide.region_3.6_spmd.clone.sunk | while | flops 1127348224 | bytes 57233532 | solution.py:105
  264.6 9.1 gather_fusion.1
  282.9 9.8 all-gather.1
  310.1 18.8 %fusion.89 = f32[512,8192]{1,0:T(8,128)} fusion(bf16[1024,8192]{1,0:T(8,128)(2,1)} %all-gather.11.cloned.1.call-done, f32[512,1024]{1,0:T(8,128)} %get-tuple-element.422, f32[1024]{0:T(1024)S(1)} %bitcast.234, f32[512]{0:T(512)S(1)} %get-tuple-element.420), kind=kOutput, calls=%fused_computation.139 | convolution fusion | flops 8591507456 | bytes 35657728 | tf_op jit(solution)/shard_map/dot_general | solution.py:118
  328.9 13.4 %all-gather.13.cloned.1.call-done = bf16[1024,4096]{1,0:T(8,128)(2,1)} async-done(((bf16[128,4096]{1,0:T(8,128)(2,1)}), bf16[1024,4096]{1,0:T(8,128)(2,1)}) %all-gather.13.cloned.1.call-update) | async-done | bytes 8388624 | tf_op jit(solution)/shard_map/all_gather | solution.py:114
  342.3 15.1 %multiply_convert_fusion.2 = (bf16[512,4096]{1,0:T(8,128)(2,1)}, bf16[512,4096]{1,0:T(8,128)(2,1)}, bf16[512,4096]{1,0:T(8,128)(2,1)S(1)}) fusion(f32[512,8192]{1,0:T(8,128)} %fusion.89, bf16[1024,4096]{1,0:T(8,128)(2,1)} %all-gather.13.cloned.1.call-done, bf16[1,512,1024]{2,1,0:T(8,128)(2,1)S(1)} %copy-done.22), kind=kOutput, calls=%fused_computation.67 | convolution fusion | flops 4326424576 | bytes 38797312 | tf_op jit(solution)/shard_map/dot_general | solution.py:137
  359.4 6.8 convert_bitcast_fusion
  366.2 11.7 %copy.151 = bf16[1024,4096]{1,0:T(8,128)(2,1)} copy(bf16[1024,4096]{0,1:T(8,128)(2,1)} %convert_bitcast_fusion) | data formatting | bytes 16777216
  377.9 18.2 %multiply_reduce_fusion.1 = (bf16[1024]{0:T(1024)(128)(2,1)}, f32[512]{0:T(512)S(1)}, f32[512,1024]{1,0:T(8,128)}) fusion(f32[512,1024]{1,0:T(8,128)} %get-tuple-element.422, f32[512]{0:T(512)S(1)} %get-tuple-element.420, f32[1024]{0:T(1024)S(1)} %bitcast.235, bf16[1024,8192]{1,0:T(8,128)(2,1)} %all-gather.11.cloned.1.call-done, ...), kind=kOutput, calls=%fused_computation.97 | convolution fusion | flops 8609855488 | bytes 29370368 | tf_op jit(solution)/shard_map/rf,df->rd/dot_general | solution.py:144
  411.3 9.6 all-to-all-done.2
  425.2 16.1 %gather_fusion.2 = bf16[2048,4,64]{2,1,0:T(4,128)(2,1)} fusion(bf16[2048,4,64]{2,1,0:T(4,128)(2,1)} %reshape.382, s32[2048]{0:T(1024)S(1)} %copy-done.27), kind=kCustom, calls=%fused_computation.2 | custom fusion | bytes 2105344 | tf_op jit(solution)/shard_map/gather | solution.py:164
  446.4 208.8 %while.29 = (s32[]{:T(128)}, f32[2048,4,64]{0,2,1:T(8,128)}, f32[2048,4,64]{0,2,1:T(8,128)}, bf16[4,512,4,64]{1,3,2,0:T(8,128)(2,1)}, bf16[4,512,4,64]{1,3,2,0:T...) while((s32[]{:T(128)}, f32[2048,4,64]{0,2,1:T(8,128)}, ...), condition=%wide.region_11.12_spmd.clone, body=%wide.region_9.11_spmd.clone.sunk | while | flops 2753296384 | bytes 268841472 | solution.py:198
  454.3 12.3 %multiply_reduce_fusion.5 = (f32[4,512]{1,0:T(4,128)}, f32[4,512,2048]{2,1,0:T(8,128)}) fusion(f32[4,512,2048]{2,1,0:T(8,128)S(1)} %fusion.146, f32[4,512]{1,0:T(4,128)S(1)} %dynamic-slice_bitcast_fusion.2, pred[512,2048]{1,0:T(8,128)(4,1)S(1)} %fusion.147, bf16[2048,4,64]{0,2,1:T(8,128)(2,1)} %get-tuple-element.638, ...), kind=kOutput, calls=%fused_computation.28.clone.1 | convolution fusion | flops 557840384 | bytes 35930116 | tf_op jit(solution)/shard_map/while/body/eval_jaxpr/qhd,khd->hqk/dot_general | solution.py:177
  466.7 11.0 multiply_convert_fusion.8
  477.6 6.7 fusion.148
  484.4 8.6 fusion.149
  506.2 12.3 %multiply_reduce_fusion.5 = (f32[4,512]{1,0:T(4,128)}, f32[4,512,2048]{2,1,0:T(8,128)}) fusion(f32[4,512,2048]{2,1,0:T(8,128)S(1)} %fusion.146, f32[4,512]{1,0:T(4,128)S(1)} %dynamic-slice_bitcast_fusion.2, pred[512,2048]{1,0:T(8,128)(4,1)S(1)} %fusion.147, bf16[2048,4,64]{0,2,1:T(8,128)(2,1)} %get-tuple-element.638, ...), kind=kOutput, calls=%fused_computation.28.clone.1 | convolution fusion | flops 557840384 | bytes 35930116 | tf_op jit(solution)/shard_map/while/body/eval_jaxpr/qhd,khd->hqk/dot_general | solution.py:177
  518.6 10.9 multiply_convert_fusion.8
  529.5 7.2 fusion.148
  536.7 8.5 fusion.149
  558.4 12.3 %multiply_reduce_fusion.5 = (f32[4,512]{1,0:T(4,128)}, f32[4,512,2048]{2,1,0:T(8,128)}) fusion(f32[4,512,2048]{2,1,0:T(8,128)S(1)} %fusion.146, f32[4,512]{1,0:T(4,128)S(1)} %dynamic-slice_bitcast_fusion.2, pred[512,2048]{1,0:T(8,128)(4,1)S(1)} %fusion.147, bf16[2048,4,64]{0,2,1:T(8,128)(2,1)} %get-tuple-element.638, ...), kind=kOutput, calls=%fused_computation.28.clone.1 | convolution fusion | flops 557840384 | bytes 35930116 | tf_op jit(solution)/shard_map/while/body/eval_jaxpr/qhd,khd->hqk/dot_general | solution.py:177
  570.8 10.9 multiply_convert_fusion.8
  581.7 7.2 fusion.148
  588.9 8.5 fusion.149
  610.6 12.3 %multiply_reduce_fusion.5 = (f32[4,512]{1,0:T(4,128)}, f32[4,512,2048]{2,1,0:T(8,128)}) fusion(f32[4,512,2048]{2,1,0:T(8,128)S(1)} %fusion.146, f32[4,512]{1,0:T(4,128)S(1)} %dynamic-slice_bitcast_fusion.2, pred[512,2048]{1,0:T(8,128)(4,1)S(1)} %fusion.147, bf16[2048,4,64]{0,2,1:T(8,128)(2,1)} %get-tuple-element.638, ...), kind=kOutput, calls=%fused_computation.28.clone.1 | convolution fusion | flops 557840384 | bytes 35930116 | tf_op jit(solution)/shard_map/while/body/eval_jaxpr/qhd,khd->hqk/dot_general | solution.py:177
  623.0 10.9 multiply_convert_fusion.8
  633.9 7.2 fusion.148
  641.1 8.5 fusion.149
  669.0 8.2 reshape.383
  677.2 9.5 pad_maximum_fusion.3
  686.7 18.7 %gather_fusion.3 = bf16[2048,3,256]{2,1,0:T(4,128)(2,1)} fusion(bf16[2048,3,256]{2,1,0:T(4,128)(2,1)} %pad_maximum_fusion.3, s32[2048]{0:T(1024)S(1)} %copy-done.25), kind=kCustom, calls=%fused_computation.3 | custom fusion | bytes 6299648 | tf_op jit(solution)/shard_map/gather | solution.py:211
  705.4 51.5 %all_to_all.60 = bf16[2048,3,1,256]{3,1,2,0:T(4,128)(2,1)S(1)} all-to-all(bf16[2048,3,1,256]{3,1,2,0:T(4,128)(2,1)} %bitcast.213), channel_id=1, replica_groups=mesh['seq'=4,'fsdp'=8] {'seq'}, dimensions={0} | all-to-all | bytes 6291456 | tf_op jit(solution)/shard_map/all_to_all | solution.py:212
  760.2 8.5 convolution_convert_fusion.1
  770.4 16.6 %convolution_convert_fusion = bf16[1024,8192]{1,0:T(8,128)(2,1)} fusion(bf16[512,4096]{1,0:T(8,128)(2,1)} %get-tuple-element.412, bf16[512,4096]{1,0:T(8,128)(2,1)} %get-tuple-element.411, f32[512,1024]{1,0:T(8,128)S(1)} %copy-done.12, f32[1024]{0:T(1024)S(1)} %bitcast.237, f32[512]{0:T(512)S(1)} %copy-done.36), kind=kOutput, calls=%fused_computation.63 | convolution fusion | flops 8616673280 | bytes 27269120 | tf_op jit(solution)/shard_map/rd,rf->df/dot_general | solution.py:141
  789.6 45.8 %reduce-scatter.7.cloned.1.call-done = bf16[128,3072]{1,0:T(8,128)(2,1)} async-done(((bf16[1024,3072]{1,0:T(8,128)(2,1)}), bf16[128,3072]{1,0:T(8,128)(2,1)}) %reduce-scatter.7.cloned.1.call-update) | async-done | bytes 786448 | tf_op jit(solution)/shard_map/reduce_scatter | solution.py:225
  835.5 169.0 %reduce-scatter.11.cloned.1.call-done = bf16[128,8192]{1,0:T(8,128)(2,1)} async-done(((bf16[1024,8192]{1,0:T(8,128)(2,1)}), bf16[128,8192]{1,0:T(8,128)(2,1)}) %reduce-scatter.11.cloned.1.call-update) | async-done | bytes 2097168 | tf_op jit(solution)/shard_map/reduce_scatter | solution.py:236
  1005.7 10.3 fusion.69
  1016.0 8.0 fusion.66
  1024.0 13.6 %all-reduce.2 = (bf16[1024]{0:T(1024)(128)(2,1)S(1)}, bf16[1024]{0:T(1024)(128)(2,1)S(1)}) all-reduce(bf16[1024]{0:T(1024)(128)(2,1)S(1)} %get-tuple-element.351, bf16[1024]{0:T(1024)(128)(2,1)S(1)} %copy-done.38), channel_id=2, replica_groups=mesh['seq'=4,'fsdp'=8] {'fsdp'}, use_global_device_ids=true, to_apply=%region_14.15.clone | all-reduce | flops 2048 | bytes 8192
  1037.8 10.2 all-reduce.3
  1052.1 59.8 %all-reduce.7.cloned.1.call-done = (bf16[128,4096]{0,1:T(8,128)(2,1)}, bf16[128,3072]{1,0:T(8,128)(2,1)}, bf16[128,1024]{1,0:T(8,128)(2,1)}, bf16[128,8192]{1,0:T(8,128)(2,1)}) async-done(((bf16[128,4096]{0,1:T(8,128)(2,1)}, bf16[128,3072]{1,0:T(8,128)(2,1)}, bf16[128,1024]{1,0:T(8,128)(2,1)}, bf16[128,8192]{1,0:T(8,128)(2,1)}), (bf16[128,4096]{0,1:T(8,128)(2,1)}, bf16[128,3072]{1,0:T(8,128)(2,1)}, ...) | async-done | bytes 4194320 | tf_op jit(solution)/shard_map/psum | solution.py:249
  (301 shorter events, 260.2 us)
Async XLA Ops:
  7.2 70.6 %all-gather.7.cloned.1.call-start = ((), (), s32[]{:S(2)}) async-start(), calls=%async_computation.8 | async-start | bytes 7077888 | tf_op jit(solution)/shard_map/all_gather | solution.py:54
  9.6 295.9 %all-gather.9.cloned.1.call-start = ((), (), s32[]{:S(2)}) async-start(), calls=%async_computation.9 | async-start | bytes 2359296 | tf_op jit(solution)/shard_map/all_gather | solution.py:55
  11.5 17.4 %copy-start.7 = (bf16[1,512,1024]{2,1,0:T(8,128)(2,1)S(1)}, bf16[1,512,1024]{2,1,0:T(8,128)(2,1)}, u32[]{:S(2)}) copy-start(bf16[1,512,1024]{2,1,0:T(8,128)(2,1)} %param.15) | copy-start | bytes 3145732
  11.5 298.6 %all-gather.11.cloned.1.call-start = ((), (), s32[]{:S(2)}) async-start(), calls=%async_computation.10 | async-start | bytes 18874368 | tf_op jit(solution)/shard_map/all_gather | solution.py:113
  28.9 48.8 %copy-start.30 = (f32[8,1,128]{2,1,0:T(1,128)}, f32[8,1,128]{2,1,0:T(1,128)S(1)}, u32[]{:S(2)}) copy-start(f32[8,1,128]{2,1,0:T(1,128)S(1)} %convert_element_type.214) | copy-start | bytes 12292
  29.8 47.9 %copy-start.33 = (f32[512]{0:T(512)}, f32[512]{0:T(512)S(1)}, u32[]{:S(2)}) copy-start(f32[512]{0:T(512)S(1)} %get-tuple-element.418) | copy-start | bytes 6148
  95.2 7.4 copy-start.37
  95.2 40.6 %all-to-all-start = ((bf16[512,3,4,256]{0,3,1,2:T(8,128)(2,1)}), bf16[512,3,4,256]{0,3,1,2:T(8,128)(2,1)S(1)}, u32[]{:S(2)}, u32[]{:S(2)}) async-start(bf16[512,3,4,256]{0,3,1,2:T(8,128)(2,1)} %copy.114), calls=%async_computation | async-start | bytes 6291456 | tf_op jit(solution)/shard_map/all_to_all | solution.py:60
  99.1 243.2 %all-gather.13.cloned.1.call-start = ((), (), s32[]{:S(2)}) async-start(), calls=%async_computation.11 | async-start | bytes 9437184 | tf_op jit(solution)/shard_map/all_gather | solution.py:114
  112.1 41.5 %copy-start.26 = (s32[2048]{0:T(1024)}, s32[2048]{0:T(1024)S(1)}, u32[]{:S(2)}) copy-start(s32[2048]{0:T(1024)S(1)} %fusion.84) | copy-start | bytes 24580
  256.0 8.6 copy-start.24
  273.7 9.2 copy-start.42
  278.5 17.8 %all-to-all-start.1 = ((bf16[4,2,65536]{2,1,0:T(2,128)(2,1)}), bf16[4,2,65536]{2,1,0:T(2,128)(2,1)}, u32[]{:S(2)}, u32[]{:S(2)}) async-start(bf16[4,2,65536]{2,1,0:T(2,128)(2,1)} %reshape.393), calls=%async_computation.1 | async-start | bytes 2097152 | tf_op jit(solution)/shard_map/all_to_all | solution.py:107
  282.8 504.3 %reduce-scatter.13.cloned.1.call-start = ((), (), s32[]{:S(2)}) async-start(), calls=%async_computation.15 | async-start | bytes 9437184
  292.7 103.4 %copy-start.28 = (f32[8,1,128]{2,1,0:T(1,128)}, f32[8,1,128]{2,1,0:T(1,128)S(1)}, u32[]{:S(2)}) copy-start(f32[8,1,128]{2,1,0:T(1,128)S(1)} %convert_element_type.215) | copy-start | bytes 12292
  292.7 12.9 %copy-start.8 = (bf16[1,512,1024]{2,1,0:T(8,128)(2,1)S(1)}, bf16[1,512,1024]{2,1,0:T(8,128)(2,1)}, u32[]{:S(2)}) copy-start(bf16[1,512,1024]{2,1,0:T(8,128)(2,1)} %param.15) | copy-start | bytes 3145732
  310.1 86.0 %copy-start.35 = (f32[512]{0:T(512)}, f32[512]{0:T(512)S(1)}, u32[]{:S(2)}) copy-start(f32[512]{0:T(512)S(1)} %get-tuple-element.420) | copy-start | bytes 6148
  310.1 32.2 %copy-start.22 = (bf16[1,512,1024]{2,1,0:T(8,128)(2,1)S(1)}, bf16[1,512,1024]{2,1,0:T(8,128)(2,1)}, u32[]{:S(2)}) copy-start(bf16[1,512,1024]{2,1,0:T(8,128)(2,1)} %param.22) | copy-start | bytes 3145732
  403.0 17.9 %all-to-all-start.2 = ((bf16[512,4,256]{0,2,1:T(8,128)(2,1)}), bf16[512,4,256]{0,2,1:T(8,128)(2,1)S(1)}, u32[]{:S(2)}, u32[]{:S(2)}) async-start(bf16[512,4,256]{0,2,1:T(8,128)(2,1)} %bitcast.222), calls=%async_computation.2 | async-start | bytes 2097152 | tf_op jit(solution)/shard_map/all_to_all | solution.py:161
  406.7 382.9 %reduce-scatter.9.cloned.1.call-start = ((), (), s32[]{:S(2)}) async-start(), calls=%async_computation.13 | async-start | bytes 2359296 | tf_op jit(solution)/shard_map/reduce_scatter | solution.py:228
  411.3 13.9 %copy-start.27 = (s32[2048]{0:T(1024)S(1)}, s32[2048]{0:T(1024)}, u32[]{:S(2)}) copy-start(s32[2048]{0:T(1024)} %copy-done.26) | copy-start | bytes 24580
  411.3 424.2 %reduce-scatter.7.cloned.1.call-start = ((), (), s32[]{:S(2)}) async-start(), calls=%async_computation.12 | async-start | bytes 7077888 | tf_op jit(solution)/shard_map/reduce_scatter | solution.py:225
  450.9 15.8 %copy-start = (f32[4,512,2048]{2,1,0:T(8,128)}, f32[4,512,2048]{2,1,0:T(8,128)S(1)}, u32[]{:S(2)}) copy-start(f32[4,512,2048]{2,1,0:T(8,128)S(1)} %fusion.146) | copy-start | bytes 50331652 | tf_op jit(solution)/shard_map/while
  477.6 15.3 %slice-start = ((s8[8388608]{0:T(1024)(128)(4,1)}), s8[4194304]{0:T(1024)(128)(4,1)S(1)}, s32[]{:S(2)}) async-start(s8[8388608]{0:T(1024)(128)(4,1)} %bitcast.211), calls=%async_computation.17 | async-start | bytes 8388608 | tf_op jit(solution)/shard_map/while
  484.4 8.6 slice-start.1
  502.8 15.8 %copy-start = (f32[4,512,2048]{2,1,0:T(8,128)}, f32[4,512,2048]{2,1,0:T(8,128)S(1)}, u32[]{:S(2)}) copy-start(f32[4,512,2048]{2,1,0:T(8,128)S(1)} %fusion.146) | copy-start | bytes 50331652 | tf_op jit(solution)/shard_map/while
  529.5 7.2 copy-start.17
  529.5 15.7 %slice-start = ((s8[8388608]{0:T(1024)(128)(4,1)}), s8[4194304]{0:T(1024)(128)(4,1)S(1)}, s32[]{:S(2)}) async-start(s8[8388608]{0:T(1024)(128)(4,1)} %bitcast.211), calls=%async_computation.17 | async-start | bytes 8388608 | tf_op jit(solution)/shard_map/while
  536.7 8.5 slice-start.1
  555.0 15.8 %copy-start = (f32[4,512,2048]{2,1,0:T(8,128)}, f32[4,512,2048]{2,1,0:T(8,128)S(1)}, u32[]{:S(2)}) copy-start(f32[4,512,2048]{2,1,0:T(8,128)S(1)} %fusion.146) | copy-start | bytes 50331652 | tf_op jit(solution)/shard_map/while
  581.7 7.2 copy-start.17
  581.7 15.7 %slice-start = ((s8[8388608]{0:T(1024)(128)(4,1)}), s8[4194304]{0:T(1024)(128)(4,1)S(1)}, s32[]{:S(2)}) async-start(s8[8388608]{0:T(1024)(128)(4,1)} %bitcast.211), calls=%async_computation.17 | async-start | bytes 8388608 | tf_op jit(solution)/shard_map/while
  588.9 8.5 slice-start.1
  607.2 15.8 %copy-start = (f32[4,512,2048]{2,1,0:T(8,128)}, f32[4,512,2048]{2,1,0:T(8,128)S(1)}, u32[]{:S(2)}) copy-start(f32[4,512,2048]{2,1,0:T(8,128)S(1)} %fusion.146) | copy-start | bytes 50331652 | tf_op jit(solution)/shard_map/while
  633.9 7.2 copy-start.17
  633.9 15.7 %slice-start = ((s8[8388608]{0:T(1024)(128)(4,1)}), s8[4194304]{0:T(1024)(128)(4,1)S(1)}, s32[]{:S(2)}) async-start(s8[8388608]{0:T(1024)(128)(4,1)} %bitcast.211), calls=%async_computation.17 | async-start | bytes 8388608 | tf_op jit(solution)/shard_map/while
  641.1 8.5 slice-start.1
  664.8 12.4 %copy-start.13 = (bf16[2048,1,256]{2,1,0:T(2,128)(2,1)S(1)}, bf16[2048,1,256]{2,1,0:T(2,128)(2,1)}, u32[]{:S(2)}) copy-start(bf16[2048,1,256]{2,1,0:T(2,128)(2,1)} %copy.136) | copy-start | bytes 3145732
  677.2 9.5 copy-start.25
  768.8 235.6 %reduce-scatter.11.cloned.1.call-start = ((), (), s32[]{:S(2)}) async-start(), calls=%async_computation.14 | async-start | bytes 18874368 | tf_op jit(solution)/shard_map/reduce_scatter | solution.py:236
  787.0 217.4 %copy-start.43 = (u32[32]{0:T(128)S(1)}, u32[32]{0:T(128)}, u32[]{:S(2)}) copy-start(u32[32]{0:T(128)} %constant.73) | copy-start | bytes 388
  787.0 324.9 %all-reduce.7.cloned.1.call-start = ((), (), s32[]{:S(2)}) async-start(), calls=%async_computation.16 | async-start | bytes 8388608 | tf_op jit(solution)/shard_map/psum | solution.py:249
  1005.7 10.3 copy-start.9
  1005.7 10.3 copy-start.15
  1016.0 8.0 copy-start.38
  1016.0 33.0 %copy-start.11 = (f32[512,1024]{1,0:T(8,128)S(1)}, f32[512,1024]{1,0:T(8,128)}, u32[]{:S(2)}) copy-start(f32[512,1024]{1,0:T(8,128)} %copy-done.10) | copy-start | bytes 6291460
  1016.0 33.0 %copy-start.32 = (f32[512]{0:T(512)S(1)}, f32[512]{0:T(512)}, u32[]{:S(2)}) copy-start(f32[512]{0:T(512)} %get-tuple-element.417) | copy-start | bytes 6148
  1112.0 6.8 copy-start.23
  (44 other events, 178.8 us)
Sparse Core Ops, SparseCore 0:
  10.2 67.4 all-gather.6
  79.9 27.7 all-gather.8
  109.3 150.5 all-gather.10
  261.9 80.2 all-gather.12
  378.0 88.1 reduce-scatter.12
  468.4 34.1 reduce-scatter.8
  768.9 66.4 reduce-scatter.6
  837.8 166.5 reduce-scatter.10
  1008.7 103.2 all-reduce.6
where the time goes:
time: 1140 us; the launch traced here: 1130 us
  waiting for transfers between devices  373 us (33%)
  matrix products  304 us (27%)
  local copies, waits for them, and re-layouts  207 us (18%)
  other arithmetic  117 us (10%)
  blocking collectives  98.6 us (9%)
  between operations  15.3 us (1%)
  starting transfers between devices  12.2 us (1%)
    reduce_scatter x1, waiting for transfers between devices, on_device(): lax.psum_scatter(grad_gate_up_term.astype(jnp.bfloat16), 'fsdp', scatter_...  169 us
    psum x1, waiting for transfers between devices, on_device(): lax.psum(mlp_shards[2].astype(jnp.bfloat16), 'seq').astype(jnp.float32)  59.8 us
    all_to_all x1, blocking collectives, on_device(): lax.all_to_all(dealt_grad.reshape(group_len, 3, 1, -1), 'seq', split_axis...  51.5 us
    dot_general x4, matrix products, backward_block(): jnp.einsum('qhd,khd->hqk', grad_blk, values, preferred_element_type=jnp.f...  49.3 us
    all_gather x1, waiting for transfers between devices, on_device(): lax.all_gather(weight_qkv.astype(jnp.bfloat16), 'fsdp', axis=0, tiled=True)  47.9 us
    reduce_scatter x1, waiting for transfers between devices, on_device(): lax.psum_scatter(grad_qkv_term.astype(jnp.bfloat16), 'fsdp', scatter_dime...  45.8 us
    unnamed x85, local copies, waits for them, and re-layouts  44.9 us
    convert_element_type x4, other arithmetic, backward_block(): grad_score = (probability * (grad_prob - row_delta)).astype(jnp.bfloat16)  43.7 us
  transfers between devices with their start and end apart: 12, of which 8 were waited for; matrix products, arithmetic and copies ran while one was open for 51% of the time, Pallas kernels for 0%

commit v1 on v0

v1 whole, which is shorter than its diff:
```python
import jax
import jax.numpy as jnp
from jax import lax
from jax.experimental import pallas as pl
from jax.experimental.pallas import tpu as pltpu
from jax.sharding import PartitionSpec as P

HEAD_DIM = 64
BLK = 256
LOG2E = 1.4426950408889634

NT = (((1,), (1,)), ((), ()))
NN = (((1,), (0,)), ((), ()))


def dot(a, b, dims=NN):
    return lax.dot_general(a, b, dims, preferred_element_type=jnp.float32)


def first_block(offs_ref, row0):
    best = jnp.int32(0)
    for k in range(offs_ref.shape[0]):
        off = offs_ref[k]
        best = jnp.where(off <= row0, jnp.maximum(best, off), best)
    return best // BLK


def sort_rows(perm_row_ref, src_ref, dst_ref):
    group_len = src_ref.shape[0]

    def step(i, carry):
        rows = pl.ds(pl.multiple_of(i * BLK, BLK), BLK)
        pos = lax.broadcasted_iota(jnp.int32, (BLK, group_len), 0) + i * BLK
        pick = (perm_row_ref[...] == pos).astype(jnp.float32).astype(jnp.bfloat16)
        dst_ref[rows, :] = dot(pick, src_ref[...]).astype(dst_ref.dtype)
        return carry

    lax.fori_loop(0, group_len // BLK, step, 0)


def deal_rows(perm_col_ref, src_ref, dst_ref):
    group_len = src_ref.shape[0]

    def step(i, carry):
        rows = pl.ds(pl.multiple_of(i * BLK, BLK), BLK)
        pos = lax.broadcasted_iota(jnp.int32, (BLK, group_len), 1)
        pick = (perm_col_ref[rows, :] == pos).astype(jnp.float32).astype(jnp.bfloat16)
        dst_ref[rows, :] = dot(pick, src_ref[...]).astype(dst_ref.dtype)
        return carry

    lax.fori_loop(0, group_len // BLK, step, 0)


def allowed_block(start_ref, cols, qb, kb):
    key_pos = lax.broadcasted_iota(jnp.int32, (BLK, BLK), 0) + kb * BLK
    query_pos = lax.broadcasted_iota(jnp.int32, (BLK, BLK), 1) + qb * BLK
    return (key_pos <= query_pos) & (key_pos >= start_ref[:, cols])


def forward_kernel(offs_ref, qkv_ref, perm_row_ref, perm_col_ref, start_ref,
                   sorted_ref, dealt_ref, wide_ref, lse_ref, vt_ref, low_ref):
    group_len = qkv_ref.shape[0]
    width = qkv_ref.shape[1] // 3
    heads = width // HEAD_DIM
    scale = HEAD_DIM ** -0.5 * LOG2E
    sort_rows(perm_row_ref, qkv_ref, sorted_ref)

    def flip(i, carry):
        rows = pl.ds(pl.multiple_of(i * BLK, BLK), BLK)
        vt_ref[:, rows] = sorted_ref[rows, 2 * width:].T
        return carry

    lax.fori_loop(0, group_len // BLK, flip, 0)

    def query_step(qb, carry):
        qrow = pl.multiple_of(qb * BLK, BLK)
        cols = pl.ds(qrow, BLK)

        def key_step(kb, state):
            krow = pl.multiple_of(kb * BLK, BLK)
            krows = pl.ds(krow, BLK)
            allowed = allowed_block(start_ref, cols, qb, kb)
            fresh = []
            for h in range(heads):
                top, total, acc = state[3 * h: 3 * h + 3]
                hq = slice(h * HEAD_DIM, (h + 1) * HEAD_DIM)
                hk = slice(width + h * HEAD_DIM, width + (h + 1) * HEAD_DIM)
                s = dot(sorted_ref[krows, hk], sorted_ref[cols, hq], NT) * scale
                s = jnp.where(allowed, s, -1e30)
                new_top = jnp.maximum(top, jnp.max(s, axis=0, keepdims=True))
                shrink = jnp.exp2(top - new_top)
                p = jnp.exp2(s - new_top)
                total = total * shrink + jnp.sum(p, axis=0, keepdims=True)
                acc = acc * shrink + dot(vt_ref[hq, krows], p.astype(jnp.bfloat16))
                fresh += [new_top, total, acc]
            return tuple(fresh)

        init = []
        for h in range(heads):
            init += [jnp.full((1, BLK), -1e30, jnp.float32), jnp.zeros((1, BLK), jnp.float32),
                     jnp.zeros((HEAD_DIM, BLK), jnp.float32)]
        state = lax.fori_loop(first_block(offs_ref, qrow), qb + 1, key_step, tuple(init))
        parts = []
        for h in range(heads):
            top, total, acc = state[3 * h: 3 * h + 3]
            out = acc / total
            wide_ref[h * HEAD_DIM:(h + 1) * HEAD_DIM, cols] = out
            lse_ref[h:h + 1, cols] = top + jnp.log2(total)
            parts.append(out)
        low_ref[cols, :] = jnp.concatenate(parts, axis=0).T.astype(jnp.bfloat16)
        return carry

    lax.fori_loop(0, group_len // BLK, query_step, 0)
    deal_rows(perm_col_ref, low_ref, dealt_ref)


def backward_kernel(offs_ref, grad_ref, sorted_ref, perm_row_ref, perm_col_ref, start_ref, wide_ref, lse_ref,
                    dealt_ref, do_ref, kt_ref, delta_ref, dk_ref, dv_ref, low_ref):
    group_len = sorted_ref.shape[0]
    width = sorted_ref.shape[1] // 3
    heads = width // HEAD_DIM
    unit = HEAD_DIM ** -0.5
    scale = unit * LOG2E
    sort_rows(perm_row_ref, grad_ref, do_ref)
    dk_ref[...] = jnp.zeros_like(dk_ref)
    dv_ref[...] = jnp.zeros_like(dv_ref)

    def flip(i, carry):
        rows = pl.ds(pl.multiple_of(i * BLK, BLK), BLK)
        kt_ref[:, rows] = sorted_ref[rows, width: 2 * width].T
        product = do_ref[rows, :].astype(jnp.float32).T * wide_ref[:, rows]
        for h in range(heads):
            delta_ref[h:h + 1, rows] = jnp.sum(product[h * HEAD_DIM:(h + 1) * HEAD_DIM], axis=0, keepdims=True)
        return carry

    lax.fori_loop(0, group_len // BLK, flip, 0)

    def query_step(qb, carry):
        qrow = pl.multiple_of(qb * BLK, BLK)
        cols = pl.ds(qrow, BLK)

        def key_step(kb, state):
            krow = pl.multiple_of(kb * BLK, BLK)
            krows = pl.ds(krow, BLK)
            allowed = allowed_block(start_ref, cols, qb, kb)
            fresh = []
            for h in range(heads):
                hq = slice(h * HEAD_DIM, (h + 1) * HEAD_DIM)
                hk = slice(width + h * HEAD_DIM, width + (h + 1) * HEAD_DIM)
                hv = slice(2 * width + h * HEAD_DIM, 2 * width + (h + 1) * HEAD_DIM)
                q = sorted_ref[cols, hq]
                do = do_ref[cols, hq]
                s = dot(sorted_ref[krows, hk], q, NT) * scale
                s = jnp.where(allowed, s, -1e30)
                p = jnp.exp2(s - lse_ref[h:h + 1, cols])
                dp = dot(sorted_ref[krows, hv], do, NT)
                ds = (p * (dp - delta_ref[h:h + 1, cols])).astype(jnp.bfloat16)
                dv_ref[krows, hq] += dot(p.astype(jnp.bfloat16), do)
                dk_ref[krows, hq] += dot(ds, q)
                fresh.append(state[h] + dot(kt_ref[hq, krows], ds))
            return tuple(fresh)

        state = lax.fori_loop(first_block(offs_ref, qrow), qb + 1, key_step,
                              tuple(jnp.zeros((HEAD_DIM, BLK), jnp.float32) for _ in range(heads)))
        low_ref[cols, :width] = (jnp.concatenate(state, axis=0) * unit).T.astype(jnp.bfloat16)
        return carry

    lax.fori_loop(0, group_len // BLK, query_step, 0)
    low_ref[:, width:2 * width] = (dk_ref[...] * unit).astype(jnp.bfloat16)
    low_ref[:, 2 * width:] = dv_ref[...].astype(jnp.bfloat16)
    deal_rows(perm_col_ref, low_ref, dealt_ref)


def vmem():
    return pl.BlockSpec(memory_space=pltpu.VMEM)


def attention_forward(offs, qkv, perm, start):
    group_len, columns = qkv.shape
    width = columns // 3
    return pl.pallas_call(
        forward_kernel,
        name="attention_forward",
        out_shape=(
            jax.ShapeDtypeStruct((group_len, columns), jnp.bfloat16),
            jax.ShapeDtypeStruct((group_len, width), jnp.bfloat16),
            jax.ShapeDtypeStruct((width, group_len), jnp.float32),
            jax.ShapeDtypeStruct((8, group_len), jnp.float32),
        ),
        in_specs=[pl.BlockSpec(memory_space=pltpu.SMEM)] + [vmem()] * 4,
        out_specs=(vmem(),) * 4,
        scratch_shapes=[pltpu.VMEM((width, group_len), jnp.bfloat16), pltpu.VMEM((group_len, width), jnp.bfloat16)],
        compiler_params=pltpu.CompilerParams(vmem_limit_bytes=48 << 20),
        cost_estimate=pl.CostEstimate(flops=20_000_000_000, bytes_accessed=16 << 20, transcendentals=0),
    )(offs, qkv, perm.reshape(1, group_len), perm.reshape(group_len, 1), start.reshape(1, group_len))


def attention_backward(offs, grad, ordered, perm, start, wide, lse):
    group_len, columns = ordered.shape
    width = columns // 3
    return pl.pallas_call(
        backward_kernel,
        name="attention_backward",
        out_shape=jax.ShapeDtypeStruct((group_len, columns), jnp.bfloat16),
        in_specs=[pl.BlockSpec(memory_space=pltpu.SMEM)] + [vmem()] * 7,
        out_specs=vmem(),
        scratch_shapes=[
            pltpu.VMEM((group_len, width), jnp.bfloat16),
            pltpu.VMEM((width, group_len), jnp.bfloat16),
            pltpu.VMEM((8, group_len), jnp.float32),
            pltpu.VMEM((group_len, width), jnp.float32),
            pltpu.VMEM((group_len, width), jnp.float32),
            pltpu.VMEM((group_len, columns), jnp.bfloat16),
        ],
        compiler_params=pltpu.CompilerParams(vmem_limit_bytes=48 << 20),
        cost_estimate=pl.CostEstimate(flops=40_000_000_000, bytes_accessed=16 << 20, transcendentals=0),
    )(offs, grad, ordered, perm.reshape(1, group_len), perm.reshape(group_len, 1), start.reshape(1, group_len), wide, lse)


epsilon = 1e-05


def rms_scale(values):
    return lax.rsqrt(jnp.mean(values * values, axis=-1, keepdims=True) + epsilon)


def norm_backward(values, inv_scale, grad_normed, gain):
    scaled = grad_normed * gain
    gain_grad = jnp.sum(grad_normed * values * inv_scale, axis=0)
    input_grad = inv_scale * scaled - values * inv_scale**3 * jnp.mean(values * scaled, axis=-1, keepdims=True)
    return (input_grad, gain_grad)


def matmul(spec, left, right):
    return jnp.einsum(spec, left, right, preferred_element_type=jnp.float32)


def on_device(block_input, norm_gain_a, weight_qkv, weight_out, norm_gain_b, weight_gate_up, weight_down,
              cotangent, permutation, lengths, offsets):
    low = jnp.bfloat16
    seq_count = lax.axis_size("seq")
    mine = lax.axis_index("seq")
    row_count, model_width = block_input.shape[1:]
    group_len = row_count * seq_count
    shard = weight_qkv.shape[0]
    head_width = weight_qkv.shape[1] // 3 // seq_count
    part_units = weight_down.shape[1] // seq_count
    perm = permutation[0]
    offs = offsets[0]
    position = jnp.arange(group_len, dtype=jnp.int32)
    start = jnp.max(jnp.where(offs[None, :] <= position[:, None], offs[None, :], 0), axis=1)

    def columns(weight, blocks, width):
        cut = weight.reshape(shard, blocks, seq_count, width)
        return lax.dynamic_index_in_dim(cut, mine, 2, keepdims=False).reshape(shard, blocks * width).astype(low)

    gather_weight = lambda piece: lax.all_gather(piece, "fsdp", axis=0, tiled=True)
    gather_rows = lambda rows: lax.all_gather(rows, "seq", axis=0, tiled=True)
    scatter_rows = lambda part: lax.psum_scatter(part.astype(low), "seq", scatter_dimension=0, tiled=True)

    gains = gather_weight(jnp.stack([norm_gain_a, norm_gain_b], axis=1)).astype(low).astype(jnp.float32)
    gain_a, gain_b = gains[:, 0], gains[:, 1]
    rows_all = gather_rows(block_input[0])
    part_qkv = gather_weight(columns(weight_qkv, 3, head_width))
    full_out = gather_weight(weight_out.astype(low))
    part_gate_up = gather_weight(columns(weight_gate_up, 2, part_units))
    part_down = gather_weight(columns(weight_down, 1, part_units))
    grad_rows_all = gather_rows(cotangent[0])

    wide_all = rows_all.astype(jnp.float32)
    normed_a = (wide_all * rms_scale(wide_all) * gain_a).astype(low)
    qkv = matmul("rd,de->re", normed_a, part_qkv).astype(low)
    ordered, dealt_out, wide_out, log_total = attention_forward(offs, qkv, perm, start)
    mixed = lax.all_to_all(
        dealt_out.reshape(group_len, 1, head_width), "seq", split_axis=0, concat_axis=1, tiled=True
    ).reshape(row_count, model_width)
    inputs = block_input[0].astype(jnp.float32)
    inv_first = rms_scale(inputs)
    hidden = inputs + matmul("rd,de->re", mixed, full_out)
    inv_second = rms_scale(hidden)
    normed_b = gather_rows((hidden * inv_second * gain_b).astype(low))

    gate_up = matmul("rd,df->rf", normed_b, part_gate_up)
    gate_part, up_part = gate_up[:, :part_units], gate_up[:, part_units:]
    gate_sigmoid = jax.nn.sigmoid(gate_part)
    gate_silu = gate_part * gate_sigmoid
    activation = (gate_silu * up_part).astype(low)
    branch_out = scatter_rows(matmul("rf,df->rd", activation, part_down)).astype(jnp.float32)
    result_rows = (hidden + branch_out).astype(low)

    grad_activation = matmul("rd,df->rf", grad_rows_all, part_down)
    grad_gate = grad_activation * up_part * gate_sigmoid * (1.0 + gate_part * (1.0 - gate_sigmoid))
    grad_up = grad_activation * gate_silu
    grad_gate_up = jnp.concatenate([grad_gate, grad_up], axis=1).astype(low)
    grad_normed_b = scatter_rows(matmul("rf,df->rd", grad_gate_up, part_gate_up)).astype(jnp.float32)
    down_term = matmul("rd,rf->df", grad_rows_all, activation)
    gate_up_term = matmul("rd,rf->df", normed_b, grad_gate_up)
    hidden_back, gain_b_term = norm_backward(hidden, inv_second, grad_normed_b, gain_b)
    grad_hidden = cotangent[0].astype(jnp.float32) + hidden_back
    grad_branch = grad_hidden.astype(low)
    grad_mixed = matmul("re,de->rd", grad_branch, full_out).astype(low)
    grad_heads = lax.all_to_all(
        grad_mixed.reshape(row_count, seq_count, head_width), "seq", split_axis=1, concat_axis=0, tiled=True
    ).reshape(group_len, head_width)
    dealt_grad = attention_backward(offs, grad_heads, ordered, perm, start, wide_out, log_total)
    out_term = matmul("rd,re->de", mixed, grad_branch)
    out_part = lax.psum_scatter(out_term.astype(low), "seq", scatter_dimension=1, tiled=True)
    qkv_term = matmul("rd,re->de", normed_a, dealt_grad)
    grad_normed_a = scatter_rows(matmul("re,de->rd", dealt_grad, part_qkv)).astype(jnp.float32)
    input_back, gain_a_term = norm_backward(inputs, inv_first, grad_normed_a, gain_a)
    input_grad = (grad_hidden + input_back).astype(low)

    def finish(term):
        piece = lax.psum_scatter(term.astype(low), "fsdp", scatter_dimension=0, tiled=True)
        return lax.all_gather(piece, "seq", axis=0, tiled=False)

    def spread(pieces, blocks):
        width = pieces.shape[-1] // blocks
        return pieces.reshape(seq_count, shard, blocks, width).transpose(1, 2, 0, 3).reshape(
            shard, -1).astype(jnp.float32)

    grad_mlp = finish(jnp.concatenate([gate_up_term, down_term], axis=1))
    grad_attn = finish(jnp.concatenate([qkv_term.astype(low), out_part], axis=1))
    gain_terms = lax.psum(jnp.stack([gain_a_term, gain_b_term]), ("seq", "fsdp"))
    gain_terms = lax.dynamic_slice_in_dim(gain_terms, lax.axis_index("fsdp") * shard, shard, axis=1)
    return (
        result_rows[None],
        input_grad[None],
        gain_terms[0],
        spread(grad_attn[:, :, : 3 * head_width], 3),
        spread(grad_attn[:, :, 3 * head_width:], 1),
        gain_terms[1],
        spread(grad_mlp[:, :, : 2 * part_units], 2),
        spread(grad_mlp[:, :, 2 * part_units:], 1),
    )


def solution(mesh):
    rows = P("fsdp", "seq", None)
    vector = P("fsdp")
    matrix = P("fsdp", None)
    return jax.shard_map(
        on_device,
        mesh=mesh,
        in_specs=(rows, vector, matrix, matrix, vector, matrix, matrix, rows, matrix, matrix, matrix),
        out_specs=(rows, rows, vector, matrix, matrix, vector, matrix, matrix),
        check_vma=False,
    )
```

time: 1140 us -> 773 us (0.68)
  matrix products: 304 us -> 106 us
  local copies, waits for them, and re-layouts: 207 us -> 57.9 us
  other arithmetic: 117 us -> 28.3 us
  Pallas kernels: 0 us -> 80.2 us
  waiting for transfers between devices: 373 us -> 387 us
    dot_general x40 -> x12, matrix products: 304 us -> 106 us  [matmul(): return jnp.einsum(spec, left, right, preferred_element_type=jnp.float32)]
    all_gather x4 -> x9, waiting for transfers between devices: 61.3 us -> 223 us  [the longest x3 136 us: on_device(): gather_rows = lambda rows: lax.all_gather(rows, 'seq', axis=0, tiled=True)]
    reduce_scatter x3 -> x5, waiting for transfers between devices: 215 us -> 134 us  [the longest x3 123 us: on_device(): lax.psum_scatter(part.astype(low), 'seq', scatter_dimension=0, tiled=True)]
    pallas_call x0 -> x2, Pallas kernels: none -> 80.2 us  [the longest x1 40.6 us: attention_forward(): pl.pallas_call(forward_kernel, name='attention_forward', out_shape=(jax.S...]
    gather x4 -> x0, local copies, waits for them, and re-layouts: 66.8 us -> none  [the longest x1 23 us: on_device(): ordered = head_rows[inverse]]
    psum x1 -> x0, waiting for transfers between devices: 59.8 us -> none  [on_device(): lax.psum(mlp_shards[2].astype(jnp.bfloat16), 'seq').astype(jnp.float32)]
    convert_element_type x17 -> x5, other arithmetic: 64.3 us -> 7.72 us  [the longest x3 5.77 us: spread(): return pieces.reshape(seq_count, shard, blocks, width).transpose(1, 2, 0,...]
    reshape x11 -> x2, local copies, waits for them, and re-layouts: 40.8 us -> 0.58 us  [the longest x1 0.51 us: on_device(): dealt_out.reshape(group_len, 1, head_width)]
  transfers between devices with their start and end apart: 12 -> 15, of which waited for: 8 -> 11; matrix products, arithmetic and copies ran while one was open for 51% -> 19% of each run, Pallas kernels for 0% -> 10%
where the time goes in v1:
time: 773 us; the launch traced here: 764 us
  waiting for transfers between devices  387 us (50%)
  matrix products  106 us (14%)
  blocking collectives  88.6 us (11%)
  Pallas kernels  80.2 us (10%)
  local copies, waits for them, and re-layouts  57.9 us (7%)
  other arithmetic  28.3 us (4%)
  between operations  14.8 us (2%)
    all_gather x3, waiting for transfers between devices, on_device(): gather_rows = lambda rows: lax.all_gather(rows, 'seq', axis=0, tiled=True)  136 us
    reduce_scatter x3, waiting for transfers between devices, on_device(): lax.psum_scatter(part.astype(low), 'seq', scatter_dimension=0, tiled=True)  123 us
    dot_general x12, matrix products, matmul(): return jnp.einsum(spec, left, right, preferred_element_type=jnp.float32)  106 us
    all_gather x4, waiting for transfers between devices, on_device(): lax.all_gather(piece, 'fsdp', axis=0, tiled=True)  44 us
    all_gather x2, waiting for transfers between devices, finish(): return lax.all_gather(piece, 'seq', axis=0, tiled=False)  42.8 us
    pallas_call x1, Pallas kernels, attention_forward(): pl.pallas_call(forward_kernel, name='attention_forward', out_shape=(jax.S...  40.6 us
    psum x1, blocking collectives, on_device(): lax.psum(jnp.stack([gain_a_term, gain_b_term]), ('seq', 'fsdp'))  39.7 us
    pallas_call x1, Pallas kernels, attention_backward(): pl.pallas_call(backward_kernel, name='attention_backward', out_shape=jax....  39.7 us
  transfers between devices with their start and end apart: 15, of which 11 were waited for; matrix products, arithmetic and copies ran while one was open for 19% of the time, Pallas kernels for 10%

profile of v1, /device:TPU:0, one launch (start us, length us, event | category | flops | bytes accessed | tf_op | source)
XLA Modules:
  0.0 764.3 jit_solution(12823742167972856778)
XLA Ops:
  11.4 3.7 copy.82
  16.4 13.4 %all_gather.37 = bf16[1024,2]{0,1:T(2,128)(2,1)S(1)} all-gather(bf16[128,2]{0,1:T(2,128)(2,1)S(1)} %pad_maximum_fusion.10), channel_id=1, replica_groups=mesh['seq'=4,'fsdp'=8] {'fsdp'}, dimensions={0}, use_global_device_ids=true | all-gather | bytes 4608 | tf_op jit(solution)/shard_map/all_gather | solution.py:257
  29.9 35.4 %all-gather.23.cloned.1.call-done = bf16[1,2048,1024]{2,1,0:T(8,128)(2,1)} async-done(((bf16[1,512,1024]{2,1,0:T(8,128)(2,1)}), bf16[1,2048,1024]{2,1,0:T(8,128)(2,1)}) %all-gather.23.cloned.1.call-update) | async-done | bytes 4194320 | tf_op jit(solution)/shard_map/all_gather | solution.py:258
  65.3 3.1 fusion
  68.4 26.3 %all-gather.15.cloned.1.call-done = bf16[1024,768]{0,1:T(8,128)(2,1)} async-done(((bf16[128,768]{0,1:T(8,128)(2,1)}), bf16[1024,768]{0,1:T(8,128)(2,1)}) %all-gather.15.cloned.1.call-update) | async-done | bytes 1572880 | tf_op jit(solution)/shard_map/all_gather | solution.py:257
  94.7 7.9 %convolution_convert_fusion.2.qkv_ref = bf16[2048,768]{1,0:T(8,128)(2,1)} fusion(bf16[1024,768]{0,1:T(8,128)(2,1)} %all-gather.15.cloned.1.call-done, bf16[1,2048,1024]{2,1,0:T(8,128)(2,1)} %all-gather.23.cloned.1.call-done, f32[1024]{0:T(1024)S(1)} %bitcast.159, f32[2048]{0:T(1024)S(1)} %add_rsqrt_fusion), kind=kOutput, calls=%fused_computation.32 | convolution fusion | flops 3231186944 | bytes 8925184 | tf_op jit(solution)/shard_map/rd,de->re/dot_general | solution.py:235
  102.6 40.6 %attention_forward.1 = (bf16[2048,768]{1,0:T(8,128)(2,1)}, bf16[2048,256]{1,0:T(8,128)(2,1)S(1)}, f32[256,2048]{1,0:T(8,128)S(1)}, f32[8,2048]{1,0:T(8,128)S(1)}) custom-call(s32[3]{0:T(128)S(1)} %bitcast.135, bf16[2048,768]{1,0:T(8,128)(2,1)} %convolution_convert_fusion.2.qkv_ref, s32[1,2048]{1,0:T(1,128)S(1)} %copy-done, s32[2048,1]{1,0:T(8,128)S(1)} %copy.79.perm_col_ref, ...), custom_call_target="tpu_custom_call" | custom-call | flops 20000000000 | bytes 16777216 | tf_op jit(solution)/shard_map/attention_forward/pallas_call | solution.py:181
  146.8 17.9 %all_to_all.30 = bf16[4,2,65536]{2,1,0:T(2,128)(2,1)} all-to-all(bf16[4,2,65536]{2,1,0:T(2,128)(2,1)S(1)} %reshape.148), channel_id=1, replica_groups=mesh['seq'=4,'fsdp'=8] {'seq'}, dimensions={0} | all-to-all | bytes 2097152 | tf_op jit(solution)/shard_map/all_to_all | solution.py:274
  164.7 2.6 reshape.149
  168.5 2.3 copy.81
  170.8 3.5 multiply_reduce_fusion
  175.6 2.5 copy.83
  180.9 47.4 %all-gather.19.cloned.1.call-done = bf16[2048,1024]{1,0:T(8,128)(2,1)} async-done(((bf16[512,1024]{1,0:T(8,128)(2,1)}), bf16[2048,1024]{1,0:T(8,128)(2,1)}) %all-gather.19.cloned.1.call-update) | async-done | bytes 4194320 | tf_op jit(solution)/shard_map/all_gather | solution.py:258
  228.3 15.1 %fusion.45 = f32[2048,2048]{0,1:T(8,128)} fusion(bf16[2048,1024]{1,0:T(8,128)(2,1)} %all-gather.19.cloned.1.call-done, bf16[1024,2048]{0,1:T(8,128)(2,1)} %all-gather.21.cloned.1.call-done), kind=kOutput, calls=%fused_computation.93 | convolution fusion | flops 8589934592 | bytes 25165824 | tf_op jit(solution)/shard_map/rd,df->rf/dot_general | solution.py:235
  243.4 17.8 %all-gather.25.cloned.1.call-done = bf16[1024,1,1,1024]{0,3,2,1:T(8,128)(2,1)} async-done(((bf16[128,1,1,1024]{0,3,2,1:T(8,128)(2,1)}), bf16[1024,1,1,1024]{0,3,2,1:T(8,128)(2,1)}) %all-gather.25.cloned.1.call-update) | async-done | bytes 2097168 | tf_op jit(solution)/shard_map/all_gather | solution.py:257
  261.2 53.6 %all-gather.27.cloned.1.call-done = bf16[1,2048,1024]{2,1,0:T(8,128)(2,1)} async-done(((bf16[1,512,1024]{2,1,0:T(8,128)(2,1)}), bf16[1,2048,1024]{2,1,0:T(8,128)(2,1)}) %all-gather.27.cloned.1.call-update) | async-done | bytes 4194320 | tf_op jit(solution)/shard_map/all_gather | solution.py:258
  314.8 16.3 %fusion.5 = (bf16[2048,1024]{0,1:T(8,128)(2,1)}, bf16[2048,1024]{0,1:T(8,128)(2,1)}, bf16[2048,1024]{0,1:T(8,128)(2,1)}) fusion(f32[2048,2048]{0,1:T(8,128)} %fusion.45, bf16[1,2048,1024]{2,1,0:T(8,128)(2,1)} %all-gather.27.cloned.1.call-done, bf16[1024,1,1,1024]{0,3,2,1:T(8,128)(2,1)} %all-gather.25.cloned.1.call-done), kind=kOutput, calls=%fused_computation.10 | convolution fusion | flops 4326424576 | bytes 35651584 | tf_op jit(solution)/shard_map/rd,df->rf/dot_general | solution.py:235
  331.2 12.9 %fusion.14 = bf16[2048,1024]{1,0:T(8,128)(2,1)} fusion(bf16[1024,2048]{0,1:T(8,128)(2,1)S(1)} %copy-done.15, bf16[2048,1024]{0,1:T(8,128)(2,1)} %get-tuple-element.21, bf16[2048,1024]{0,1:T(8,128)(2,1)} %get-tuple-element.20), kind=kOutput, calls=%fused_computation.28 | convolution fusion | flops 8608808960 | bytes 16777216 | tf_op jit(solution)/shard_map/rf,df->rd/dot_general | solution.py:235
  344.6 9.5 %convolution_convert_fusion.1 = bf16[2048,1024]{1,0:T(8,128)(2,1)} fusion(bf16[2048,1024]{0,1:T(8,128)(2,1)} %get-tuple-element.22, bf16[1024,1,1,1024]{0,3,2,1:T(8,128)(2,1)} %all-gather.25.cloned.1.call-done), kind=kOutput, calls=%fused_computation.31 | convolution fusion | flops 4297064448 | bytes 10485760 | tf_op jit(solution)/shard_map/rf,df->rd/dot_general | solution.py:235
  354.1 42.9 %reduce-scatter.11.cloned.1.call-done = bf16[512,1024]{1,0:T(8,128)(2,1)} async-done(((bf16[2048,1024]{1,0:T(8,128)(2,1)}), bf16[512,1024]{1,0:T(8,128)(2,1)}) %reduce-scatter.11.cloned.1.call-update) | async-done | bytes 1048592 | tf_op jit(solution)/shard_map/reduce_scatter | solution.py:259
  397.0 2.0 fusion.26
  399.0 54.0 %reduce-scatter.9.cloned.1.call-done = bf16[512,1024]{1,0:T(8,128)(2,1)} async-done(((bf16[2048,1024]{1,0:T(8,128)(2,1)}), bf16[512,1024]{1,0:T(8,128)(2,1)}) %reduce-scatter.9.cloned.1.call-update) | async-done | bytes 1048592 | tf_op jit(solution)/shard_map/reduce_scatter | solution.py:259
  453.0 3.7 fusion.23
  458.0 2.7 convolution_convert_fusion.3
  460.9 8.2 %convert_bitcast_fusion.1 = bf16[1024,1024]{1,0:T(8,128)(2,1)S(1)} fusion(bf16[2048,1024]{0,1:T(8,128)(2,1)} %get-tuple-element.22, bf16[1,2048,1024]{2,1,0:T(8,128)(2,1)} %all-gather.27.cloned.1.call-done), kind=kOutput, calls=%fused_computation.57 | convolution fusion | flops 4296015872 | bytes 10485760 | tf_op jit(solution)/shard_map/rd,rf->df/dot_general | solution.py:235
  469.1 11.8 %fusion.15 = bf16[1024,2048]{1,0:T(8,128)(2,1)S(1)} fusion(bf16[2048,1024]{1,0:T(8,128)(2,1)S(1)} %copy-done.16, bf16[2048,1024]{0,1:T(8,128)(2,1)} %get-tuple-element.21, bf16[2048,1024]{0,1:T(8,128)(2,1)} %get-tuple-element.20), kind=kOutput, calls=%fused_computation.29 | convolution fusion | flops 8608808960 | bytes 16777216 | tf_op jit(solution)/shard_map/rd,rf->df/dot_general | solution.py:235
  480.8 3.2 pad_maximum_fusion.1
  485.7 3.2 convolution_convert_fusion.5
  489.0 17.6 %all_to_all.31 = bf16[512,4,256]{2,0,1:T(8,128)(2,1)S(1)} all-to-all(bf16[512,4,256]{2,0,1:T(8,128)(2,1)S(1)} %bitcast.141), channel_id=1, replica_groups=mesh['seq'=4,'fsdp'=8] {'seq'}, dimensions={1} | all-to-all | bytes 2097152 | tf_op jit(solution)/shard_map/all_to_all | solution.py:302
  506.6 39.7 %attention_backward.1 = bf16[2048,768]{1,0:T(8,128)(2,1)} custom-call(s32[3]{0:T(128)S(1)} %bitcast.136, bf16[2048,256]{1,0:T(8,128)(2,1)S(1)} %bitcast.130, bf16[2048,768]{1,0:T(8,128)(2,1)} %get-tuple-element.13.sorted_ref, s32[1,2048]{1,0:T(1,128)S(1)} %copy-done, s32[2048,1]{1,0:T(8,128)S(1)} %copy.79.perm_col_ref, s32[1,2048]{1,0:T(1,128)S(1)} %bitcast.133, ...), custom_call_target="tpu_custom_call" | custom-call | flops 40000000000 | bytes 16777216 | tf_op jit(solution)/shard_map/attention_backward/pallas_call | solution.py:201
  546.3 7.0 convolution_convert_fusion.4
  553.3 1.8 pad_maximum_fusion.8
  555.1 2.6 copy.95
  557.7 11.4 %reduce-scatter.17.cloned.1.call-done = bf16[128,3072]{1,0:T(8,128)(2,1)} async-done(((bf16[1024,3072]{1,0:T(8,128)(2,1)}), bf16[128,3072]{1,0:T(8,128)(2,1)}) %reduce-scatter.17.cloned.1.call-update) | async-done | bytes 786448 | tf_op jit(solution)/shard_map/reduce_scatter | solution.py:314
  569.2 7.7 %convolution_convert_fusion = bf16[2048,1024]{1,0:T(8,128)(2,1)} fusion(bf16[2048,768]{1,0:T(8,128)(2,1)} %attention_backward.1, bf16[1024,768]{0,1:T(8,128)(2,1)} %all-gather.15.cloned.1.call-done), kind=kOutput, calls=%fused_computation.30 | convolution fusion | flops 3223322624 | bytes 8912896 | tf_op jit(solution)/shard_map/re,de->rd/dot_general | solution.py:235
  578.4 27.7 %reduce-scatter.19.cloned.1.call-done = bf16[128,1024]{1,0:T(8,128)(2,1)} async-done(((bf16[1024,1024]{1,0:T(8,128)(2,1)}), bf16[128,1024]{1,0:T(8,128)(2,1)}) %reduce-scatter.19.cloned.1.call-update) | async-done | bytes 262160
  606.1 1.8 copy.96
  608.0 42.8 %all-gather.31.cloned.1.call-done = bf16[512,3072]{1,0:T(8,128)(2,1)} async-done(((bf16[128,3072]{1,0:T(8,128)(2,1)}), bf16[512,3072]{1,0:T(8,128)(2,1)}) %all-gather.31.cloned.1.call-update) | async-done | bytes 3145744 | tf_op jit(solution)/shard_map/all_gather | solution.py:315
  650.8 4.1 slice_convert_fusion
  654.9 6.7 reshape.136
  661.6 6.9 copy.103
  668.4 6.1 reshape.132
  677.5 3.0 copy.100
  680.5 26.2 %reduce-scatter.13.cloned.1.call-done = bf16[512,1024]{1,0:T(8,128)(2,1)} async-done(((bf16[2048,1024]{1,0:T(8,128)(2,1)}), bf16[512,1024]{1,0:T(8,128)(2,1)}) %reduce-scatter.13.cloned.1.call-update) | async-done | bytes 1048592 | tf_op jit(solution)/shard_map/reduce_scatter | solution.py:259
  706.6 2.1 fusion.31
  708.7 39.7 %psum.7 = f32[2,1024]{1,0:T(2,128)S(1)} all-reduce(f32[2,1024]{1,0:T(2,128)S(1)} %pad_maximum_fusion.9), channel_id=1, replica_groups=mesh['seq'=4,'fsdp'=8] {'seq','fsdp'}, use_global_device_ids=true, to_apply=%region_11.12 | all-reduce | flops 2048 | bytes 16384 | tf_op jit(solution)/shard_map/psum | solution.py:324
  749.0 2.8 fusion.39
  754.2 2.0 reshape.130
  (104 shorter events, 26.6 us)
Async XLA Ops:
  7.2 3.4 copy-start.10
  7.2 58.1 %all-gather.23.cloned.1.call-start = ((), (), s32[]{:S(2)}) async-start(), calls=%async_computation.17 | async-start | bytes 5242880 | tf_op jit(solution)/shard_map/all_gather | solution.py:258
  7.9 86.7 %all-gather.15.cloned.1.call-start = ((), (), s32[]{:S(2)}) async-start(), calls=%async_computation.8 | async-start | bytes 1769472 | tf_op jit(solution)/shard_map/all_gather | solution.py:257
  10.5 160.3 %all-gather.17.cloned.1.call-start = ((), (), s32[]{:S(2)}) async-start(), calls=%async_computation.9 | async-start | bytes 2359296 | tf_op jit(solution)/shard_map/all_gather | solution.py:257
  11.3 4.7 copy-start
  11.3 5.1 copy-start.17
  11.3 5.1 copy-start.18
  11.3 18.5 %copy-start.1 = (s32[1,3]{1,0:T(1,128)S(1)}, s32[1,3]{1,0:T(1,128)}, u32[]{:S(2)}) copy-start(s32[1,3]{1,0:T(1,128)} %param.20) | copy-start | bytes 40
  11.3 169.6 %all-gather.21.cloned.1.call-start = ((), (), s32[]{:S(2)}) async-start(), calls=%async_computation.11 | async-start | bytes 4718592 | tf_op jit(solution)/shard_map/all_gather | solution.py:257
  16.0 212.3 %all-gather.19.cloned.1.call-start = ((), (), s32[]{:S(2)}) async-start(), calls=%async_computation.10 | async-start | bytes 5242880 | tf_op jit(solution)/shard_map/all_gather | solution.py:258
  29.9 72.6 %copy-start.11 = (f32[1024,1]{0,1:T(1,128)}, f32[1024,1]{0,1:T(1,128)S(1)}, u32[]{:S(2)}) copy-start(f32[1024,1]{0,1:T(1,128)S(1)} %get-tuple-element.26) | copy-start | bytes 12292
  68.4 34.2 %copy-start.13 = (f32[2048]{0:T(1024)}, f32[2048]{0:T(1024)S(1)}, u32[]{:S(2)}) copy-start(f32[2048]{0:T(1024)S(1)} %add_rsqrt_fusion) | copy-start | bytes 24580
  143.1 1.3 copy-start.2
  175.6 85.6 %all-gather.25.cloned.1.call-start = ((), (), s32[]{:S(2)}) async-start(), calls=%async_computation.18 | async-start | bytes 2359296 | tf_op jit(solution)/shard_map/all_gather | solution.py:257
  179.9 135.0 %all-gather.27.cloned.1.call-start = ((), (), s32[]{:S(2)}) async-start(), calls=%async_computation.19 | async-start | bytes 5242880 | tf_op jit(solution)/shard_map/all_gather | solution.py:258
  180.6 216.3 %reduce-scatter.11.cloned.1.call-start = ((), (), s32[]{:S(2)}) async-start(), calls=%async_computation.13 | async-start | bytes 5242880 | tf_op jit(solution)/shard_map/reduce_scatter | solution.py:259
  314.8 16.3 %copy-start.15 = (bf16[1024,2048]{0,1:T(8,128)(2,1)S(1)}, bf16[1024,2048]{0,1:T(8,128)(2,1)}, u32[]{:S(2)}) copy-start(bf16[1024,2048]{0,1:T(8,128)(2,1)} %all-gather.21.cloned.1.call-done) | copy-start | bytes 12582916
  344.1 108.9 %reduce-scatter.9.cloned.1.call-start = ((), (), s32[]{:S(2)}) async-start(), calls=%async_computation.12 | async-start | bytes 5242880 | tf_op jit(solution)/shard_map/reduce_scatter | solution.py:259
  354.1 199.2 %reduce-scatter.15.cloned.1.call-start = ((), (), s32[]{:S(2)}) async-start(), calls=%async_computation.15 | async-start | bytes 2621440 | tf_op jit(solution)/shard_map/reduce_scatter | solution.py:307
  453.0 5.0 copy-start.9
  456.6 1.3 copy-start.5
  460.7 108.4 %reduce-scatter.17.cloned.1.call-start = ((), (), s32[]{:S(2)}) async-start(), calls=%async_computation.16 | async-start | bytes 7077888 | tf_op jit(solution)/shard_map/reduce_scatter | solution.py:314
  460.9 8.2 %copy-start.16 = (bf16[2048,1024]{1,0:T(8,128)(2,1)S(1)}, bf16[2048,1024]{1,0:T(8,128)(2,1)}, u32[]{:S(2)}) copy-start(bf16[2048,1024]{1,0:T(8,128)(2,1)} %all-gather.19.cloned.1.call-done) | copy-start | bytes 12582916
  484.1 1.6 copy-start.6
  484.1 122.1 %reduce-scatter.19.cloned.1.call-start = ((), (), s32[]{:S(2)}) async-start(), calls=%async_computation.22 | async-start | bytes 2359296
  485.7 20.9 %copy-start.3 = (f32[256,2048]{1,0:T(8,128)S(1)}, f32[256,2048]{1,0:T(8,128)}, u32[]{:S(2)}) copy-start(f32[256,2048]{1,0:T(8,128)} %copy-done.2) | copy-start | bytes 6291460
  506.6 39.7 %copy-start.8 = (bf16[1,2048,1024]{2,1,0:T(8,128)(2,1)S(1)}, bf16[1,2048,1024]{2,1,0:T(8,128)(2,1)}, u32[]{:S(2)}) copy-start(bf16[1,2048,1024]{2,1,0:T(8,128)(2,1)} %all-gather.23.cloned.1.call-done) | copy-start | bytes 12582916
  506.6 39.7 %copy-start.12 = (f32[1024,1]{0,1:T(1,128)S(1)}, f32[1024,1]{0,1:T(1,128)}, u32[]{:S(2)}) copy-start(f32[1024,1]{0,1:T(1,128)} %copy-done.11) | copy-start | bytes 12292
  506.6 39.7 %copy-start.14 = (f32[2048]{0:T(1024)S(1)}, f32[2048]{0:T(1024)}, u32[]{:S(2)}) copy-start(f32[2048]{0:T(1024)} %copy-done.13) | copy-start | bytes 24580
  557.6 93.1 %all-gather.31.cloned.1.call-start = ((), (), s32[]{:S(2)}) async-start(), calls=%async_computation.21 | async-start | bytes 3932160 | tf_op jit(solution)/shard_map/all_gather | solution.py:315
  569.1 137.5 %reduce-scatter.13.cloned.1.call-start = ((), (), s32[]{:S(2)}) async-start(), calls=%async_computation.14 | async-start | bytes 5242880 | tf_op jit(solution)/shard_map/reduce_scatter | solution.py:259
  576.9 1.2 copy-start.4
  576.9 174.9 %all-gather.29.cloned.1.call-start = ((), (), s32[]{:S(2)}) async-start(), calls=%async_computation.20 | async-start | bytes 1310720 | tf_op jit(solution)/shard_map/all_gather | solution.py:315
  677.5 71.5 %copy-start.7 = (f32[512,1024]{1,0:T(8,128)S(1)}, f32[512,1024]{1,0:T(8,128)}, u32[]{:S(2)}) copy-start(f32[512,1024]{1,0:T(8,128)} %copy-done.5) | copy-start | bytes 6291460
Sparse Core Ops, SparseCore 0:
  9.9 55.3 all-gather.22
  67.5 27.1 all-gather.14
  96.8 28.2 all-gather.16
  127.1 47.3 all-gather.20
  176.8 51.5 all-gather.18
  230.3 30.8 all-gather.24
  263.0 51.7 all-gather.26
  344.2 52.6 reduce-scatter.10
  400.2 52.6 reduce-scatter.8
  460.8 35.8 reduce-scatter.14
  499.1 69.9 reduce-scatter.16
  571.9 34.1 reduce-scatter.18
  608.1 42.6 all-gather.30
  653.9 52.6 reduce-scatter.12
  708.9 26.5 all-gather.28

commit v2 on v1

--- a/solution.py
+++ b/solution.py
@@ -230,9 +230,236 @@
     input_grad = inv_scale * scaled - values * inv_scale**3 * jnp.mean(values * scaled, axis=-1, keepdims=True)
     return (input_grad, gain_grad)
 
+MESH = pl.DeviceIdType.MESH
+TN = (((0,), (0,)), ((), ()))
+TILE = 256
+
+
+def seq_peers():
+    mine = lax.axis_index("seq")
+    return mine, (mine + 1 - 2 * lax.rem(mine, 2), lax.rem(mine + 2, 4), 3 - mine)
+
+
+def greet(peers, axis):
+    barrier = pltpu.get_barrier_semaphore()
+    for peer in peers:
+        pl.semaphore_signal(barrier, inc=1, device_id={axis: peer}, device_id_type=MESH)
+    pl.semaphore_wait(barrier, len(peers))
+
+
+def middle_kernel(out_ref, x_ref, weight_ref, gain_ref, dy0_ref, dy1_ref, dy2_ref, dy3_ref,
+                  hidden_ref, branch_ref, grad_gate_up_ref, grad_down_ref, grad_out_ref, dh_ref, do_ref, gain_grad_ref,
+                  heads_ref, normed_ref, act_ref, dgu_ref, give_ref, take_ref, own_ref, do_give_ref,
+                  send_sem, recv_sem):
+    low = jnp.bfloat16
+    rows, model = x_ref.shape
+    width = out_ref.shape[1]
+    units = grad_down_ref.shape[1]
+    gate_at, up_at, down_at = model, model + units, model + 2 * units
+    dy_refs = (dy0_ref, dy1_ref, dy2_ref, dy3_ref)
+    mine, peers = seq_peers()
+    half = rows // 2
+    top, bottom = pl.ds(0, half), pl.ds(half, half)
+
+    def send(index, src, dst, peer):
+        return pltpu.make_async_remote_copy(
+            src_ref=src, dst_ref=dst, send_sem=send_sem.at[index], recv_sem=recv_sem.at[index],
+            device_id={"seq": peer}, device_id_type=MESH)
+
+    def rows_of(peer, size):
+        return pl.ds(pl.multiple_of(peer * size, size), size)
+
+    def tiles(count, body):
+        def step(i, carry):
+            body(pl.multiple_of(i * TILE, TILE))
+            return carry
+        lax.fori_loop(0, count // TILE, step, 0)
+
+    greet(peers, "seq")
+    turn = [send(k, out_ref.at[rows_of(peer, rows), :], heads_ref.at[k], peer) for k, peer in enumerate(peers)]
+    for k in (2, 0, 1):
+        turn[k].start()
+
+    def project(source, peer, base):
+        def body(c):
+            cols = pl.ds(c, TILE)
+            hidden_ref[:, cols] = base(cols) + dot(source, weight_ref[rows_of(peer, width), cols])
+        tiles(model, body)
+
+    project(out_ref[rows_of(mine, rows), :], mine, lambda cols: x_ref[:, cols].astype(jnp.float32))
+    for k, peer in enumerate(peers):
+        turn[k].wait()
+        project(heads_ref[k], peer, lambda cols: hidden_ref[:, cols])
+
+    def norm(i, carry):
+        part = pl.ds(pl.multiple_of(i * 128, 128), 128)
+        h = hidden_ref[part, :]
+        normed_ref[0, part, :] = (h * rms_scale(h) * gain_ref[...]).astype(low)
+        return carry
+
+    lax.fori_loop(0, rows // 128, norm, 0)
+
+    px, py, pd = peers
+    x_top = send(3, normed_ref.at[0, top], normed_ref.at[1, top], px)
+    y_bottom = send(4, normed_ref.at[0, bottom], normed_ref.at[2, bottom], py)
+    x_bottom = send(5, normed_ref.at[0, bottom], normed_ref.at[1, bottom], px)
+    y_top = send(6, normed_ref.at[0, top], normed_ref.at[2, top], py)
+    for copy in (x_top, y_bottom, x_bottom, y_top):
+        copy.start()
+
+    def feed(slot):
+        def body(f):
+            gate = dot(normed_ref[slot], weight_ref[:, pl.ds(gate_at + f, TILE)])
+            up = dot(normed_ref[slot], weight_ref[:, pl.ds(up_at + f, TILE)])
+            grad_act = dot(dy_refs[slot][...], weight_ref[:, pl.ds(down_at + f, TILE)])
+            sigmoid = jax.nn.sigmoid(gate)
+            silu = gate * sigmoid
+            act_ref[slot, :, pl.ds(f, TILE)] = (silu * up).astype(low)
+            dgu_ref[slot, :, pl.ds(f, TILE)] = (
+                grad_act * up * sigmoid * (1.0 + gate * (1.0 - sigmoid))).astype(low)
+            dgu_ref[slot, :, pl.ds(units + f, TILE)] = (grad_act * silu).astype(low)
+        tiles(units, body)
+
+    def back(slot, store):
+        def body(c):
+            cols = pl.ds(c, TILE)
+            store(cols, dot(dgu_ref[slot], weight_ref[cols, gate_at:down_at], NT))
+        tiles(model, body)
+
+    def keep(cols, value):
+        own_ref[:, cols] = value
+
+    def branch(slot):
+        def body(c):
+            cols = pl.ds(c, TILE)
+            branch_ref[slot, :, cols] = dot(act_ref[slot], weight_ref[cols, down_at:], NT).astype(low)
+        tiles(model, body)
+
+    feed(0)
+    back(0, keep)
+    x_top.wait_recv()
+    x_relay = send(7, normed_ref.at[1, top], normed_ref.at[3, top], py)
+    x_relay.start()
+    y_bottom.wait_recv()
+    y_relay = send(8, normed_ref.at[2, bottom], normed_ref.at[3, bottom], px)
+    y_relay.start()
+    branch(0)
+    partials = [send(9 + k, give_ref.at[k], take_ref.at[k], peer) for k, peer in enumerate(peers)]
+    waits = ((x_bottom,), (y_top,), (x_relay, y_relay))
+    for k in range(3):
+        for copy in waits[k]:
+            copy.wait_recv()
+        feed(k + 1)
+
+        def hand(cols, value, k=k):
+            give_ref[k, :, cols] = value.astype(low)
+
+        back(k + 1, hand)
+        partials[k].start()
+    for copy in (x_top, y_bottom, x_bottom, y_top, x_relay, y_relay):
+        copy.wait_send()
+
+    def gate_up_grad(f):
+        for d in range(0, model, 512):
+            part = pl.ds(d, 512)
+            acc = dot(normed_ref[0, :, part], dgu_ref[0, :, pl.ds(f, TILE)], TN)
+            for slot in range(1, 4):
+                acc += dot(normed_ref[slot, :, part], dgu_ref[slot, :, pl.ds(f, TILE)], TN)
+            grad_gate_up_ref[part, pl.ds(f, TILE)] = acc.astype(low)
+
+    tiles(2 * units, gate_up_grad)
+    for slot in range(1, 4):
+        branch(slot)
+    for copy in partials:
+        copy.wait()
+
+    gain_grad_ref[...] = jnp.zeros_like(gain_grad_ref)
+
+    def norm_back(i, carry):
+        part = pl.ds(pl.multiple_of(i * 64, 64), 64)
+        h = hidden_ref[part, :]
+        inv = rms_scale(h)
+        grad = own_ref[part, :]
+        for k in range(3):
+            grad += take_ref[k, part, :].astype(jnp.float32)
+        gain_grad_ref[0:1, :] += jnp.sum(grad * h * inv, axis=0, keepdims=True)
+        scaled = grad * gain_ref[...]
+        dh = dy0_ref[part, :].astype(jnp.float32) + (
+            inv * scaled - h * inv**3 * jnp.mean(h * scaled, axis=-1, keepdims=True))
+        dh_ref[part, :] = dh
+        normed_ref[1, part, :] = dh.astype(low)
+        return carry
+
+    lax.fori_loop(0, rows // 64, norm_back, 0)
+
+    sends = [send(12 + k, do_give_ref.at[k], do_ref.at[rows_of(mine, rows), :], peer) for k, peer in enumerate(peers)]
+    for k in (2, 0, 1):
+        do_give_ref[k] = dot(normed_ref[1], weight_ref[rows_of(peers[k], width), :model], NT).astype(low)
+        sends[k].start()
+    do_ref[rows_of(mine, rows), :] = dot(normed_ref[1], weight_ref[rows_of(mine, width), :model], NT).astype(low)
+
+    def down_grad(f):
+        for d in range(0, model, 512):
+            part = pl.ds(d, 512)
+            acc = dot(dy_refs[0][:, part], act_ref[0, :, pl.ds(f, TILE)], TN)
+            for slot in range(1, 4):
+                acc += dot(dy_refs[slot][:, part], act_ref[slot, :, pl.ds(f, TILE)], TN)
+            grad_down_ref[part, pl.ds(f, TILE)] = acc.astype(low)
+
+    tiles(units, down_grad)
+    grad_out_ref[rows_of(mine, width), :] = dot(out_ref[rows_of(mine, rows), :], normed_ref[1], TN).astype(low)
+    for k, peer in enumerate(peers):
+        grad_out_ref[rows_of(peer, width), :] = dot(heads_ref[k], normed_ref[1], TN).astype(low)
+    for copy in sends:
+        copy.wait()
+
+
+def middle(dealt_out, x, weights, gain, dy, units):
+    low = jnp.bfloat16
+    group_len, width = dealt_out.shape
+    rows, model = x.shape
+    f32 = jnp.float32
+    shape = jax.ShapeDtypeStruct
+    return pl.pallas_call(
+        middle_kernel,
+        name="middle",
+        out_shape=(
+            shape((rows, model), f32),
+            shape((4, rows, model), low),
+            shape((model, 2 * units), low),
+            shape((model, units), low),
+            shape((model, model), low),
+            shape((rows, model), f32),
+            shape((group_len, width), low),
+            shape((8, model), f32),
+        ),
+        in_specs=[vmem()] * 8,
+        out_specs=(vmem(),) * 8,
+        scratch_shapes=[
+            pltpu.VMEM((3, rows, width), low),
+            pltpu.VMEM((4, rows, model), low),
+            pltpu.VMEM((4, rows, units), low),
+            pltpu.VMEM((4, rows, 2 * units), low),
+            pltpu.VMEM((3, rows, model), low),
+            pltpu.VMEM((3, rows, model), low),
+            pltpu.VMEM((rows, model), f32),
+            pltpu.VMEM((3, rows, width), low),
+            pltpu.SemaphoreType.DMA((15,)),
+            pltpu.SemaphoreType.DMA((15,)),
+        ],
+        compiler_params=pltpu.CompilerParams(
+            vmem_limit_bytes=62 << 20, collective_id=1, has_side_effects=True),
+        cost_estimate=pl.CostEstimate(flops=60_000_000_000, bytes_accessed=40 << 20, transcendentals=0),
+    )(dealt_out, x, weights, gain, *dy)
+
 
 def matmul(spec, left, right):
     return jnp.einsum(spec, left, right, preferred_element_type=jnp.float32)
+
+
+def swaps(rows):
+    return [lax.ppermute(piece, "seq", table) for piece, table in zip(
+        rows, ([(i, i ^ 1) for i in range(4)], [(i, (i + 2) % 4) for i in range(4)], [(i, 3 - i) for i in range(4)]))]
 
 
 def on_device(block_input, norm_gain_a, weight_qkv, weight_out, norm_gain_b, weight_gate_up, weight_down,
@@ -262,52 +489,26 @@
     gain_a, gain_b = gains[:, 0], gains[:, 1]
     rows_all = gather_rows(block_input[0])
     part_qkv = gather_weight(columns(weight_qkv, 3, head_width))
-    full_out = gather_weight(weight_out.astype(low))
-    part_gate_up = gather_weight(columns(weight_gate_up, 2, part_units))
-    part_down = gather_weight(columns(weight_down, 1, part_units))
-    grad_rows_all = gather_rows(cotangent[0])
+    weights = gather_weight(jnp.concatenate(
+        [weight_out.astype(low), columns(weight_gate_up, 2, part_units), columns(weight_down, 1, part_units)], axis=1))
+    grad_rows = [cotangent[0]] + swaps([cotangent[0]] * 3)
 
     wide_all = rows_all.astype(jnp.float32)
     normed_a = (wide_all * rms_scale(wide_all) * gain_a).astype(low)
     qkv = matmul("rd,de->re", normed_a, part_qkv).astype(low)
     ordered, dealt_out, wide_out, log_total = attention_forward(offs, qkv, perm, start)
-    mixed = lax.all_to_all(
-        dealt_out.reshape(group_len, 1, head_width), "seq", split_axis=0, concat_axis=1, tiled=True
-    ).reshape(row_count, model_width)
-    inputs = block_input[0].astype(jnp.float32)
-    inv_first = rms_scale(inputs)
-    hidden = inputs + matmul("rd,de->re", mixed, full_out)
-    inv_second = rms_scale(hidden)
-    normed_b = gather_rows((hidden * inv_second * gain_b).astype(low))
-
-    gate_up = matmul("rd,df->rf", normed_b, part_gate_up)
-    gate_part, up_part = gate_up[:, :part_units], gate_up[:, part_units:]
-    gate_sigmoid = jax.nn.sigmoid(gate_part)
-    gate_silu = gate_part * gate_sigmoid
-    activation = (gate_silu * up_part).astype(low)
-    branch_out = scatter_rows(matmul("rf,df->rd", activation, part_down)).astype(jnp.float32)
-    result_rows = (hidden + branch_out).astype(low)
-
-    grad_activation = matmul("rd,df->rf", grad_rows_all, part_down)
-    grad_gate = grad_activation * up_part * gate_sigmoid * (1.0 + gate_part * (1.0 - gate_sigmoid))
-    grad_up = grad_activation * gate_silu
-    grad_gate_up = jnp.concatenate([grad_gate, grad_up], axis=1).astype(low)
-    grad_normed_b = scatter_rows(matmul("rf,df->rd", grad_gate_up, part_gate_up)).astype(jnp.float32)
-    down_term = matmul("rd,rf->df", grad_rows_all, activation)
-    gate_up_term = matmul("rd,rf->df", normed_b, grad_gate_up)
-    hidden_back, gain_b_term = norm_backward(hidden, inv_second, grad_normed_b, gain_b)
-    grad_hidden = cotangent[0].astype(jnp.float32) + hidden_back
-    grad_branch = grad_hidden.astype(low)
-    grad_mixed = matmul("re,de->rd", grad_branch, full_out).astype(low)
-    grad_heads = lax.all_to_all(
-        grad_mixed.reshape(row_count, seq_count, head_width), "seq", split_axis=1, concat_axis=0, tiled=True
-    ).reshape(group_len, head_width)
+    hidden, branch, gate_up_term, down_term, out_term, grad_hidden, grad_heads, gain_b_term = middle(
+        dealt_out, block_input[0], weights, gain_b.reshape(1, model_width), grad_rows, part_units)
+    branch_sum = branch[0].astype(jnp.float32)
+    for piece in swaps([branch[k] for k in (1, 2, 3)]):
+        branch_sum = branch_sum + piece.astype(jnp.float32)
+    result_rows = (hidden + branch_sum).astype(low)
     dealt_grad = attention_backward(offs, grad_heads, ordered, perm, start, wide_out, log_total)
-    out_term = matmul("rd,re->de", mixed, grad_branch)
-    out_part = lax.psum_scatter(out_term.astype(low), "seq", scatter_dimension=1, tiled=True)
+    out_part = lax.psum_scatter(out_term, "seq", scatter_dimension=1, tiled=True)
     qkv_term = matmul("rd,re->de", normed_a, dealt_grad)
     grad_normed_a = scatter_rows(matmul("re,de->rd", dealt_grad, part_qkv)).astype(jnp.float32)
-    input_back, gain_a_term = norm_backward(inputs, inv_first, grad_normed_a, gain_a)
+    inputs = block_input[0].astype(jnp.float32)
+    input_back, gain_a_term = norm_backward(inputs, rms_scale(inputs), grad_normed_a, gain_a)
     input_grad = (grad_hidden + input_back).astype(low)
 
     def finish(term):
@@ -321,7 +522,7 @@
 
     grad_mlp = finish(jnp.concatenate([gate_up_term, down_term], axis=1))
     grad_attn = finish(jnp.concatenate([qkv_term.astype(low), out_part], axis=1))
-    gain_terms = lax.psum(jnp.stack([gain_a_term, gain_b_term]), ("seq", "fsdp"))
+    gain_terms = lax.psum(jnp.stack([gain_a_term, gain_b_term[0]]), ("seq", "fsdp"))
     gain_terms = lax.dynamic_slice_in_dim(gain_terms, lax.axis_index("fsdp") * shard, shard, axis=1)
     return (
         result_rows[None],

time: 773 us -> 719 us (0.930)
  Pallas kernels: 80.2 us -> 209 us
  matrix products: 106 us -> 21.7 us
  waiting for transfers between devices: 387 us -> 318 us
  blocking collectives: 88.6 us -> 51.8 us
    pallas_call x0 -> x1, Pallas kernels: none -> 129 us  [middle(): pl.pallas_call(middle_kernel, name='middle', out_shape=(shape((rows, mode...]
    reduce_scatter x3 -> x1, waiting for transfers between devices: 123 us -> 17.1 us  [on_device(): lax.psum_scatter(part.astype(low), 'seq', scatter_dimension=0, tiled=True)]
    dot_general x12 -> x3, matrix products: 106 us -> 21.7 us  [matmul(): return jnp.einsum(spec, left, right, preferred_element_type=jnp.float32)]
    all_gather x3 -> x1, waiting for transfers between devices: 136 us -> 58.9 us  [on_device(): gather_rows = lambda rows: lax.all_gather(rows, 'seq', axis=0, tiled=True)]
    ppermute x0 -> x6, waiting for transfers between devices: none -> 64.4 us  [swaps(): lax.ppermute(piece, 'seq', table)]
    reduce_scatter x1, waiting for transfers between devices: 11.4 us -> 68.8 us  [finish(): lax.psum_scatter(term.astype(low), 'fsdp', scatter_dimension=0, tiled=True)]
    all_to_all x2 -> x0, blocking collectives: 35.5 us -> none  [the longest x1 17.9 us: on_device(): lax.all_to_all(dealt_out.reshape(group_len, 1, head_width), 'seq', split_...]
    all_gather x4 -> x2, waiting for transfers between devices: 44 us -> 63.6 us  [on_device(): lax.all_gather(piece, 'fsdp', axis=0, tiled=True)]
  transfers between devices with their start and end apart: 15 -> 15, of which waited for: 11 -> 10; matrix products, arithmetic and copies ran while one was open for 19% -> 9% of each run, Pallas kernels for 10% -> 11%
where the time goes in v2:
time: 719 us; the launch traced here: 711 us
  waiting for transfers between devices  318 us (44%)
  Pallas kernels  209 us (29%)
  local copies, waits for them, and re-layouts  60.1 us (8%)
  blocking collectives  51.8 us (7%)
  other arithmetic  26.8 us (4%)
  matrix products  21.7 us (3%)
  between operations  14.3 us (2%)
  starting transfers between devices  8.47 us (1%)
    pallas_call x1, Pallas kernels, middle(): pl.pallas_call(middle_kernel, name='middle', out_shape=(shape((rows, mode...  129 us
    reduce_scatter x1, waiting for transfers between devices, finish(): lax.psum_scatter(term.astype(low), 'fsdp', scatter_dimension=0, tiled=True)  68.8 us
    ppermute x6, waiting for transfers between devices, swaps(): lax.ppermute(piece, 'seq', table)  64.4 us
    all_gather x2, waiting for transfers between devices, on_device(): lax.all_gather(piece, 'fsdp', axis=0, tiled=True)  63.6 us
    all_gather x1, waiting for transfers between devices, on_device(): gather_rows = lambda rows: lax.all_gather(rows, 'seq', axis=0, tiled=True)  58.9 us
    pallas_call x1, Pallas kernels, attention_forward(): pl.pallas_call(forward_kernel, name='attention_forward', out_shape=(jax.S...  40.9 us
    pallas_call x1, Pallas kernels, attention_backward(): pl.pallas_call(backward_kernel, name='attention_backward', out_shape=jax....  39.9 us
    psum x1, blocking collectives, on_device(): lax.psum(jnp.stack([gain_a_term, gain_b_term[0]]), ('seq', 'fsdp'))  39.4 us
  transfers between devices with their start and end apart: 15, of which 10 were waited for; matrix products, arithmetic and copies ran while one was open for 9% of the time, Pallas kernels for 11%

profile of v2, /device:TPU:0, one launch (start us, length us, event | category | flops | bytes accessed | tf_op | source)
XLA Modules:
  0.0 710.6 jit_solution(7987454851106450235)
XLA Ops:
  8.0 1.8 copy.56
  10.5 3.3 reshape.93
  16.5 1.4 copy.59
  20.8 2.9 collective-permute-start
  23.7 1.5 collective-permute-start.1
  25.2 12.4 %all_gather.25 = bf16[1024,2]{0,1:T(2,128)(2,1)S(1)} all-gather(bf16[128,2]{0,1:T(2,128)(2,1)S(1)} %pad_maximum_fusion.4), channel_id=1, replica_groups=mesh['seq'=4,'fsdp'=8] {'fsdp'}, dimensions={0}, use_global_device_ids=true | all-gather | bytes 4608 | tf_op jit(solution)/shard_map/all_gather | solution.py:484
  38.7 58.9 %all-gather.13.cloned.1.call-done = bf16[1,2048,1024]{2,1,0:T(8,128)(2,1)} async-done(((bf16[1,512,1024]{2,1,0:T(8,128)(2,1)}), bf16[1,2048,1024]{2,1,0:T(8,128)(2,1)}) %all-gather.13.cloned.1.call-update) | async-done | bytes 4194320 | tf_op jit(solution)/shard_map/all_gather | solution.py:485
  97.6 3.1 fusion
  100.7 31.2 %all-gather.9.cloned.1.call-done = bf16[1024,768]{0,1:T(8,128)(2,1)} async-done(((bf16[128,768]{0,1:T(8,128)(2,1)}), bf16[1024,768]{0,1:T(8,128)(2,1)}) %all-gather.9.cloned.1.call-update) | async-done | bytes 1572880 | tf_op jit(solution)/shard_map/all_gather | solution.py:484
  131.9 7.9 %convolution_convert_fusion.1.qkv_ref = bf16[2048,768]{1,0:T(8,128)(2,1)} fusion(bf16[1024,768]{0,1:T(8,128)(2,1)} %all-gather.9.cloned.1.call-done, bf16[1,2048,1024]{2,1,0:T(8,128)(2,1)} %all-gather.13.cloned.1.call-done, f32[1024]{0:T(1024)S(1)} %bitcast.106, f32[2048]{0:T(1024)S(1)} %add_rsqrt_fusion), kind=kOutput, calls=%fused_computation.12 | convolution fusion | flops 3231186944 | bytes 8925184 | tf_op jit(solution)/shard_map/rd,de->re/dot_general | solution.py:457
  139.8 40.9 %attention_forward.1 = (bf16[2048,768]{1,0:T(8,128)(2,1)}, bf16[2048,256]{1,0:T(8,128)(2,1)S(1)}, f32[256,2048]{1,0:T(8,128)S(1)}, f32[8,2048]{1,0:T(8,128)S(1)}) custom-call(s32[3]{0:T(128)S(1)} %bitcast.88, bf16[2048,768]{1,0:T(8,128)(2,1)} %convolution_convert_fusion.1.qkv_ref, s32[1,2048]{1,0:T(1,128)S(1)} %copy-done, s32[2048,1]{1,0:T(8,128)S(1)} %copy.57.perm_col_ref, ...), custom_call_target="tpu_custom_call" | custom-call | flops 20000000000 | bytes 16777216 | tf_op jit(solution)/shard_map/attention_forward/pallas_call | solution.py:181
  180.7 1.3 copy-done.2
  183.0 32.4 %all-gather.11.cloned.1.call-done.weight_ref = bf16[1024,4096]{1,0:T(8,128)(2,1)} async-done(((bf16[128,4096]{1,0:T(8,128)(2,1)}), bf16[1024,4096]{1,0:T(8,128)(2,1)}) %all-gather.11.cloned.1.call-update) | async-done | bytes 8388624 | tf_op jit(solution)/shard_map/all_gather | solution.py:484
  215.4 128.7 %middle.1 = (f32[512,1024]{1,0:T(8,128)}, bf16[4,512,1024]{2,1,0:T(8,128)(2,1)}, bf16[1024,2048]{1,0:T(8,128)(2,1)}, bf16[1024,1024]{1,0:T(8,128)(2,1)}, bf16[10...) custom-call(bf16[2048,256]{1,0:T(8,128)(2,1)} %copy-done.4, ...), custom_call_target="tpu_custom_call" | custom-call | flops 60000002048 | bytes 41943040 | tf_op jit(solution)/shard_map/middle/pallas_call | solution.py:423
  345.3 1.6 copy-done.3
  346.9 39.9 %attention_backward.1 = bf16[2048,768]{1,0:T(8,128)(2,1)} custom-call(s32[3]{0:T(128)S(1)} %bitcast.89, bf16[2048,256]{1,0:T(8,128)(2,1)S(1)} %copy-done.5, bf16[2048,768]{1,0:T(8,128)(2,1)} %get-tuple-element.25.sorted_ref, s32[1,2048]{1,0:T(1,128)S(1)} %copy-done, s32[2048,1]{1,0:T(8,128)S(1)} %copy.57.perm_col_ref, s32[1,2048]{1,0:T(1,128)S(1)} %bitcast.86, ...), custom_call_target="tpu_custom_call" | custom-call | flops 40000000000 | bytes 16777216 | tf_op jit(solution)/shard_map/attention_backward/pallas_call | solution.py:201
  386.8 7.0 convolution_convert_fusion.2
  393.8 1.2 copy.62
  395.0 1.6 pad_maximum_fusion.1
  396.6 2.6 copy.67
  399.3 1.5 copy-done.11
  400.8 5.4 pad_maximum_fusion
  406.3 1.3 copy-done.13
  407.6 6.8 convolution_convert_fusion
  414.7 19.9 %reduce-scatter.13.cloned.1.call-done = bf16[128,1024]{1,0:T(8,128)(2,1)} async-done(((bf16[1024,1024]{1,0:T(8,128)(2,1)}), bf16[128,1024]{1,0:T(8,128)(2,1)}) %reduce-scatter.13.cloned.1.call-update) | async-done | bytes 262160
  434.6 1.8 copy.68
  436.4 68.8 %reduce-scatter.11.cloned.1.call-done = bf16[128,3072]{1,0:T(8,128)(2,1)} async-done(((bf16[1024,3072]{1,0:T(8,128)(2,1)}), bf16[128,3072]{1,0:T(8,128)(2,1)}) %reduce-scatter.11.cloned.1.call-update) | async-done | bytes 786448 | tf_op jit(solution)/shard_map/reduce_scatter | solution.py:515
  505.3 3.7 slice_bitcast_fusion.3
  509.0 1.5 collective-permute-start.3
  510.5 1.5 collective-permute-start.4
  513.6 41.2 %collective-permute-done.3 = bf16[512,1024]{1,0:T(8,128)(2,1)} collective-permute-done((bf16[512,1024]{1,0:T(8,128)(2,1)}, bf16[512,1024]{1,0:T(8,128)(2,1)}, u32[]{:S(2)}, u32[]{:S(2)}) %collective-permute-start.3) | collective-permute-done | bytes 1048608 | tf_op jit(solution)/shard_map/ppermute | solution.py:461
  554.8 21.6 %collective-permute-done.4 = bf16[512,1024]{1,0:T(8,128)(2,1)} collective-permute-done((bf16[512,1024]{1,0:T(8,128)(2,1)}, bf16[512,1024]{1,0:T(8,128)(2,1)}, u32[]{:S(2)}, u32[]{:S(2)}) %collective-permute-start.4) | collective-permute-done | bytes 1048608 | tf_op jit(solution)/shard_map/ppermute | solution.py:461
  576.4 1.6 collective-permute-done.5
  578.0 4.2 fusion.18
  582.2 17.1 %reduce-scatter.7.cloned.1.call-done = bf16[512,1024]{1,0:T(8,128)(2,1)} async-done(((bf16[2048,1024]{1,0:T(8,128)(2,1)}), bf16[512,1024]{1,0:T(8,128)(2,1)}) %reduce-scatter.7.cloned.1.call-update) | async-done | bytes 1048592 | tf_op jit(solution)/shard_map/reduce_scatter | solution.py:486
  599.3 2.2 fusion.11
  601.5 39.4 %psum.7 = f32[2,1024]{1,0:T(2,128)S(1)} all-reduce(f32[2,1024]{1,0:T(2,128)S(1)} %pad_maximum_fusion.3), channel_id=1, replica_groups=mesh['seq'=4,'fsdp'=8] {'seq','fsdp'}, use_global_device_ids=true, to_apply=%region_6.7 | all-reduce | flops 2048 | bytes 16384 | tf_op jit(solution)/shard_map/psum | solution.py:525
  641.5 3.2 fusion.19
  644.7 1.3 reshape.105
  647.0 2.0 reshape.96
  650.1 24.3 %all-gather.17.cloned.1.call-done = bf16[512,3072]{1,0:T(8,128)(2,1)} async-done(((bf16[128,3072]{1,0:T(8,128)(2,1)}), bf16[512,3072]{1,0:T(8,128)(2,1)}) %all-gather.17.cloned.1.call-update) | async-done | bytes 3145744 | tf_op jit(solution)/shard_map/all_gather | solution.py:516
  674.4 4.1 slice_convert_fusion
  678.6 1.5 convert_bitcast_fusion
  680.0 6.6 reshape.102
  686.6 6.9 copy.77
  693.5 6.0 reshape.98
  699.5 1.4 copy.66
  700.9 3.0 copy.73
  (82 shorter events, 15.0 us)
Async XLA Ops:
  7.2 90.4 %all-gather.13.cloned.1.call-start = ((), (), s32[]{:S(2)}) async-start(), calls=%async_computation.9 | async-start | bytes 5242880 | tf_op jit(solution)/shard_map/all_gather | solution.py:485
  7.9 124.0 %all-gather.9.cloned.1.call-start = ((), (), s32[]{:S(2)}) async-start(), calls=%async_computation.4 | async-start | bytes 1769472 | tf_op jit(solution)/shard_map/all_gather | solution.py:484
  10.5 204.9 %all-gather.11.cloned.1.call-start = ((), (), s32[]{:S(2)}) async-start(), calls=%async_computation.5 | async-start | bytes 9437184 | tf_op jit(solution)/shard_map/all_gather | solution.py:484
  14.9 1.6 copy-start.10
  16.5 2.5 copy-start.12
  19.0 1.7 copy-start.14
  19.0 6.2 copy-start.15
  19.0 6.2 copy-start.16
  19.1 18.6 %copy-start = (s32[1,2048]{1,0:T(1,128)S(1)}, s32[1,2048]{1,0:T(1,128)}, u32[]{:S(2)}) copy-start(s32[1,2048]{1,0:T(1,128)} %perm_row_ref.3) | copy-start | bytes 24580
  19.1 18.9 %copy-start.1 = (s32[1,3]{1,0:T(1,128)S(1)}, s32[1,3]{1,0:T(1,128)}, u32[]{:S(2)}) copy-start(s32[1,3]{1,0:T(1,128)} %param.20) | copy-start | bytes 40
  20.2 373.6 %reduce-scatter.9.cloned.1.call-start = ((), (), s32[]{:S(2)}) async-start(), calls=%async_computation.7 | async-start | bytes 2621440 | tf_op jit(solution)/shard_map/reduce_scatter | solution.py:507
  20.8 162.2 %collective-permute-start = (bf16[512,1024]{1,0:T(8,128)(2,1)S(1)}, bf16[512,1024]{1,0:T(8,128)(2,1)}, u32[]{:S(2)}, u32[]{:S(2)}) collective-permute-start(bf16[512,1024]{1,0:T(8,128)(2,1)S(1)} %bitcast.112), channel_id=1, source_target_pairs={{0,8},{8,0},{16,24},{24,16},{1,9},{9,1},{17,25},{25,17},{2,10},{10... | collective-permute-start | bytes 3145736 | tf_op jit(solution)/shard_map/ppermute | solution.py:461
  23.7 159.3 %collective-permute-start.1 = (bf16[512,1024]{1,0:T(8,128)(2,1)S(1)}, bf16[512,1024]{1,0:T(8,128)(2,1)}, u32[]{:S(2)}, u32[]{:S(2)}) collective-permute-start(bf16[512,1024]{1,0:T(8,128)(2,1)S(1)} %bitcast.113), channel_id=1, source_target_pairs={{0,16},{8,24},{16,0},{24,8},{1,17},{9,25},{17,1},{25,9},{2,18},{10... | collective-permute-start | bytes 3145736 | tf_op jit(solution)/shard_map/ppermute | solution.py:461
  25.2 157.8 %collective-permute-start.2 = (bf16[512,1024]{1,0:T(8,128)(2,1)S(1)}, bf16[512,1024]{1,0:T(8,128)(2,1)}, u32[]{:S(2)}, u32[]{:S(2)}) collective-permute-start(bf16[512,1024]{1,0:T(8,128)(2,1)S(1)} %bitcast.114), channel_id=1, source_target_pairs={{0,24},{8,16},{16,8},{24,0},{1,25},{9,17},{17,9},{25,1},{2,26},{10... | collective-permute-start | bytes 3145736 | tf_op jit(solution)/shard_map/ppermute | solution.py:461
  180.7 1.3 copy-start.2
  182.0 1.0 copy-start.4
  344.1 1.2 copy-start.5
  344.1 90.4 %reduce-scatter.13.cloned.1.call-start = ((), (), s32[]{:S(2)}) async-start(), calls=%async_computation.12 | async-start | bytes 2359296
  345.3 1.6 copy-start.3
  346.9 39.9 %copy-start.8 = (bf16[1,2048,1024]{2,1,0:T(8,128)(2,1)S(1)}, bf16[1,2048,1024]{2,1,0:T(8,128)(2,1)}, u32[]{:S(2)}) copy-start(bf16[1,2048,1024]{2,1,0:T(8,128)(2,1)} %all-gather.13.cloned.1.call-done) | copy-start | bytes 12582916
  399.2 1.6 copy-start.11
  399.2 106.0 %reduce-scatter.11.cloned.1.call-start = ((), (), s32[]{:S(2)}) async-start(), calls=%async_computation.8 | async-start | bytes 7077888 | tf_op jit(solution)/shard_map/reduce_scatter | solution.py:515
  406.2 1.4 copy-start.13
  406.2 193.1 %reduce-scatter.7.cloned.1.call-start = ((), (), s32[]{:S(2)}) async-start(), calls=%async_computation.6 | async-start | bytes 5242880 | tf_op jit(solution)/shard_map/reduce_scatter | solution.py:486
  414.5 230.2 %all-gather.15.cloned.1.call-start = ((), (), s32[]{:S(2)}) async-start(), calls=%async_computation.10 | async-start | bytes 1310720 | tf_op jit(solution)/shard_map/all_gather | solution.py:516
  436.4 238.1 %all-gather.17.cloned.1.call-start = ((), (), s32[]{:S(2)}) async-start(), calls=%async_computation.11 | async-start | bytes 3932160 | tf_op jit(solution)/shard_map/all_gather | solution.py:516
  505.3 7.3 %copy-start.6 = (bf16[1,512,1024]{2,1,0:T(8,128)(2,1)S(1)}, bf16[1,512,1024]{2,1,0:T(8,128)(2,1)}, u32[]{:S(2)}) copy-start(bf16[1,512,1024]{2,1,0:T(8,128)(2,1)} %param.11) | copy-start | bytes 3145732
  505.3 72.7 %copy-start.9 = (f32[512,1024]{1,0:T(8,128)S(1)}, f32[512,1024]{1,0:T(8,128)}, u32[]{:S(2)}) copy-start(f32[512,1024]{1,0:T(8,128)} %get-tuple-element.21) | copy-start | bytes 6291460
  509.0 45.8 %collective-permute-start.3 = (bf16[512,1024]{1,0:T(8,128)(2,1)}, bf16[512,1024]{1,0:T(8,128)(2,1)}, u32[]{:S(2)}, u32[]{:S(2)}) collective-permute-start(bf16[512,1024]{1,0:T(8,128)(2,1)} %get-tuple-element.34), channel_id=1, source_target_pairs={{0,8},{8,0},{16,24},{24,16},{1,9},{9,1},{17,25},{25,17},{2,10},{10... | collective-permute-start | bytes 3145736 | tf_op jit(solution)/shard_map/ppermute | solution.py:461
  510.5 65.9 %collective-permute-start.4 = (bf16[512,1024]{1,0:T(8,128)(2,1)}, bf16[512,1024]{1,0:T(8,128)(2,1)}, u32[]{:S(2)}, u32[]{:S(2)}) collective-permute-start(bf16[512,1024]{1,0:T(8,128)(2,1)} %get-tuple-element.36), channel_id=1, source_target_pairs={{0,16},{8,24},{16,0},{24,8},{1,17},{9,25},{17,1},{25,9},{2,18},{10... | collective-permute-start | bytes 3145736 | tf_op jit(solution)/shard_map/ppermute | solution.py:461
  512.0 66.1 %collective-permute-start.5 = (bf16[512,1024]{1,0:T(8,128)(2,1)}, bf16[512,1024]{1,0:T(8,128)(2,1)}, u32[]{:S(2)}, u32[]{:S(2)}) collective-permute-start(bf16[512,1024]{1,0:T(8,128)(2,1)} %get-tuple-element.35), channel_id=1, source_target_pairs={{0,24},{8,16},{16,8},{24,0},{1,25},{9,17},{17,9},{25,1},{2,26},{10... | collective-permute-start | bytes 3145736 | tf_op jit(solution)/shard_map/ppermute | solution.py:461
  599.3 42.2 %copy-start.7 = (bf16[512,1024]{1,0:T(8,128)(2,1)S(1)}, bf16[512,1024]{1,0:T(8,128)(2,1)}, u32[]{:S(2)}) copy-start(bf16[512,1024]{1,0:T(8,128)(2,1)} %reduce-scatter.7.cloned.1.call-done) | copy-start | bytes 3145732
Sparse Core Ops, SparseCore 0:
  9.8 87.7 all-gather.12
  99.8 32.1 all-gather.8
  134.1 81.2 all-gather.10
  344.3 31.8 reduce-scatter.8
  399.3 35.1 reduce-scatter.12
  436.8 68.3 reduce-scatter.10
  509.1 90.2 reduce-scatter.6
  601.7 26.5 all-gather.14
  630.2 44.2 all-gather.16

commit v3 on v2

--- a/solution.py
+++ b/solution.py
@@ -224,12 +224,6 @@
     return lax.rsqrt(jnp.mean(values * values, axis=-1, keepdims=True) + epsilon)
 
 
-def norm_backward(values, inv_scale, grad_normed, gain):
-    scaled = grad_normed * gain
-    gain_grad = jnp.sum(grad_normed * values * inv_scale, axis=0)
-    input_grad = inv_scale * scaled - values * inv_scale**3 * jnp.mean(values * scaled, axis=-1, keepdims=True)
-    return (input_grad, gain_grad)
-
 MESH = pl.DeviceIdType.MESH
 TN = (((0,), (0,)), ((), ()))
 TILE = 256
@@ -240,21 +234,109 @@
     return mine, (mine + 1 - 2 * lax.rem(mine, 2), lax.rem(mine + 2, 4), 3 - mine)
 
 
-def greet(peers, axis):
+def greet(peers, others=()):
     barrier = pltpu.get_barrier_semaphore()
+    for peer in others:
+        pl.semaphore_signal(barrier, inc=1, device_id={"fsdp": peer}, device_id_type=MESH)
     for peer in peers:
-        pl.semaphore_signal(barrier, inc=1, device_id={axis: peer}, device_id_type=MESH)
-    pl.semaphore_wait(barrier, len(peers))
+        pl.semaphore_signal(barrier, inc=1, device_id={"seq": peer}, device_id_type=MESH)
+    pl.semaphore_wait(barrier, len(peers) + len(others))
+
+
+def span(index, size):
+    return pl.ds(pl.multiple_of(index * size, size), size)
+
+
+def sender(send_sem, recv_sem):
+    def send(index, src, dst, axis, peer):
+        return pltpu.make_async_remote_copy(
+            src_ref=src, dst_ref=dst, send_sem=send_sem.at[index], recv_sem=recv_sem.at[index],
+            device_id={axis: peer}, device_id_type=MESH)
+    return send
+
+
+def shard_peers(count):
+    mine = lax.axis_index("fsdp")
+    sibling = mine + 1 - 2 * lax.rem(mine, 2)
+    return mine, sibling, [lax.rem(mine + 2 * k, count) for k in range(1, count // 2)]
+
+
+def spread(send, base, own, slots, peers):
+    px, py, _ = peers
+    half = own.shape[0] // 2
+    top, bottom = pl.ds(0, half), pl.ds(half, half)
+    x_slot, y_slot, far_slot = slots
+    x_top = send(base, own.at[top], x_slot.at[top], "seq", px)
+    y_bottom = send(base + 1, own.at[bottom], y_slot.at[bottom], "seq", py)
+    x_bottom = send(base + 2, own.at[bottom], x_slot.at[bottom], "seq", px)
+    y_top = send(base + 3, own.at[top], y_slot.at[top], "seq", py)
+    x_relay = send(base + 4, x_slot.at[top], far_slot.at[top], "seq", py)
+    y_relay = send(base + 5, y_slot.at[bottom], far_slot.at[bottom], "seq", px)
+    for copy in (x_top, y_bottom, x_bottom, y_top):
+        copy.start()
+
+    def forward():
+        x_top.wait_recv()
+        x_relay.start()
+        y_bottom.wait_recv()
+        y_relay.start()
+
+    def finish():
+        for copy in (x_top, y_bottom, x_bottom, y_top, x_relay, y_relay):
+            copy.wait_send()
+
+    return forward, (x_bottom.wait_recv, y_top.wait_recv, lambda: (x_relay.wait_recv(), y_relay.wait_recv())), finish
+
+
+def collect(send, base, give, transit, take, peers):
+    px, py, _ = peers
+    half = give.shape[1] // 2
+    top, bottom = pl.ds(0, half), pl.ds(half, half)
+    far_top = send(base, give.at[2, top], transit.at[0], "seq", px)
+    far_bottom = send(base + 1, give.at[2, bottom], transit.at[1], "seq", py)
+    x_top = send(base + 2, give.at[0, top], take.at[0, top], "seq", px)
+    y_bottom = send(base + 3, give.at[1, bottom], take.at[1, bottom], "seq", py)
+    y_top = send(base + 4, give.at[1, top], take.at[1, top], "seq", py)
+    x_bottom = send(base + 5, give.at[0, bottom], take.at[0, bottom], "seq", px)
+
+    def add(k, part, t):
+        def step(i, carry):
+            rows = pl.ds(pl.multiple_of(part.start + i * 64, 64), 64)
+            more = pl.ds(pl.multiple_of(i * 64, 64), 64)
+            give[k, rows, :] = (give[k, rows, :].astype(jnp.float32)
+                                + transit[t, more, :].astype(jnp.float32)).astype(jnp.bfloat16)
+            return carry
+        lax.fori_loop(0, half // 64, step, 0)
+
+    def far():
+        far_top.start()
+        far_bottom.start()
+
+    def merge():
+        far_top.wait_recv()
+        add(1, top, 0)
+        y_top.start()
+        far_bottom.wait_recv()
+        add(0, bottom, 1)
+        x_bottom.start()
+
+    def finish():
+        for copy in (x_top, y_bottom, y_top, x_bottom):
+            copy.wait()
+        far_top.wait_send()
+        far_bottom.wait_send()
+
+    return far, x_top.start, y_bottom.start, merge, finish
 
 
 def middle_kernel(out_ref, x_ref, weight_ref, gain_ref, dy0_ref, dy1_ref, dy2_ref, dy3_ref,
-                  hidden_ref, branch_ref, grad_gate_up_ref, grad_down_ref, grad_out_ref, dh_ref, do_ref, gain_grad_ref,
+                  hidden_ref, branch_ref, grads_ref, dh_ref, do_ref, gain_grad_ref,
                   heads_ref, normed_ref, act_ref, dgu_ref, give_ref, take_ref, own_ref, do_give_ref,
                   send_sem, recv_sem):
     low = jnp.bfloat16
     rows, model = x_ref.shape
     width = out_ref.shape[1]
-    units = grad_down_ref.shape[1]
+    units = act_ref.shape[2]
     gate_at, up_at, down_at = model, model + units, model + 2 * units
     dy_refs = (dy0_ref, dy1_ref, dy2_ref, dy3_ref)
     mine, peers = seq_peers()
@@ -275,7 +357,7 @@
             return carry
         lax.fori_loop(0, count // TILE, step, 0)
 
-    greet(peers, "seq")
+    greet(peers)
     turn = [send(k, out_ref.at[rows_of(peer, rows), :], heads_ref.at[k], peer) for k, peer in enumerate(peers)]
     for k in (2, 0, 1):
         turn[k].start()
@@ -365,7 +447,7 @@
             acc = dot(normed_ref[0, :, part], dgu_ref[0, :, pl.ds(f, TILE)], TN)
             for slot in range(1, 4):
                 acc += dot(normed_ref[slot, :, part], dgu_ref[slot, :, pl.ds(f, TILE)], TN)
-            grad_gate_up_ref[part, pl.ds(f, TILE)] = acc.astype(low)
+            grads_ref[part, pl.ds(f, TILE)] = acc.astype(low)
 
     tiles(2 * units, gate_up_grad)
     for slot in range(1, 4):
@@ -404,12 +486,12 @@
             acc = dot(dy_refs[0][:, part], act_ref[0, :, pl.ds(f, TILE)], TN)
             for slot in range(1, 4):
                 acc += dot(dy_refs[slot][:, part], act_ref[slot, :, pl.ds(f, TILE)], TN)
-            grad_down_ref[part, pl.ds(f, TILE)] = acc.astype(low)
+            grads_ref[part, pl.ds(2 * units + f, TILE)] = acc.astype(low)
 
     tiles(units, down_grad)
-    grad_out_ref[rows_of(mine, width), :] = dot(out_ref[rows_of(mine, rows), :], normed_ref[1], TN).astype(low)
+    grads_ref[rows_of(mine, width), 3 * units:] = dot(out_ref[rows_of(mine, rows), :], normed_ref[1], TN).astype(low)
     for k, peer in enumerate(peers):
-        grad_out_ref[rows_of(peer, width), :] = dot(heads_ref[k], normed_ref[1], TN).astype(low)
+        grads_ref[rows_of(peer, width), 3 * units:] = dot(heads_ref[k], normed_ref[1], TN).astype(low)
     for copy in sends:
         copy.wait()
 
@@ -426,15 +508,13 @@
         out_shape=(
             shape((rows, model), f32),
             shape((4, rows, model), low),
-            shape((model, 2 * units), low),
-            shape((model, units), low),
-            shape((model, model), low),
+            shape((model, 3 * units + model), low),
             shape((rows, model), f32),
             shape((group_len, width), low),
             shape((8, model), f32),
         ),
         in_specs=[vmem()] * 8,
-        out_specs=(vmem(),) * 8,
+        out_specs=(vmem(),) * 6,
         scratch_shapes=[
             pltpu.VMEM((3, rows, width), low),
             pltpu.VMEM((4, rows, model), low),
@@ -453,8 +533,305 @@
     )(dealt_out, x, weights, gain, *dy)
 
 
-def matmul(spec, left, right):
-    return jnp.einsum(spec, left, right, preferred_element_type=jnp.float32)
+def front_kernel(x_ref, weight_ref, gain_cols_ref, qkv_ref, normed_ref, slab_ref, gains_ref, slots_ref, send_sem, recv_sem):
+    low = jnp.bfloat16
+    rows, model = x_ref.shape
+    shard = weight_ref.shape[0]
+    width = weight_ref.shape[1] // 12
+    count = model // shard
+    mine, peers = seq_peers()
+    place, sibling, others = shard_peers(count)
+    send = sender(send_sem, recv_sem)
+    own = span(place, shard)
+    for b in range(3):
+        slab_ref[own, b * width:(b + 1) * width] = weight_ref[:, pl.ds(
+            pl.multiple_of(b * 4 * width + mine * width, width), width)].astype(low)
+    slab_ref[own, 3 * width:] = gain_cols_ref[...].astype(low)
+    greet(peers, [sibling] + others)
+    forward, arrivals, finish = spread(send, 0, x_ref, [slots_ref.at[k] for k in range(3)], peers)
+    direct = [send(6 + k, slab_ref.at[own], slab_ref.at[own], "fsdp", peer) for k, peer in enumerate(others)]
+    twins = [send(6 + len(others), slab_ref.at[own], slab_ref.at[own], "fsdp", sibling)]
+    for copy in direct:
+        copy.start()
+    twins[0].start()
+
+    def pass_on(k):
+        direct[k].wait_recv()
+        part = span(lax.rem(place - 2 * (k + 1) + count, count), shard)
+        copy = send(7 + len(others) + k, slab_ref.at[part], slab_ref.at[part], "fsdp", sibling)
+        copy.start()
+        twins.append(copy)
+
+    pass_on(0)
+    forward()
+    for k in range(1, len(others)):
+        pass_on(k)
+    for copy in twins:
+        copy.wait_recv()
+
+    def flip(i, carry):
+        part = pl.ds(pl.multiple_of(i * 128, 128), 128)
+        gains_ref[:, part] = slab_ref[part, 3 * width:].astype(jnp.float32).T[:8]
+        return carry
+
+    lax.fori_loop(0, model // 128, flip, 0)
+
+    def project(source, owner):
+        def norm(i, carry):
+            part = pl.ds(pl.multiple_of(i * 64, 64), 64)
+            x = source[part, :].astype(jnp.float32)
+            normed_ref[pl.ds(pl.multiple_of(owner * rows + i * 64, 64), 64), :] = (
+                x * rms_scale(x) * gains_ref[0:1, :]).astype(low)
+            return carry
+
+        lax.fori_loop(0, rows // 64, norm, 0)
+        block = span(owner, rows)
+        for b in range(3):
+            part = slice(b * width, (b + 1) * width)
+            qkv_ref[block, part] = dot(normed_ref[block, :], slab_ref[:, part]).astype(low)
+
+    project(x_ref, mine)
+    for k in range(3):
+        arrivals[k]()
+        project(slots_ref.at[k], peers[k])
+    finish()
+    for copy in direct + twins:
+        copy.wait_send()
+
+
+def front(x, weight, gain_cols):
+    low = jnp.bfloat16
+    rows, model = x.shape
+    shard, columns = weight.shape
+    part = columns // 4
+    shape = jax.ShapeDtypeStruct
+    copies = 8 + 2 * (model // shard // 2)
+    return pl.pallas_call(
+        front_kernel,
+        name="front",
+        out_shape=(
+            shape((4 * rows, part), low),
+            shape((4 * rows, model), low),
+            shape((model, part + 128), low),
+            shape((8, model), jnp.float32),
+        ),
+        in_specs=[vmem()] * 3,
+        out_specs=(vmem(),) * 4,
+        scratch_shapes=[
+            pltpu.VMEM((3, rows, model), low),
+            pltpu.SemaphoreType.DMA((copies,)),
+            pltpu.SemaphoreType.DMA((copies,)),
+        ],
+        compiler_params=pltpu.CompilerParams(
+            vmem_limit_bytes=40 << 20, collective_id=0, has_side_effects=True),
+        cost_estimate=pl.CostEstimate(flops=40_000_000_000, bytes_accessed=20 << 20, transcendentals=0),
+    )(x, weight, gain_cols)
+
+
+def rear_kernel(grad_ref, normed_ref, slab_ref, gains_ref, x_ref, dh_ref, input_grad_ref, gain_grad_ref, piece_ref,
+                give_ref, transit_ref, take_ref, own_ref, term_ref, twin_ref, sum_ref, shard_take_ref, send_sem, recv_sem):
+    low = jnp.bfloat16
+    rows, model = x_ref.shape
+    shard, columns = piece_ref.shape
+    count = model // shard
+    mine, peers = seq_peers()
+    place, sibling, others = shard_peers(count)
+    send = sender(send_sem, recv_sem)
+
+    def partial(owner, store):
+        block = span(owner, rows)
+        def body(i, carry):
+            cols = pl.ds(pl.multiple_of(i * TILE, TILE), TILE)
+            store(cols, dot(grad_ref[block, :], slab_ref[cols, :columns], NT))
+            return carry
+        lax.fori_loop(0, model // TILE, body, 0)
+
+    def hand(k):
+        def store(cols, value):
+            give_ref[k, :, cols] = value.astype(low)
+        return store
+
+    def keep(cols, value):
+        own_ref[:, cols] = value
+
+    greet(peers, [sibling] + others)
+    far, x_start, y_start, merge, finish = collect(send, 0, give_ref, transit_ref, take_ref, peers)
+    partial(peers[2], hand(2))
+    far()
+    partial(peers[0], hand(0))
+    x_start()
+    partial(peers[1], hand(1))
+    y_start()
+
+    def weight_term(i, carry):
+        part = pl.ds(pl.multiple_of(i * TILE, TILE), TILE)
+        term_ref[part, :] = dot(normed_ref[:, part], grad_ref[...], TN).astype(low)
+        return carry
+
+    lax.fori_loop(0, model // TILE, weight_term, 0)
+    twins = []
+    for k in range(count // 2):
+        part = span(lax.rem(sibling + 2 * k, count), shard)
+        twins.append(send(6 + k, term_ref.at[part], twin_ref.at[k], "fsdp", sibling))
+        twins[k].start()
+    merge()
+    direct = []
+    for k in range(count // 2):
+        twins[k].wait_recv()
+        part = span(lax.rem(place + 2 * k, count), shard)
+        sum_ref[k] = (term_ref[part, :].astype(jnp.float32) + twin_ref[k].astype(jnp.float32)).astype(low)
+        if k > 0:
+            copy = send(6 + count // 2 + k, sum_ref.at[k], shard_take_ref.at[k], "fsdp", others[k - 1])
+            copy.start()
+            direct.append(copy)
+    partial(mine, keep)
+    for copy in twins:
+        copy.wait_send()
+    finish()
+    gain_grad_ref[...] = jnp.zeros_like(gain_grad_ref)
+
+    def norm_back(i, carry):
+        part = pl.ds(pl.multiple_of(i * 64, 64), 64)
+        x = x_ref[part, :].astype(jnp.float32)
+        inv = rms_scale(x)
+        grad = own_ref[part, :] + take_ref[0, part, :].astype(jnp.float32) + take_ref[1, part, :].astype(jnp.float32)
+        gain_grad_ref[0:1, :] += jnp.sum(grad * x * inv, axis=0, keepdims=True)
+        scaled = grad * gains_ref[0:1, :]
+        input_grad_ref[part, :] = (dh_ref[part, :] + (
+            inv * scaled - x * inv**3 * jnp.mean(x * scaled, axis=-1, keepdims=True))).astype(low)
+        return carry
+
+    lax.fori_loop(0, rows // 64, norm_back, 0)
+    total = sum_ref[0].astype(jnp.float32)
+    for k in range(1, count // 2):
+        direct[k - 1].wait()
+        total += shard_take_ref[k].astype(jnp.float32)
+    piece_ref[...] = total.astype(low)
+
+
+def rear(grad, normed, slab, gains, x, dh, shard):
+    low = jnp.bfloat16
+    rows, model = x.shape
+    columns = grad.shape[1]
+    count = model // shard
+    shape = jax.ShapeDtypeStruct
+    copies = 8 + count
+    return pl.pallas_call(
+        rear_kernel,
+        name="rear",
+        out_shape=(shape((rows, model), low), shape((8, model), jnp.float32), shape((shard, columns), low)),
+        in_specs=[vmem()] * 6,
+        out_specs=(vmem(),) * 3,
+        scratch_shapes=[
+            pltpu.VMEM((3, rows, model), low),
+            pltpu.VMEM((2, rows // 2, model), low),
+            pltpu.VMEM((2, rows, model), low),
+            pltpu.VMEM((rows, model), jnp.float32),
+            pltpu.VMEM((model, columns), low),
+            pltpu.VMEM((count // 2, shard, columns), low),
+            pltpu.VMEM((count // 2, shard, columns), low),
+            pltpu.VMEM((count // 2, shard, columns), low),
+            pltpu.SemaphoreType.DMA((copies,)),
+            pltpu.SemaphoreType.DMA((copies,)),
+        ],
+        compiler_params=pltpu.CompilerParams(
+            vmem_limit_bytes=48 << 20, collective_id=2, has_side_effects=True),
+        cost_estimate=pl.CostEstimate(flops=50_000_000_000, bytes_accessed=20 << 20, transcendentals=0),
+    )(grad, normed, slab, gains, x, dh)
+
+
+def last_kernel(pieces_ref, qkv_ref, gain_a_ref, gain_b_ref, out_qkv_ref, out_out_ref, out_gate_up_ref, out_down_ref,
+                gains_ref, block_ref, slots_ref, gain_own_ref, gain_take_ref, gain_slots_ref, send_sem, recv_sem):
+    low = jnp.bfloat16
+    shard, columns = qkv_ref.shape
+    model = gain_a_ref.shape[1]
+    count = model // shard
+    units = out_down_ref.shape[1] // 4
+    width = columns // 3
+    mine, peers = seq_peers()
+    place, sibling, _ = shard_peers(count)
+    everyone = [lax.rem(place + k, count) for k in range(1, count)]
+    send = sender(send_sem, recv_sem)
+    block_ref[:, :columns] = qkv_ref[...]
+    block_ref[:, columns:] = pieces_ref[...]
+    gain_own_ref[0:1, :] = gain_a_ref[0:1, :]
+    gain_own_ref[1:2, :] = gain_b_ref[0:1, :]
+    gain_own_ref[2:8, :] = jnp.zeros((6, model), jnp.float32)
+    greet(peers, everyone)
+    forward, arrivals, finish = spread(send, 0, block_ref, [slots_ref.at[k] for k in range(3)], peers)
+    gain_sends = [send(6 + k, gain_own_ref, gain_take_ref.at[k], "fsdp", peer) for k, peer in enumerate(everyone)]
+    for copy in gain_sends:
+        copy.start()
+
+    def place_block(source, owner, first):
+        at = columns
+        for b in range(3):
+            out_qkv_ref[:, span(b * 4 + owner, width)] = source[:, b * width:(b + 1) * width]
+        for b in range(2):
+            out_gate_up_ref[:, span(b * 4 + owner, units)] = source[:, at:at + units]
+            at += units
+        out_down_ref[:, span(owner, units)] = source[:, at:at + units]
+        at += units
+        if first:
+            out_out_ref[...] = source[:, at:].astype(jnp.float32)
+        else:
+            out_out_ref[...] += source[:, at:].astype(jnp.float32)
+
+    place_block(block_ref, mine, True)
+    forward()
+    total = gain_own_ref[...]
+    for k, copy in enumerate(gain_sends):
+        copy.wait_recv()
+        total += gain_take_ref[k]
+    gains_ref[...] = total
+    seq_sends = [send(6 + len(everyone) + k, gains_ref, gain_slots_ref.at[k], "seq", peer) for k, peer in enumerate(peers)]
+    for copy in seq_sends:
+        copy.start()
+    for k in range(3):
+        arrivals[k]()
+        place_block(slots_ref.at[k], peers[k], False)
+    for copy in seq_sends:
+        copy.wait()
+    gains_ref[...] += gain_slots_ref[0] + gain_slots_ref[1] + gain_slots_ref[2]
+    for copy in gain_sends:
+        copy.wait_send()
+    finish()
+
+
+def last(pieces, qkv_piece, gain_a, gain_b, units):
+    low = jnp.bfloat16
+    shard, columns = qkv_piece.shape
+    model = gain_a.shape[1]
+    count = model // shard
+    f32 = jnp.float32
+    shape = jax.ShapeDtypeStruct
+    wide = columns + pieces.shape[1]
+    copies = 9 + count
+    return pl.pallas_call(
+        last_kernel,
+        name="last",
+        out_shape=(
+            shape((shard, 4 * columns), low),
+            shape((shard, model), f32),
+            shape((shard, 8 * units), low),
+            shape((shard, 4 * units), low),
+            shape((8, model), f32),
+        ),
+        in_specs=[vmem()] * 4,
+        out_specs=(vmem(),) * 5,
+        scratch_shapes=[
+            pltpu.VMEM((shard, wide), low),
+            pltpu.VMEM((3, shard, wide), low),
+            pltpu.VMEM((8, model), f32),
+            pltpu.VMEM((count - 1, 8, model), f32),
+            pltpu.VMEM((3, 8, model), f32),
+            pltpu.SemaphoreType.DMA((copies,)),
+            pltpu.SemaphoreType.DMA((copies,)),
+        ],
+        compiler_params=pltpu.CompilerParams(
+            vmem_limit_bytes=40 << 20, collective_id=3, has_side_effects=True),
+        cost_estimate=pl.CostEstimate(flops=40_000_000_000, bytes_accessed=20 << 20, transcendentals=0),
+    )(pieces, qkv_piece, gain_a, gain_b)
 
 
 def swaps(rows):
@@ -465,12 +842,12 @@
 def on_device(block_input, norm_gain_a, weight_qkv, weight_out, norm_gain_b, weight_gate_up, weight_down,
               cotangent, permutation, lengths, offsets):
     low = jnp.bfloat16
+    f32 = jnp.float32
     seq_count = lax.axis_size("seq")
     mine = lax.axis_index("seq")
     row_count, model_width = block_input.shape[1:]
     group_len = row_count * seq_count
     shard = weight_qkv.shape[0]
-    head_width = weight_qkv.shape[1] // 3 // seq_count
     part_units = weight_down.shape[1] // seq_count
     perm = permutation[0]
     offs = offsets[0]
@@ -481,58 +858,35 @@
         cut = weight.reshape(shard, blocks, seq_count, width)
         return lax.dynamic_index_in_dim(cut, mine, 2, keepdims=False).reshape(shard, blocks * width).astype(low)
 
-    gather_weight = lambda piece: lax.all_gather(piece, "fsdp", axis=0, tiled=True)
-    gather_rows = lambda rows: lax.all_gather(rows, "seq", axis=0, tiled=True)
-    scatter_rows = lambda part: lax.psum_scatter(part.astype(low), "seq", scatter_dimension=0, tiled=True)
-
-    gains = gather_weight(jnp.stack([norm_gain_a, norm_gain_b], axis=1)).astype(low).astype(jnp.float32)
-    gain_a, gain_b = gains[:, 0], gains[:, 1]
-    rows_all = gather_rows(block_input[0])
-    part_qkv = gather_weight(columns(weight_qkv, 3, head_width))
-    weights = gather_weight(jnp.concatenate(
-        [weight_out.astype(low), columns(weight_gate_up, 2, part_units), columns(weight_down, 1, part_units)], axis=1))
-    grad_rows = [cotangent[0]] + swaps([cotangent[0]] * 3)
-
-    wide_all = rows_all.astype(jnp.float32)
-    normed_a = (wide_all * rms_scale(wide_all) * gain_a).astype(low)
-    qkv = matmul("rd,de->re", normed_a, part_qkv).astype(low)
+    weights = lax.all_gather(jnp.concatenate(
+        [weight_out.astype(low), columns(weight_gate_up, 2, part_units), columns(weight_down, 1, part_units)], axis=1),
+        "fsdp", axis=0, tiled=True)
+    gain_cols = jnp.pad(jnp.stack([norm_gain_a, norm_gain_b], axis=1), ((0, 0), (0, 126)))
+    qkv, normed_a, slab, gains = front(block_input[0], weight_qkv, gain_cols)
+    grad_own, qkv = lax.optimization_barrier((cotangent[0], qkv))
+    grad_rows = [cotangent[0]] + swaps([grad_own] * 3)
     ordered, dealt_out, wide_out, log_total = attention_forward(offs, qkv, perm, start)
-    hidden, branch, gate_up_term, down_term, out_term, grad_hidden, grad_heads, gain_b_term = middle(
-        dealt_out, block_input[0], weights, gain_b.reshape(1, model_width), grad_rows, part_units)
-    branch_sum = branch[0].astype(jnp.float32)
+    hidden, branch, grads, grad_hidden, grad_heads, gain_b_term = middle(
+        dealt_out, block_input[0], weights, gains[1:2], grad_rows, part_units)
+    pieces = lax.psum_scatter(grads, "fsdp", scatter_dimension=0, tiled=True)
+    branch_sum = branch[0].astype(f32)
     for piece in swaps([branch[k] for k in (1, 2, 3)]):
-        branch_sum = branch_sum + piece.astype(jnp.float32)
+        branch_sum = branch_sum + piece.astype(f32)
     result_rows = (hidden + branch_sum).astype(low)
     dealt_grad = attention_backward(offs, grad_heads, ordered, perm, start, wide_out, log_total)
-    out_part = lax.psum_scatter(out_term, "seq", scatter_dimension=1, tiled=True)
-    qkv_term = matmul("rd,re->de", normed_a, dealt_grad)
-    grad_normed_a = scatter_rows(matmul("re,de->rd", dealt_grad, part_qkv)).astype(jnp.float32)
-    inputs = block_input[0].astype(jnp.float32)
-    input_back, gain_a_term = norm_backward(inputs, rms_scale(inputs), grad_normed_a, gain_a)
-    input_grad = (grad_hidden + input_back).astype(low)
-
-    def finish(term):
-        piece = lax.psum_scatter(term.astype(low), "fsdp", scatter_dimension=0, tiled=True)
-        return lax.all_gather(piece, "seq", axis=0, tiled=False)
-
-    def spread(pieces, blocks):
-        width = pieces.shape[-1] // blocks
-        return pieces.reshape(seq_count, shard, blocks, width).transpose(1, 2, 0, 3).reshape(
-            shard, -1).astype(jnp.float32)
-
-    grad_mlp = finish(jnp.concatenate([gate_up_term, down_term], axis=1))
-    grad_attn = finish(jnp.concatenate([qkv_term.astype(low), out_part], axis=1))
-    gain_terms = lax.psum(jnp.stack([gain_a_term, gain_b_term[0]]), ("seq", "fsdp"))
+    input_grad, gain_a_term, qkv_piece = rear(dealt_grad, normed_a, slab, gains, block_input[0], grad_hidden, shard)
+    grad_qkv, grad_out, grad_gate_up, grad_down, gain_terms = last(
+        pieces, qkv_piece, gain_a_term, gain_b_term, part_units)
     gain_terms = lax.dynamic_slice_in_dim(gain_terms, lax.axis_index("fsdp") * shard, shard, axis=1)
     return (
         result_rows[None],
         input_grad[None],
         gain_terms[0],
-        spread(grad_attn[:, :, : 3 * head_width], 3),
-        spread(grad_attn[:, :, 3 * head_width:], 1),
+        grad_qkv.astype(f32),
+        grad_out,
         gain_terms[1],
-        spread(grad_mlp[:, :, : 2 * part_units], 2),
-        spread(grad_mlp[:, :, 2 * part_units:], 1),
+        grad_gate_up.astype(f32),
+        grad_down.astype(f32),
     )
 
 

time: 719 us -> 429 us (0.60)
  waiting for transfers between devices: 318 us -> 7.41 us
  Pallas kernels: 209 us -> 364 us
  blocking collectives: 51.8 us -> 0 us
  local copies, waits for them, and re-layouts: 60.1 us -> 23.4 us
  matrix products: 21.7 us -> 0 us
  other arithmetic: 26.8 us -> 10.7 us
    pallas_call x0 -> x3, Pallas kernels: none -> 153 us  [the longest x1 60.2 us: rear(): pl.pallas_call(rear_kernel, name='rear', out_shape=(shape((rows, model),...]
    all_gather x5 -> x1, waiting for transfers between devices: 147 us -> 0.01 us  [on_device(): lax.all_gather(jnp.concatenate([weight_out.astype(low), columns(weight_ga...]
    reduce_scatter x3 -> x1, waiting for transfers between devices: 85.9 us -> 5.05 us  [on_device(): pieces = lax.psum_scatter(grads, 'fsdp', scatter_dimension=0, tiled=True)]
    ppermute x6, waiting for transfers between devices: 64.4 us -> 2.33 us  [swaps(): lax.ppermute(piece, 'seq', table)]
    psum x1 -> x0, blocking collectives: 39.4 us -> none  [on_device(): lax.psum(jnp.stack([gain_a_term, gain_b_term[0]]), ('seq', 'fsdp'))]
    convert_element_type x8 -> x0, local copies, waits for them, and re-layouts: 24.4 us -> none  [the longest x7 23.7 us: spread(): return pieces.reshape(seq_count, shard, blocks, width).transpose(1, 2, 0,...]
    dot_general x3 -> x0, matrix products: 21.7 us -> none  [matmul(): return jnp.einsum(spec, left, right, preferred_element_type=jnp.float32)]
    unnamed x10 -> x2, waiting for transfers between devices: 20.7 us -> 0.03 us
  transfers between devices with their start and end apart: 15 -> 8, of which waited for: 10 -> 2; matrix products, arithmetic and copies ran while one was open for 9% -> 2% of each run, Pallas kernels for 11% -> 43%
where the time goes in v3:
time: 429 us; the launch traced here: 428 us
  Pallas kernels  364 us (85%)
  local copies, waits for them, and re-layouts  23.4 us (5%)
  between operations  14.3 us (3%)
  other arithmetic  10.7 us (2%)
  waiting for transfers between devices  7.41 us (2%)
  starting transfers between devices  7.3 us (2%)
    pallas_call x1, Pallas kernels, middle(): pl.pallas_call(middle_kernel, name='middle', out_shape=(shape((rows, mode...  132 us
    pallas_call x1, Pallas kernels, rear(): pl.pallas_call(rear_kernel, name='rear', out_shape=(shape((rows, model),...  60.2 us
    pallas_call x1, Pallas kernels, last(): pl.pallas_call(last_kernel, name='last', out_shape=(shape((shard, 4 * col...  49.3 us
    pallas_call x1, Pallas kernels, front(): pl.pallas_call(front_kernel, name='front', out_shape=(shape((4 * rows, pa...  43.3 us
    pallas_call x1, Pallas kernels, attention_forward(): pl.pallas_call(forward_kernel, name='attention_forward', out_shape=(jax.S...  40.3 us
    pallas_call x1, Pallas kernels, attention_backward(): pl.pallas_call(backward_kernel, name='attention_backward', out_shape=jax....  39.7 us
    unnamed x46, local copies, waits for them, and re-layouts  15 us
  transfers between devices with their start and end apart: 8, of which 2 were waited for; matrix products, arithmetic and copies ran while one was open for 2% of the time, Pallas kernels for 43%

profile of v3, /device:TPU:0, one launch (start us, length us, event | category | flops | bytes accessed | tf_op | source)
XLA Modules:
  0.0 427.5 jit_solution(6841154313461076752)
XLA Ops:
  7.2 0.0 all-gather.2.cloned.1.call-start
  7.2 1.1 convert_element_type.44
  8.3 1.8 copy.37
  10.2 0.9 copy.41
  11.0 3.3 reshape.35
  14.3 1.1 constant_dynamic-slice_fusion.2
  15.4 0.5 copy.44
  16.0 0.0 copy-start.17
  16.0 0.0 copy-start.2
  16.0 0.1 copy.42
  16.2 1.1 pad_maximum_fusion
  17.2 0.0 all-gather.2.cloned.1.call-update
  17.2 0.2 reduce-scatter.2.cloned.1.call-start
  17.5 0.1 copy.34
  17.6 0.2 copy-done.2
  17.8 1.2 copy-done.3
  19.0 43.3 %front.1 = (bf16[2048,768]{1,0:T(8,128)(2,1)S(1)}, bf16[2048,1024]{1,0:T(8,128)(2,1)S(1)}, bf16[1024,896]{1,0:T(8,128)(2,1)S(1)}, f32[8,1024]{1,0:T(8,128)S(1)}) custom-call(bf16[512,1024]{1,0:T(8,128)(2,1)S(1)} %bitcast.39, f32[128,3072]{1,0:T(8,128)S(1)} %copy-done.2, f32[128,128]{1,0:T(8,128)S(1)} %pad.4.gain_cols_ref), custom_call_target="tpu_custom_call" | custom-call | flops 40000000000 | bytes 20971520 | tf_op jit(solution)/shard_map/front/pallas_call | solution.py:609
  62.3 1.6 copy-done.6
  63.9 2.0 copy-done.10
  66.0 1.3 copy-done.11
  67.3 1.5 collective-permute-start.2
  68.7 1.5 collective-permute-start.1
  70.2 0.5 collective-permute-start
  70.8 0.4 copy.35.perm_col_ref
  71.1 0.6 slice.21.gain_ref
  71.8 0.1 select_reduce_fusion
  71.9 40.3 %attention_forward.1 = (bf16[2048,768]{1,0:T(8,128)(2,1)}, bf16[2048,256]{1,0:T(8,128)(2,1)S(1)}, f32[256,2048]{1,0:T(8,128)S(1)}, f32[8,2048]{1,0:T(8,128)S(1)}) custom-call(s32[3]{0:T(128)S(1)} %bitcast.36, bf16[2048,768]{1,0:T(8,128)(2,1)} %copy-done.6, s32[1,2048]{1,0:T(1,128)S(1)} %copy-done, s32[2048,1]{1,0:T(8,128)S(1)} %copy.35.perm_col_ref, ...), custom_call_target="tpu_custom_call" | custom-call | flops 20000000000 | bytes 16777216 | tf_op jit(solution)/shard_map/attention_forward/pallas_call | solution.py:181
  112.2 1.3 copy-done.7
  113.5 1.0 copy-done.9
  114.5 2.3 collective-permute-done.1.dy2_ref
  116.8 131.6 %middle.1 = (f32[512,1024]{1,0:T(8,128)}, bf16[4,512,1024]{2,1,0:T(8,128)(2,1)}, bf16[1024,4096]{1,0:T(8,128)(2,1)}, f32[512,1024]{1,0:T(8,128)}, bf16[2048,256]{1,0:T(8,128)(2,1)}, /*index=5*/f32[8,1024]{1,0:T(8,128)}) custom-call(bf16[2048,256]{1,0:T(8,128)(2,1)} %copy-done.9, bf16[512,1024]{1,0:T(8,128)(2,1)} %bitcast.38, ...), custom_call_target="tpu_custom_call" | custom-call | flops 60000002048 | bytes 41943040 | tf_op jit(solution)/shard_map/middle/pallas_call | solution.py:505
  248.4 0.0 reduce-scatter.2.cloned.1.call-update
  248.4 2.3 slice_bitcast_fusion.2
  250.7 1.1 collective-permute-start.3
  251.9 1.5 collective-permute-start.5
  253.3 1.0 collective-permute-start.4
  254.3 39.7 %attention_backward.1.grad_ref = bf16[2048,768]{1,0:T(8,128)(2,1)} custom-call(s32[3]{0:T(128)S(1)} %bitcast.37, bf16[2048,256]{1,0:T(8,128)(2,1)S(1)} %copy-done.13, bf16[2048,768]{1,0:T(8,128)(2,1)} %get-tuple-element.40.sorted_ref, s32[1,2048]{1,0:T(1,128)S(1)} %copy-done, s32[2048,1]{1,0:T(8,128)S(1)} %copy.35.perm_col_ref, s32[1,2048]{1,0:T(1,128)S(1)} %bitcast.34, ...), custom_call_target="tpu_custom_call" | custom-call | flops 40000000000 | bytes 16777216 | tf_op jit(solution)/shard_map/attention_backward/pallas_call | solution.py:201
  294.0 60.2 %rear.1 = (bf16[512,1024]{1,0:T(8,128)(2,1)S(1)}, f32[8,1024]{1,0:T(8,128)S(1)}, bf16[128,768]{1,0:T(8,128)(2,1)S(1)}) custom-call(bf16[2048,768]{1,0:T(8,128)(2,1)} %attention_backward.1.grad_ref, bf16[2048,1024]{1,0:T(8,128)(2,1)} %copy-done.10, bf16[1024,896]{1,0:T(8,128)(2,1)S(1)} %copy-done.12, f32[8,1024]{1,0:T(8,128)S(1)} %get-tuple-element.35.gains_ref, ...), custom_call_target="tpu_custom_call" | custom-call | flops 49999998976 | bytes 20971520 | tf_op jit(solution)/shard_map/rear/pallas_call | solution.py:719
  354.3 3.2 fusion.4
  357.5 5.0 %reduce-scatter.2.cloned.1.call-done.pieces_ref = bf16[128,4096]{1,0:T(8,128)(2,1)} async-done(((bf16[1024,4096]{1,0:T(8,128)(2,1)}), bf16[128,4096]{1,0:T(8,128)(2,1)}) %reduce-scatter.2.cloned.1.call-update) | async-done | bytes 1048592 | tf_op jit(solution)/shard_map/reduce_scatter | solution.py:871
  362.6 1.2 copy-done.5
  363.8 49.3 %last.1 = (bf16[128,3072]{1,0:T(8,128)(2,1)S(1)}, f32[128,1024]{1,0:T(8,128)S(1)}, bf16[128,8192]{1,0:T(8,128)(2,1)S(1)}, bf16[128,4096]{1,0:T(8,128)(2,1)S(1)}, f32[8,1024]{1,0:T(8,128)S(1)}) custom-call(bf16[128,4096]{1,0:T(8,128)(2,1)S(1)} %copy-done.5, bf16[128,768]{1,0:T(8,128)(2,1)S(1)} %get-tuple-element.48.qkv_ref, ...), custom_call_target="tpu_custom_call" | custom-call | flops 40000000000 | bytes 20971520 | tf_op jit(solution)/shard_map/last/pallas_call | solution.py:810
  413.1 0.5 slice_bitcast_fusion.3
  413.6 1.3 convert_element_type.55
  414.9 1.5 convert_element_type.57
  416.5 2.4 convert_element_type.56
  418.9 1.0 copy.47
  419.9 0.8 copy.48
  (40 shorter events, 0.1 us)
Async XLA Ops:
  7.2 109.6 %all-gather.2.cloned.1.call-start = ((), (), s32[]{:S(2)}) async-start(), calls=%async_computation.1 | async-start | bytes 9437184 | tf_op jit(solution)/shard_map/all_gather | solution.py:861
  14.3 1.8 copy-start.16
  16.0 1.5 copy-start.17
  16.0 1.5 copy-start.18
  16.0 1.8 copy-start.2
  17.2 345.3 %reduce-scatter.2.cloned.1.call-start = ((), (), s32[]{:S(2)}) async-start(), calls=%async_computation.2 | async-start | bytes 9437184 | tf_op jit(solution)/shard_map/reduce_scatter | solution.py:871
  17.8 1.2 copy-start.3
  19.0 48.2 %copy-start.19 = (bf16[1,512,1024]{2,1,0:T(8,128)(2,1)S(1)}, bf16[1,512,1024]{2,1,0:T(8,128)(2,1)}, u32[]{:S(2)}) copy-start(bf16[1,512,1024]{2,1,0:T(8,128)(2,1)} %param.18) | copy-start | bytes 3145732
  19.0 51.7 %copy-start = (s32[1,2048]{1,0:T(1,128)S(1)}, s32[1,2048]{1,0:T(1,128)}, u32[]{:S(2)}) copy-start(s32[1,2048]{1,0:T(1,128)} %perm_row_ref.3) | copy-start | bytes 24580
  19.0 52.7 %copy-start.1 = (s32[1,3]{1,0:T(1,128)S(1)}, s32[1,3]{1,0:T(1,128)}, u32[]{:S(2)}) copy-start(s32[1,3]{1,0:T(1,128)} %param.20) | copy-start | bytes 40
  62.3 1.6 copy-start.6
  63.9 2.0 copy-start.10
  66.0 1.3 copy-start.11
  67.3 47.2 %collective-permute-start.2 = (bf16[512,1024]{1,0:T(8,128)(2,1)S(1)}, bf16[512,1024]{1,0:T(8,128)(2,1)}, u32[]{:S(2)}, u32[]{:S(2)}) collective-permute-start(bf16[512,1024]{1,0:T(8,128)(2,1)S(1)} %bitcast.48), channel_id=1, source_target_pairs={{0,24},{8,16},{16,8},{24,0},{1,25},{9,17},{17,9},{25,1},{2,26},{10... | collective-permute-start | bytes 3145736 | tf_op jit(solution)/shard_map/ppermute | solution.py:838
  68.7 48.0 %collective-permute-start.1 = (bf16[512,1024]{1,0:T(8,128)(2,1)S(1)}, bf16[512,1024]{1,0:T(8,128)(2,1)}, u32[]{:S(2)}, u32[]{:S(2)}) collective-permute-start(bf16[512,1024]{1,0:T(8,128)(2,1)S(1)} %bitcast.49), channel_id=1, source_target_pairs={{0,16},{8,24},{16,0},{24,8},{1,17},{9,25},{17,1},{25,9},{2,18},{10... | collective-permute-start | bytes 3145736 | tf_op jit(solution)/shard_map/ppermute | solution.py:838
  70.2 46.6 %collective-permute-start = (bf16[512,1024]{1,0:T(8,128)(2,1)S(1)}, bf16[512,1024]{1,0:T(8,128)(2,1)}, u32[]{:S(2)}, u32[]{:S(2)}) collective-permute-start(bf16[512,1024]{1,0:T(8,128)(2,1)S(1)} %bitcast.50), channel_id=1, source_target_pairs={{0,8},{8,0},{16,24},{24,16},{1,9},{9,1},{17,25},{25,17},{2,10},{10... | collective-permute-start | bytes 3145736 | tf_op jit(solution)/shard_map/ppermute | solution.py:838
  112.2 1.3 copy-start.7
  113.5 1.0 copy-start.9
  248.4 5.9 %copy-start.8 = (f32[256,2048]{1,0:T(8,128)S(1)}, f32[256,2048]{1,0:T(8,128)}, u32[]{:S(2)}) copy-start(f32[256,2048]{1,0:T(8,128)} %copy-done.7) | copy-start | bytes 6291460
  248.4 5.9 %copy-start.13 = (bf16[2048,256]{1,0:T(8,128)(2,1)S(1)}, bf16[2048,256]{1,0:T(8,128)(2,1)}, u32[]{:S(2)}) copy-start(bf16[2048,256]{1,0:T(8,128)(2,1)} %get-tuple-element.39.grad_ref) | copy-start | bytes 3145732
  250.7 103.5 %collective-permute-start.3 = (bf16[512,1024]{1,0:T(8,128)(2,1)S(1)}, bf16[512,1024]{1,0:T(8,128)(2,1)S(1)}, u32[]{:S(2)}, u32[]{:S(2)}) collective-permute-start(bf16[512,1024]{1,0:T(8,128)(2,1)S(1)} %get-tuple-element.56), channel_id=1, source_target_pairs={{0,8},{8,0},{16,24},{24,16},{1,9},{9,1},{17,25},{25,17},{2,10},{10... | collective-permute-start | bytes 3145736 | tf_op jit(solution)/shard_map/ppermute | solution.py:838
  251.9 102.4 %collective-permute-start.5 = (bf16[512,1024]{1,0:T(8,128)(2,1)S(1)}, bf16[512,1024]{1,0:T(8,128)(2,1)S(1)}, u32[]{:S(2)}, u32[]{:S(2)}) collective-permute-start(bf16[512,1024]{1,0:T(8,128)(2,1)S(1)} %get-tuple-element.57), channel_id=1, source_target_pairs={{0,24},{8,16},{16,8},{24,0},{1,25},{9,17},{17,9},{25,1},{2,26},{10... | collective-permute-start | bytes 3145736 | tf_op jit(solution)/shard_map/ppermute | solution.py:838
  253.3 101.0 %collective-permute-start.4 = (bf16[512,1024]{1,0:T(8,128)(2,1)S(1)}, bf16[512,1024]{1,0:T(8,128)(2,1)S(1)}, u32[]{:S(2)}, u32[]{:S(2)}) collective-permute-start(bf16[512,1024]{1,0:T(8,128)(2,1)S(1)} %get-tuple-element.58), channel_id=1, source_target_pairs={{0,16},{8,24},{16,0},{24,8},{1,17},{9,25},{17,1},{25,9},{2,18},{10... | collective-permute-start | bytes 3145736 | tf_op jit(solution)/shard_map/ppermute | solution.py:838
  254.3 39.7 %copy-start.4 = (bf16[1,512,1024]{2,1,0:T(8,128)(2,1)S(1)}, bf16[1,512,1024]{2,1,0:T(8,128)(2,1)}, u32[]{:S(2)}) copy-start(bf16[1,512,1024]{2,1,0:T(8,128)(2,1)} %param.11) | copy-start | bytes 3145732
  254.3 39.7 %copy-start.12 = (bf16[1024,896]{1,0:T(8,128)(2,1)S(1)}, bf16[1024,896]{1,0:T(8,128)(2,1)}, u32[]{:S(2)}) copy-start(bf16[1024,896]{1,0:T(8,128)(2,1)} %copy-done.11) | copy-start | bytes 5505028
  294.0 60.3 %copy-start.15 = (f32[512,1024]{1,0:T(8,128)S(1)}, f32[512,1024]{1,0:T(8,128)}, u32[]{:S(2)}) copy-start(f32[512,1024]{1,0:T(8,128)} %get-tuple-element.37) | copy-start | bytes 6291460
  354.3 8.2 %copy-start.14 = (f32[8,1024]{1,0:T(8,128)S(1)}, f32[8,1024]{1,0:T(8,128)}, u32[]{:S(2)}) copy-start(f32[8,1024]{1,0:T(8,128)} %get-tuple-element.50.gain_b_ref) | copy-start | bytes 98308
  362.6 1.2 copy-start.5
Sparse Core Ops, SparseCore 0:
  17.4 97.5 all-gather.1
  248.5 114.0 reduce-scatter.1

commit v4 on v3

--- a/solution.py
+++ b/solution.py
@@ -57,12 +57,30 @@
     return (key_pos <= query_pos) & (key_pos >= start_ref[:, cols])
 
 
-def forward_kernel(offs_ref, qkv_ref, perm_row_ref, perm_col_ref, start_ref,
-                   sorted_ref, dealt_ref, wide_ref, lse_ref, vt_ref, low_ref):
-    group_len = qkv_ref.shape[0]
+def forward_kernel(offs_ref, x_ref, slab_ref, perm_row_ref, perm_col_ref, start_ref,
+                   sorted_ref, dealt_ref, wide_ref, lse_ref, normed_ref, gains_ref, qkv_ref, vt_ref, low_ref):
+    group_len, model = x_ref.shape
     width = qkv_ref.shape[1] // 3
     heads = width // HEAD_DIM
     scale = HEAD_DIM ** -0.5 * LOG2E
+
+    def gain(i, carry):
+        part = pl.ds(pl.multiple_of(i * 128, 128), 128)
+        gains_ref[:, part] = slab_ref[part, 3 * width:].astype(jnp.float32).T[:8]
+        return carry
+
+    lax.fori_loop(0, model // 128, gain, 0)
+
+    def project(i, carry):
+        rows = pl.ds(pl.multiple_of(i * BLK, BLK), BLK)
+        for r in range(0, BLK, 64):
+            part = pl.ds(pl.multiple_of(i * BLK + r, 64), 64)
+            x = x_ref[part, :].astype(jnp.float32)
+            normed_ref[part, :] = (x * rms_scale(x) * gains_ref[0:1, :]).astype(jnp.bfloat16)
+        qkv_ref[rows, :] = dot(normed_ref[rows, :], slab_ref[:, :3 * width]).astype(jnp.bfloat16)
+        return carry
+
+    lax.fori_loop(0, group_len // BLK, project, 0)
     sort_rows(perm_row_ref, qkv_ref, sorted_ref)
 
     def flip(i, carry):
@@ -171,28 +189,40 @@
     deal_rows(perm_col_ref, low_ref, dealt_ref)
 
 
+def hbm():
+    return pl.BlockSpec(memory_space=pl.ANY)
+
+
 def vmem():
     return pl.BlockSpec(memory_space=pltpu.VMEM)
 
 
-def attention_forward(offs, qkv, perm, start):
-    group_len, columns = qkv.shape
+def attention_forward(offs, rows, slab, perm, start):
+    group_len, model = rows.shape
+    columns = slab.shape[1] - 128
     width = columns // 3
+    shape = jax.ShapeDtypeStruct
     return pl.pallas_call(
         forward_kernel,
         name="attention_forward",
         out_shape=(
-            jax.ShapeDtypeStruct((group_len, columns), jnp.bfloat16),
-            jax.ShapeDtypeStruct((group_len, width), jnp.bfloat16),
-            jax.ShapeDtypeStruct((width, group_len), jnp.float32),
-            jax.ShapeDtypeStruct((8, group_len), jnp.float32),
+            shape((group_len, columns), jnp.bfloat16),
+            shape((group_len, width), jnp.bfloat16),
+            shape((width, group_len), jnp.float32),
+            shape((8, group_len), jnp.float32),
+            shape((group_len, model), jnp.bfloat16),
+            shape((8, model), jnp.float32),
         ),
-        in_specs=[pl.BlockSpec(memory_space=pltpu.SMEM)] + [vmem()] * 4,
-        out_specs=(vmem(),) * 4,
-        scratch_shapes=[pltpu.VMEM((width, group_len), jnp.bfloat16), pltpu.VMEM((group_len, width), jnp.bfloat16)],
+        in_specs=[pl.BlockSpec(memory_space=pltpu.SMEM)] + [vmem()] * 5,
+        out_specs=(vmem(),) * 6,
+        scratch_shapes=[
+            pltpu.VMEM((group_len, columns), jnp.bfloat16),
+            pltpu.VMEM((width, group_len), jnp.bfloat16),
+            pltpu.VMEM((group_len, width), jnp.bfloat16),
+        ],
         compiler_params=pltpu.CompilerParams(vmem_limit_bytes=48 << 20),
-        cost_estimate=pl.CostEstimate(flops=20_000_000_000, bytes_accessed=16 << 20, transcendentals=0),
-    )(offs, qkv, perm.reshape(1, group_len), perm.reshape(group_len, 1), start.reshape(1, group_len))
+        cost_estimate=pl.CostEstimate(flops=24_000_000_000, bytes_accessed=16 << 20, transcendentals=0),
+    )(offs, rows, slab, perm.reshape(1, group_len), perm.reshape(group_len, 1), start.reshape(1, group_len))
 
 
 def attention_backward(offs, grad, ordered, perm, start, wide, lse):
@@ -288,68 +318,69 @@
     return forward, (x_bottom.wait_recv, y_top.wait_recv, lambda: (x_relay.wait_recv(), y_relay.wait_recv())), finish
 
 
-def collect(send, base, give, transit, take, peers):
+def collect(send, base, give, transit, take, peers, cut):
     px, py, _ = peers
     half = give.shape[1] // 2
-    top, bottom = pl.ds(0, half), pl.ds(half, half)
-    far_top = send(base, give.at[2, top], transit.at[0], "seq", px)
-    far_bottom = send(base + 1, give.at[2, bottom], transit.at[1], "seq", py)
-    x_top = send(base + 2, give.at[0, top], take.at[0, top], "seq", px)
-    y_bottom = send(base + 3, give.at[1, bottom], take.at[1, bottom], "seq", py)
-    y_top = send(base + 4, give.at[1, top], take.at[1, top], "seq", py)
-    x_bottom = send(base + 5, give.at[0, bottom], take.at[0, bottom], "seq", px)
-
-    def add(k, part, t):
+    size = half // cut
+    halves = (pl.ds(0, half), pl.ds(half, half))
+    pieces = [[pl.ds(h * half + c * size, size) for c in range(cut)] for h in range(2)]
+    first, second = (px, py), (py, px)
+    far = [[send(base + h * cut + c, give.at[2, pieces[h][c]], transit.at[h, pl.ds(c * size, size)], "seq", first[h])
+            for c in range(cut)] for h in range(2)]
+    plain = [send(base + 2 * cut + h, give.at[h, halves[h]], take.at[h, halves[h]], "seq", first[h]) for h in range(2)]
+    summed = [[send(base + 2 * cut + 2 + h * cut + c, give.at[1 - h, pieces[h][c]], take.at[1 - h, pieces[h][c]],
+                    "seq", second[h]) for c in range(cut)] for h in range(2)]
+
+    def start_far(h):
+        for copy in far[h]:
+            copy.start()
+
+    def merge(h, c):
+        far[h][c].wait_recv()
+
         def step(i, carry):
-            rows = pl.ds(pl.multiple_of(part.start + i * 64, 64), 64)
-            more = pl.ds(pl.multiple_of(i * 64, 64), 64)
-            give[k, rows, :] = (give[k, rows, :].astype(jnp.float32)
-                                + transit[t, more, :].astype(jnp.float32)).astype(jnp.bfloat16)
+            rows = pl.ds(pl.multiple_of(h * half + c * size + i * 64, 64), 64)
+            more = pl.ds(pl.multiple_of(c * size + i * 64, 64), 64)
+            give[1 - h, rows, :] = (give[1 - h, rows, :].astype(jnp.float32)
+                                    + transit[h, more, :].astype(jnp.float32)).astype(jnp.bfloat16)
             return carry
-        lax.fori_loop(0, half // 64, step, 0)
-
-    def far():
-        far_top.start()
-        far_bottom.start()
-
-    def merge():
-        far_top.wait_recv()
-        add(1, top, 0)
-        y_top.start()
-        far_bottom.wait_recv()
-        add(0, bottom, 1)
-        x_bottom.start()
-
-    def finish():
-        for copy in (x_top, y_bottom, y_top, x_bottom):
-            copy.wait()
-        far_top.wait_send()
-        far_bottom.wait_send()
-
-    return far, x_top.start, y_bottom.start, merge, finish
-
-
-def middle_kernel(out_ref, x_ref, weight_ref, gain_ref, dy0_ref, dy1_ref, dy2_ref, dy3_ref,
-                  hidden_ref, branch_ref, grads_ref, dh_ref, do_ref, gain_grad_ref,
-                  heads_ref, normed_ref, act_ref, dgu_ref, give_ref, take_ref, own_ref, do_give_ref,
-                  send_sem, recv_sem):
+
+        lax.fori_loop(0, size // 64, step, 0)
+        summed[h][c].start()
+
+    def finish(h):
+        plain[h].wait()
+        for c in range(cut):
+            summed[h][c].wait()
+            far[h][c].wait_send()
+
+    return start_far, (plain[0].start, plain[1].start), merge, finish
+
+
+def middle_kernel(out_ref, x_ref, weight_in, gain_ref, dy0_in, dy1_in, dy2_in, dy3_in,
+                  hidden_out, branch_out, grads_out, dh_out, do_ref, gain_grad_ref,
+                  weight_ref, dy_ref, hidden_ref, branch_ref, grads_ref, dh_ref, mixed_ref, normed_ref, act_ref, dgu_ref, give_ref, transit_ref, take_ref, own_ref, low_ref, do_give_ref,
+                  local_sem, send_sem, recv_sem):
     low = jnp.bfloat16
     rows, model = x_ref.shape
     width = out_ref.shape[1]
     units = act_ref.shape[2]
     gate_at, up_at, down_at = model, model + units, model + 2 * units
-    dy_refs = (dy0_ref, dy1_ref, dy2_ref, dy3_ref)
     mine, peers = seq_peers()
+    px, py, _ = peers
+
+    def local(index, src, dst):
+        copy = pltpu.make_async_copy(src, dst, local_sem.at[index])
+        copy.start()
+        return copy
+
+    out_in = local(0, weight_in.at[:, :model], weight_ref.at[:, :model])
+    feed_in = [local(1, weight_in.at[:, model:], weight_ref.at[:, model:])]
+    feed_in += [local(2 + k, dy_in, dy_ref.at[k]) for k, dy_in in enumerate((dy0_in, dy1_in, dy2_in, dy3_in))]
     half = rows // 2
-    top, bottom = pl.ds(0, half), pl.ds(half, half)
-
-    def send(index, src, dst, peer):
-        return pltpu.make_async_remote_copy(
-            src_ref=src, dst_ref=dst, send_sem=send_sem.at[index], recv_sem=recv_sem.at[index],
-            device_id={"seq": peer}, device_id_type=MESH)
-
-    def rows_of(peer, size):
-        return pl.ds(pl.multiple_of(peer * size, size), size)
+    halves = (pl.ds(0, half), pl.ds(half, half))
+    whole = pl.ds(0, rows)
+    send = sender(send_sem, recv_sem)
 
     def tiles(count, body):
         def step(i, carry):
@@ -357,59 +388,65 @@
             return carry
         lax.fori_loop(0, count // TILE, step, 0)
 
+    def half_of(owner, h):
+        return pl.ds(pl.multiple_of(owner * rows + h * half, half), half)
+
     greet(peers)
-    turn = [send(k, out_ref.at[rows_of(peer, rows), :], heads_ref.at[k], peer) for k, peer in enumerate(peers)]
-    for k in (2, 0, 1):
-        turn[k].start()
-
-    def project(source, peer, base):
+    turn = [[send(3 * h + k, out_ref.at[half_of(peer, h), :], mixed_ref.at[halves[h], span(mine, width)], "seq", peer)
+             for k, peer in enumerate(peers)] for h in range(2)]
+    for h in range(2):
+        for k in (2, 0, 1):
+            turn[h][k].start()
+    mixed_ref[:, span(mine, width)] = out_ref[span(mine, rows), :]
+    x_sends = [send(6 + h, normed_ref.at[0, halves[h]], normed_ref.at[1, halves[h]], "seq", px) for h in range(2)]
+    y_sends = [send(8 + h, normed_ref.at[0, halves[h]], normed_ref.at[2, halves[h]], "seq", py) for h in range(2)]
+    x_relay = send(10, normed_ref.at[1, halves[0]], normed_ref.at[3, halves[0]], "seq", py)
+    y_relay = send(11, normed_ref.at[2, halves[1]], normed_ref.at[3, halves[1]], "seq", px)
+    for h in range(2):
+        for k in range(3):
+            turn[h][k].wait_recv()
+        if h == 0:
+            out_in.wait()
+
+        def project(c, h=h):
+            cols = pl.ds(c, TILE)
+            hidden_ref[halves[h], cols] = x_ref[halves[h], cols].astype(jnp.float32) + dot(
+                mixed_ref[halves[h], :], weight_ref[:, cols])
+
+        tiles(model, project)
+
+        def norm(i, carry, h=h):
+            part = pl.ds(pl.multiple_of(h * half + i * 64, 64), 64)
+            value = hidden_ref[part, :]
+            normed_ref[0, part, :] = (value * rms_scale(value) * gain_ref[...]).astype(low)
+            return carry
+
+        lax.fori_loop(0, half // 64, norm, 0)
+        x_sends[h].start()
+        y_sends[h].start()
+
+    def feed(slot, part):
+        def body(f):
+            gate = dot(normed_ref[slot, part, :], weight_ref[:, pl.ds(gate_at + f, TILE)])
+            up = dot(normed_ref[slot, part, :], weight_ref[:, pl.ds(up_at + f, TILE)])
+            grad_act = dot(dy_ref[slot, part, :], weight_ref[:, pl.ds(down_at + f, TILE)])
+            sigmoid = jax.nn.sigmoid(gate)
+            silu = gate * sigmoid
+            act_ref[slot, part, pl.ds(f, TILE)] = (silu * up).astype(low)
+            dgu_ref[slot, part, pl.ds(f, TILE)] = (
+                grad_act * up * sigmoid * (1.0 + gate * (1.0 - sigmoid))).astype(low)
+            dgu_ref[slot, part, pl.ds(units + f, TILE)] = (grad_act * silu).astype(low)
+        tiles(units, body)
+
+    def back(slot, part):
         def body(c):
             cols = pl.ds(c, TILE)
-            hidden_ref[:, cols] = base(cols) + dot(source, weight_ref[rows_of(peer, width), cols])
+            value = dot(dgu_ref[slot, part, :], weight_ref[cols, gate_at:down_at], NT)
+            if slot == 0:
+                own_ref[part, cols] = value
+            else:
+                give_ref[slot - 1, part, cols] = value.astype(low)
         tiles(model, body)
-
-    project(out_ref[rows_of(mine, rows), :], mine, lambda cols: x_ref[:, cols].astype(jnp.float32))
-    for k, peer in enumerate(peers):
-        turn[k].wait()
-        project(heads_ref[k], peer, lambda cols: hidden_ref[:, cols])
-
-    def norm(i, carry):
-        part = pl.ds(pl.multiple_of(i * 128, 128), 128)
-        h = hidden_ref[part, :]
-        normed_ref[0, part, :] = (h * rms_scale(h) * gain_ref[...]).astype(low)
-        return carry
-
-    lax.fori_loop(0, rows // 128, norm, 0)
-
-    px, py, pd = peers
-    x_top = send(3, normed_ref.at[0, top], normed_ref.at[1, top], px)
-    y_bottom = send(4, normed_ref.at[0, bottom], normed_ref.at[2, bottom], py)
-    x_bottom = send(5, normed_ref.at[0, bottom], normed_ref.at[1, bottom], px)
-    y_top = send(6, normed_ref.at[0, top], normed_ref.at[2, top], py)
-    for copy in (x_top, y_bottom, x_bottom, y_top):
-        copy.start()
-
-    def feed(slot):
-        def body(f):
-            gate = dot(normed_ref[slot], weight_ref[:, pl.ds(gate_at + f, TILE)])
-            up = dot(normed_ref[slot], weight_ref[:, pl.ds(up_at + f, TILE)])
-            grad_act = dot(dy_refs[slot][...], weight_ref[:, pl.ds(down_at + f, TILE)])
-            sigmoid = jax.nn.sigmoid(gate)
-            silu = gate * sigmoid
-            act_ref[slot, :, pl.ds(f, TILE)] = (silu * up).astype(low)
-            dgu_ref[slot, :, pl.ds(f, TILE)] = (
-                grad_act * up * sigmoid * (1.0 + gate * (1.0 - sigmoid))).astype(low)
-            dgu_ref[slot, :, pl.ds(units + f, TILE)] = (grad_act * silu).astype(low)
-        tiles(units, body)
-
-    def back(slot, store):
-        def body(c):
-            cols = pl.ds(c, TILE)
-            store(cols, dot(dgu_ref[slot], weight_ref[cols, gate_at:down_at], NT))
-        tiles(model, body)
-
-    def keep(cols, value):
-        own_ref[:, cols] = value
 
     def branch(slot):
         def body(c):
@@ -417,83 +454,115 @@
             branch_ref[slot, :, cols] = dot(act_ref[slot], weight_ref[cols, down_at:], NT).astype(low)
         tiles(model, body)
 
-    feed(0)
-    back(0, keep)
-    x_top.wait_recv()
-    x_relay = send(7, normed_ref.at[1, top], normed_ref.at[3, top], py)
+    def work(slot, h):
+        feed(slot, halves[h])
+        back(slot, halves[h])
+
+    start_far, start_plain, merge, finish = collect(send, 12, give_ref, transit_ref, take_ref, peers, 2)
+    outs = [local(6, hidden_ref, hidden_out)]
+    for copy in feed_in:
+        copy.wait()
+    feed(0, whole)
+    back(0, whole)
+    x_sends[0].wait_recv()
     x_relay.start()
-    y_bottom.wait_recv()
-    y_relay = send(8, normed_ref.at[2, bottom], normed_ref.at[3, bottom], px)
+    work(1, 0)
+    start_plain[0]()
+    y_sends[0].wait_recv()
+    work(2, 0)
+    y_sends[1].wait_recv()
     y_relay.start()
+    work(2, 1)
+    start_plain[1]()
+    x_sends[1].wait_recv()
+    work(1, 1)
     branch(0)
-    partials = [send(9 + k, give_ref.at[k], take_ref.at[k], peer) for k, peer in enumerate(peers)]
-    waits = ((x_bottom,), (y_top,), (x_relay, y_relay))
-    for k in range(3):
-        for copy in waits[k]:
-            copy.wait_recv()
-        feed(k + 1)
-
-        def hand(cols, value, k=k):
-            give_ref[k, :, cols] = value.astype(low)
-
-        back(k + 1, hand)
-        partials[k].start()
-    for copy in (x_top, y_bottom, x_bottom, y_top, x_relay, y_relay):
-        copy.wait_send()
-
-    def gate_up_grad(f):
-        for d in range(0, model, 512):
-            part = pl.ds(d, 512)
-            acc = dot(normed_ref[0, :, part], dgu_ref[0, :, pl.ds(f, TILE)], TN)
-            for slot in range(1, 4):
-                acc += dot(normed_ref[slot, :, part], dgu_ref[slot, :, pl.ds(f, TILE)], TN)
-            grads_ref[part, pl.ds(f, TILE)] = acc.astype(low)
-
-    tiles(2 * units, gate_up_grad)
-    for slot in range(1, 4):
-        branch(slot)
-    for copy in partials:
-        copy.wait()
-
+    outs.append(local(7, branch_ref.at[0], branch_out.at[0]))
+    x_relay.wait_recv()
+    work(3, 0)
+    start_far(0)
+    y_relay.wait_recv()
+    work(3, 1)
+    start_far(1)
+
+    def gate_up_grad(first, count):
+        def step(i, carry):
+            f = pl.multiple_of(i * TILE, TILE)
+            for d in range(0, model, 512):
+                part = pl.ds(d, 512)
+                acc = dot(normed_ref[0, :, part], dgu_ref[0, :, pl.ds(f, TILE)], TN)
+                for slot in range(1, 4):
+                    acc += dot(normed_ref[slot, :, part], dgu_ref[slot, :, pl.ds(f, TILE)], TN)
+                grads_ref[part, pl.ds(f, TILE)] = acc.astype(low)
+            return carry
+        lax.fori_loop(first, first + count, step, 0)
+
+    merge(0, 0)
+    gate_up_grad(0, 1)
+    merge(1, 0)
+    merge(0, 1)
+    gate_up_grad(1, 1)
+    merge(1, 1)
+    gate_up_grad(2, 2 * units // TILE - 2)
+    outs.append(local(8, grads_ref.at[:, :2 * units], grads_out.at[:, :2 * units]))
     gain_grad_ref[...] = jnp.zeros_like(gain_grad_ref)
-
-    def norm_back(i, carry):
-        part = pl.ds(pl.multiple_of(i * 64, 64), 64)
-        h = hidden_ref[part, :]
-        inv = rms_scale(h)
-        grad = own_ref[part, :]
-        for k in range(3):
-            grad += take_ref[k, part, :].astype(jnp.float32)
-        gain_grad_ref[0:1, :] += jnp.sum(grad * h * inv, axis=0, keepdims=True)
-        scaled = grad * gain_ref[...]
-        dh = dy0_ref[part, :].astype(jnp.float32) + (
-            inv * scaled - h * inv**3 * jnp.mean(h * scaled, axis=-1, keepdims=True))
-        dh_ref[part, :] = dh
-        normed_ref[1, part, :] = dh.astype(low)
-        return carry
-
-    lax.fori_loop(0, rows // 64, norm_back, 0)
-
-    sends = [send(12 + k, do_give_ref.at[k], do_ref.at[rows_of(mine, rows), :], peer) for k, peer in enumerate(peers)]
-    for k in (2, 0, 1):
-        do_give_ref[k] = dot(normed_ref[1], weight_ref[rows_of(peers[k], width), :model], NT).astype(low)
-        sends[k].start()
-    do_ref[rows_of(mine, rows), :] = dot(normed_ref[1], weight_ref[rows_of(mine, width), :model], NT).astype(low)
+    sends = [[send(22 + 3 * h + k, do_give_ref.at[k, halves[h]], do_ref.at[half_of(mine, h), :], "seq", peer)
+              for k, peer in enumerate(peers)] for h in range(2)]
+    for h in range(2):
+        finish(h)
+
+        def norm_back(i, carry, h=h):
+            part = pl.ds(pl.multiple_of(h * half + i * 64, 64), 64)
+            value = hidden_ref[part, :]
+            inv = rms_scale(value)
+            grad = own_ref[part, :] + take_ref[0, part, :].astype(jnp.float32) + take_ref[1, part, :].astype(jnp.float32)
+            gain_grad_ref[0:1, :] += jnp.sum(grad * value * inv, axis=0, keepdims=True)
+            scaled = grad * gain_ref[...]
+            dh = dy_ref[0, part, :].astype(jnp.float32) + (
+                inv * scaled - value * inv**3 * jnp.mean(value * scaled, axis=-1, keepdims=True))
+            dh_ref[part, :] = dh
+            low_ref[part, :] = dh.astype(low)
+            return carry
+
+        lax.fori_loop(0, half // 64, norm_back, 0)
+        for k in (2, 0, 1):
+            do_give_ref[k, halves[h], :] = dot(
+                low_ref[halves[h], :], weight_ref[span(peers[k], width), :model], NT).astype(low)
+            sends[h][k].start()
+        do_ref[half_of(mine, h), :] = dot(low_ref[halves[h], :], weight_ref[span(mine, width), :model], NT).astype(low)
+
+    outs.append(local(9, dh_ref, dh_out))
 
     def down_grad(f):
         for d in range(0, model, 512):
             part = pl.ds(d, 512)
-            acc = dot(dy_refs[0][:, part], act_ref[0, :, pl.ds(f, TILE)], TN)
+            acc = dot(dy_ref[0, :, part], act_ref[0, :, pl.ds(f, TILE)], TN)
             for slot in range(1, 4):
-                acc += dot(dy_refs[slot][:, part], act_ref[slot, :, pl.ds(f, TILE)], TN)
+                acc += dot(dy_ref[slot, :, part], act_ref[slot, :, pl.ds(f, TILE)], TN)
             grads_ref[part, pl.ds(2 * units + f, TILE)] = acc.astype(low)
 
     tiles(units, down_grad)
-    grads_ref[rows_of(mine, width), 3 * units:] = dot(out_ref[rows_of(mine, rows), :], normed_ref[1], TN).astype(low)
-    for k, peer in enumerate(peers):
-        grads_ref[rows_of(peer, width), 3 * units:] = dot(heads_ref[k], normed_ref[1], TN).astype(low)
-    for copy in sends:
+    outs.append(local(10, grads_ref.at[:, 2 * units:3 * units], grads_out.at[:, 2 * units:3 * units]))
+    for slot in range(1, 4):
+        branch(slot)
+        outs.append(local(10 + slot, branch_ref.at[slot], branch_out.at[slot]))
+
+    def out_grad(c):
+        cols = pl.ds(c, TILE)
+        grads_ref[:, pl.ds(3 * units + c, TILE)] = dot(mixed_ref[...], low_ref[:, cols], TN).astype(low)
+
+    tiles(model, out_grad)
+    outs.append(local(14, grads_ref.at[:, 3 * units:], grads_out.at[:, 3 * units:]))
+    for copy in outs:
         copy.wait()
+    for h in range(2):
+        x_sends[h].wait_send()
+        y_sends[h].wait_send()
+        for k in range(3):
+            turn[h][k].wait_send()
+            sends[h][k].wait()
+    x_relay.wait_send()
+    y_relay.wait_send()
 
 
 def middle(dealt_out, x, weights, gain, dy, units):
@@ -513,19 +582,28 @@
             shape((group_len, width), low),
             shape((8, model), f32),
         ),
-        in_specs=[vmem()] * 8,
-        out_specs=(vmem(),) * 6,
+        in_specs=[vmem(), vmem(), hbm(), vmem()] + [hbm()] * 4,
+        out_specs=(hbm(), hbm(), hbm(), hbm(), vmem(), vmem()),
         scratch_shapes=[
-            pltpu.VMEM((3, rows, width), low),
+            pltpu.VMEM(weights.shape, low),
+            pltpu.VMEM((4, rows, model), low),
+            pltpu.VMEM((rows, model), f32),
+            pltpu.VMEM((4, rows, model), low),
+            pltpu.VMEM((model, 3 * units + model), low),
+            pltpu.VMEM((rows, model), f32),
+            pltpu.VMEM((rows, model), low),
             pltpu.VMEM((4, rows, model), low),
             pltpu.VMEM((4, rows, units), low),
             pltpu.VMEM((4, rows, 2 * units), low),
             pltpu.VMEM((3, rows, model), low),
-            pltpu.VMEM((3, rows, model), low),
+            pltpu.VMEM((2, rows // 2, model), low),
+            pltpu.VMEM((2, rows, model), low),
             pltpu.VMEM((rows, model), f32),
+            pltpu.VMEM((rows, model), low),
             pltpu.VMEM((3, rows, width), low),
             pltpu.SemaphoreType.DMA((15,)),
-            pltpu.SemaphoreType.DMA((15,)),
+            pltpu.SemaphoreType.DMA((28,)),
+            pltpu.SemaphoreType.DMA((28,)),
         ],
         compiler_params=pltpu.CompilerParams(
             vmem_limit_bytes=62 << 20, collective_id=1, has_side_effects=True),
@@ -533,99 +611,54 @@
     )(dealt_out, x, weights, gain, *dy)
 
 
-def front_kernel(x_ref, weight_ref, gain_cols_ref, qkv_ref, normed_ref, slab_ref, gains_ref, slots_ref, send_sem, recv_sem):
-    low = jnp.bfloat16
-    rows, model = x_ref.shape
-    shard = weight_ref.shape[0]
-    width = weight_ref.shape[1] // 12
-    count = model // shard
+def gather_kernel(x_ref, all_ref, local_sem, send_sem, recv_sem):
+    rows = x_ref.shape[0]
     mine, peers = seq_peers()
-    place, sibling, others = shard_peers(count)
     send = sender(send_sem, recv_sem)
-    own = span(place, shard)
-    for b in range(3):
-        slab_ref[own, b * width:(b + 1) * width] = weight_ref[:, pl.ds(
-            pl.multiple_of(b * 4 * width + mine * width, width), width)].astype(low)
-    slab_ref[own, 3 * width:] = gain_cols_ref[...].astype(low)
-    greet(peers, [sibling] + others)
-    forward, arrivals, finish = spread(send, 0, x_ref, [slots_ref.at[k] for k in range(3)], peers)
-    direct = [send(6 + k, slab_ref.at[own], slab_ref.at[own], "fsdp", peer) for k, peer in enumerate(others)]
-    twins = [send(6 + len(others), slab_ref.at[own], slab_ref.at[own], "fsdp", sibling)]
-    for copy in direct:
+    half = rows // 2
+    px, py, _ = peers
+
+    def part(owner, h):
+        return all_ref.at[pl.ds(pl.multiple_of(owner * rows + h * half, half), half)]
+
+    greet(peers)
+    x_sends = [send(h, x_ref.at[pl.ds(h * half, half)], part(mine, h), "seq", px) for h in range(2)]
+    y_sends = [send(2 + h, x_ref.at[pl.ds(h * half, half)], part(mine, h), "seq", py) for h in range(2)]
+    for copy in (x_sends[0], y_sends[1], x_sends[1], y_sends[0]):
         copy.start()
-    twins[0].start()
-
-    def pass_on(k):
-        direct[k].wait_recv()
-        part = span(lax.rem(place - 2 * (k + 1) + count, count), shard)
-        copy = send(7 + len(others) + k, slab_ref.at[part], slab_ref.at[part], "fsdp", sibling)
-        copy.start()
-        twins.append(copy)
-
-    pass_on(0)
-    forward()
-    for k in range(1, len(others)):
-        pass_on(k)
-    for copy in twins:
-        copy.wait_recv()
-
-    def flip(i, carry):
-        part = pl.ds(pl.multiple_of(i * 128, 128), 128)
-        gains_ref[:, part] = slab_ref[part, 3 * width:].astype(jnp.float32).T[:8]
-        return carry
-
-    lax.fori_loop(0, model // 128, flip, 0)
-
-    def project(source, owner):
-        def norm(i, carry):
-            part = pl.ds(pl.multiple_of(i * 64, 64), 64)
-            x = source[part, :].astype(jnp.float32)
-            normed_ref[pl.ds(pl.multiple_of(owner * rows + i * 64, 64), 64), :] = (
-                x * rms_scale(x) * gains_ref[0:1, :]).astype(low)
-            return carry
-
-        lax.fori_loop(0, rows // 64, norm, 0)
-        block = span(owner, rows)
-        for b in range(3):
-            part = slice(b * width, (b + 1) * width)
-            qkv_ref[block, part] = dot(normed_ref[block, :], slab_ref[:, part]).astype(low)
-
-    project(x_ref, mine)
-    for k in range(3):
-        arrivals[k]()
-        project(slots_ref.at[k], peers[k])
-    finish()
-    for copy in direct + twins:
+    keep = pltpu.make_async_copy(x_ref, all_ref.at[span(mine, rows)], local_sem)
+    keep.start()
+    x_relay = send(4, part(px, 0), part(px, 0), "seq", py)
+    y_relay = send(5, part(py, 1), part(py, 1), "seq", px)
+    x_sends[0].wait_recv()
+    x_relay.start()
+    y_sends[1].wait_recv()
+    y_relay.start()
+    x_sends[1].wait_recv()
+    y_sends[0].wait_recv()
+    for copy in x_sends + y_sends:
         copy.wait_send()
-
-
-def front(x, weight, gain_cols):
-    low = jnp.bfloat16
+    x_relay.wait()
+    y_relay.wait()
+    keep.wait()
+
+
+def gather_rows(x):
     rows, model = x.shape
-    shard, columns = weight.shape
-    part = columns // 4
-    shape = jax.ShapeDtypeStruct
-    copies = 8 + 2 * (model // shard // 2)
     return pl.pallas_call(
-        front_kernel,
-        name="front",
-        out_shape=(
-            shape((4 * rows, part), low),
-            shape((4 * rows, model), low),
-            shape((model, part + 128), low),
-            shape((8, model), jnp.float32),
-        ),
-        in_specs=[vmem()] * 3,
-        out_specs=(vmem(),) * 4,
+        gather_kernel,
+        name="gather_rows",
+        out_shape=jax.ShapeDtypeStruct((4 * rows, model), x.dtype),
+        in_specs=[pl.BlockSpec(memory_space=pl.ANY)],
+        out_specs=pl.BlockSpec(memory_space=pl.ANY),
         scratch_shapes=[
-            pltpu.VMEM((3, rows, model), low),
-            pltpu.SemaphoreType.DMA((copies,)),
-            pltpu.SemaphoreType.DMA((copies,)),
+            pltpu.SemaphoreType.DMA,
+            pltpu.SemaphoreType.DMA((6,)),
+            pltpu.SemaphoreType.DMA((6,)),
         ],
-        compiler_params=pltpu.CompilerParams(
-            vmem_limit_bytes=40 << 20, collective_id=0, has_side_effects=True),
+        compiler_params=pltpu.CompilerParams(collective_id=0, has_side_effects=True),
         cost_estimate=pl.CostEstimate(flops=40_000_000_000, bytes_accessed=20 << 20, transcendentals=0),
-    )(x, weight, gain_cols)
+    )(x)
 
 
 def rear_kernel(grad_ref, normed_ref, slab_ref, gains_ref, x_ref, dh_ref, input_grad_ref, gain_grad_ref, piece_ref,
@@ -638,30 +671,33 @@
     place, sibling, others = shard_peers(count)
     send = sender(send_sem, recv_sem)
 
-    def partial(owner, store):
-        block = span(owner, rows)
+    half = rows // 2
+
+    def partial(owner, first, count, store):
+        block = pl.ds(pl.multiple_of(owner * rows + first, half), count)
+
         def body(i, carry):
             cols = pl.ds(pl.multiple_of(i * TILE, TILE), TILE)
             store(cols, dot(grad_ref[block, :], slab_ref[cols, :columns], NT))
             return carry
         lax.fori_loop(0, model // TILE, body, 0)
 
-    def hand(k):
+    def hand(k, first, count):
         def store(cols, value):
-            give_ref[k, :, cols] = value.astype(low)
-        return store
+            give_ref[k, pl.ds(first, count), cols] = value.astype(low)
+        partial(peers[k], first, count, store)
 
     def keep(cols, value):
         own_ref[:, cols] = value
 
     greet(peers, [sibling] + others)
-    far, x_start, y_start, merge, finish = collect(send, 0, give_ref, transit_ref, take_ref, peers)
-    partial(peers[2], hand(2))
-    far()
-    partial(peers[0], hand(0))
-    x_start()
-    partial(peers[1], hand(1))
-    y_start()
+    start_far, start_plain, merge, finish = collect(send, 0, give_ref, transit_ref, take_ref, peers, 2)
+    for h in range(2):
+        hand(2, h * half, half)
+        start_far(h)
+    for h in range(2):
+        hand(h, 0, rows)
+        start_plain[h]()
 
     def weight_term(i, carry):
         part = pl.ds(pl.multiple_of(i * TILE, TILE), TILE)
@@ -672,22 +708,23 @@
     twins = []
     for k in range(count // 2):
         part = span(lax.rem(sibling + 2 * k, count), shard)
-        twins.append(send(6 + k, term_ref.at[part], twin_ref.at[k], "fsdp", sibling))
+        twins.append(send(10 + k, term_ref.at[part], twin_ref.at[k], "fsdp", sibling))
         twins[k].start()
-    merge()
+    for c in range(2):
+        for h in range(2):
+            merge(h, c)
     direct = []
     for k in range(count // 2):
         twins[k].wait_recv()
         part = span(lax.rem(place + 2 * k, count), shard)
         sum_ref[k] = (term_ref[part, :].astype(jnp.float32) + twin_ref[k].astype(jnp.float32)).astype(low)
         if k > 0:
-            copy = send(6 + count // 2 + k, sum_ref.at[k], shard_take_ref.at[k], "fsdp", others[k - 1])
+            copy = send(10 + count // 2 + k, sum_ref.at[k], shard_take_ref.at[k], "fsdp", others[k - 1])
             copy.start()
             direct.append(copy)
-    partial(mine, keep)
+    partial(mine, 0, rows, keep)
     for copy in twins:
         copy.wait_send()
-    finish()
     gain_grad_ref[...] = jnp.zeros_like(gain_grad_ref)
 
     def norm_back(i, carry):
@@ -701,7 +738,9 @@
             inv * scaled - x * inv**3 * jnp.mean(x * scaled, axis=-1, keepdims=True))).astype(low)
         return carry
 
-    lax.fori_loop(0, rows // 64, norm_back, 0)
+    for h in range(2):
+        finish(h)
+        lax.fori_loop(h * half // 64, (h + 1) * half // 64, norm_back, 0)
     total = sum_ref[0].astype(jnp.float32)
     for k in range(1, count // 2):
         direct[k - 1].wait()
@@ -715,7 +754,7 @@
     columns = grad.shape[1]
     count = model // shard
     shape = jax.ShapeDtypeStruct
-    copies = 8 + count
+    copies = 12 + count
     return pl.pallas_call(
         rear_kernel,
         name="rear",
@@ -848,24 +887,27 @@
     row_count, model_width = block_input.shape[1:]
     group_len = row_count * seq_count
     shard = weight_qkv.shape[0]
+    head_width = weight_qkv.shape[1] // 3 // seq_count
     part_units = weight_down.shape[1] // seq_count
     perm = permutation[0]
     offs = offsets[0]
     position = jnp.arange(group_len, dtype=jnp.int32)
     start = jnp.max(jnp.where(offs[None, :] <= position[:, None], offs[None, :], 0), axis=1)
 
-    def columns(weight, blocks, width):
-        cut = weight.reshape(shard, blocks, seq_count, width)
-        return lax.dynamic_index_in_dim(cut, mine, 2, keepdims=False).reshape(shard, blocks * width).astype(low)
-
-    weights = lax.all_gather(jnp.concatenate(
-        [weight_out.astype(low), columns(weight_gate_up, 2, part_units), columns(weight_down, 1, part_units)], axis=1),
-        "fsdp", axis=0, tiled=True)
+    def columns(weight, width):
+        blocks = weight.shape[1] // (seq_count * width)
+        return [lax.dynamic_slice_in_dim(weight, (b * seq_count + mine) * width, width, axis=1) for b in range(blocks)]
+
+    def gather_weight(parts):
+        return lax.all_gather(jnp.concatenate(parts, axis=1).astype(low), "fsdp", axis=0, tiled=True)
+
     gain_cols = jnp.pad(jnp.stack([norm_gain_a, norm_gain_b], axis=1), ((0, 0), (0, 126)))
-    qkv, normed_a, slab, gains = front(block_input[0], weight_qkv, gain_cols)
-    grad_own, qkv = lax.optimization_barrier((cotangent[0], qkv))
+    slab = gather_weight(columns(weight_qkv, head_width) + [gain_cols])
+    weights = gather_weight([weight_out] + columns(weight_gate_up, part_units) + columns(weight_down, part_units))
+    rows_all = gather_rows(block_input[0])
+    grad_own, rows_all = lax.optimization_barrier((cotangent[0], rows_all))
     grad_rows = [cotangent[0]] + swaps([grad_own] * 3)
-    ordered, dealt_out, wide_out, log_total = attention_forward(offs, qkv, perm, start)
+    ordered, dealt_out, wide_out, log_total, normed_a, gains = attention_forward(offs, rows_all, slab, perm, start)
     hidden, branch, grads, grad_hidden, grad_heads, gain_b_term = middle(
         dealt_out, block_input[0], weights, gains[1:2], grad_rows, part_units)
     pieces = lax.psum_scatter(grads, "fsdp", scatter_dimension=0, tiled=True)

time: 429 us -> 401 us (0.935)
  Pallas kernels: 364 us -> 345 us
  local copies, waits for them, and re-layouts: 23.4 us -> 13.3 us
    pallas_call x1, Pallas kernels: 132 us -> 111 us  [middle(): pl.pallas_call(middle_kernel, name='middle', out_shape=(shape((rows, mode...]
    pallas_call x1, Pallas kernels: 60.2 us -> 45.6 us  [rear(): pl.pallas_call(rear_kernel, name='rear', out_shape=(shape((rows, model),...]
    pallas_call x2, Pallas kernels: 83.6 us -> 93 us  [the longest x1 54 us: attention_forward(): pl.pallas_call(forward_kernel, name='attention_forward', out_shape=(shape...]
    all_gather x1 -> x2, waiting for transfers between devices: 0.01 us -> 8.56 us  [gather_weight(): lax.all_gather(jnp.concatenate(parts, axis=1).astype(low), 'fsdp', axis=0...]
    unnamed x46 -> x28, local copies, waits for them, and re-layouts: 15 us -> 6.83 us
    pallas_call x1, Pallas kernels: 39.7 us -> 44.5 us  [attention_backward(): pl.pallas_call(backward_kernel, name='attention_backward', out_shape=jax....]
  transfers between devices with their start and end apart: 8 -> 9, of which waited for: 2 -> 2; matrix products, arithmetic and copies ran while one was open for 2% -> 3% of each run, Pallas kernels for 43% -> 46%
where the time goes in v4:
time: 401 us
  Pallas kernels  345 us (86%)
  between operations  14 us (3%)
  local copies, waits for them, and re-layouts  13.3 us (3%)
  other arithmetic  12.1 us (3%)
  waiting for transfers between devices  9.71 us (2%)
  starting transfers between devices  7.23 us (2%)
    pallas_call x1, Pallas kernels, middle(): pl.pallas_call(middle_kernel, name='middle', out_shape=(shape((rows, mode...  111 us
    pallas_call x1, Pallas kernels, attention_forward(): pl.pallas_call(forward_kernel, name='attention_forward', out_shape=(shape...  54 us
    pallas_call x1, Pallas kernels, last(): pl.pallas_call(last_kernel, name='last', out_shape=(shape((shard, 4 * col...  50.8 us
    pallas_call x1, Pallas kernels, rear(): pl.pallas_call(rear_kernel, name='rear', out_shape=(shape((rows, model),...  45.6 us
    pallas_call x1, Pallas kernels, attention_backward(): pl.pallas_call(backward_kernel, name='attention_backward', out_shape=jax....  44.5 us
    pallas_call x1, Pallas kernels, gather_rows(): pl.pallas_call(gather_kernel, name='gather_rows', out_shape=jax.ShapeDtyp...  39 us
    all_gather x2, waiting for transfers between devices, gather_weight(): lax.all_gather(jnp.concatenate(parts, axis=1).astype(low), 'fsdp', axis=0...  8.56 us
  transfers between devices with their start and end apart: 9, of which 2 were waited for; matrix products, arithmetic and copies ran while one was open for 3% of the time, Pallas kernels for 46%

profile of v4, /device:TPU:0, one launch (start us, length us, event | category | flops | bytes accessed | tf_op | source)
XLA Modules:
  0.0 401.0 jit_solution(18417188512999261245)
XLA Ops:
  7.2 0.0 all-gather.3.cloned.1.call-start
  7.2 0.7 convert_bitcast_fusion
  7.9 0.1 copy.27
  8.1 1.1 dynamic-slice_convert_fusion.5
  9.1 0.7 fusion.6
  9.8 0.0 all-gather.3.cloned.1.call-update
  9.8 0.0 all-gather.5.cloned.1.call-start
  9.9 1.1 convert.38
  11.0 1.5 dynamic-slice_convert_fusion.2
  12.5 1.0 pad_maximum_fusion
  13.5 0.0 all-gather.5.cloned.1.call-update
  13.5 0.0 reduce-scatter.2.cloned.1.call-start
  13.6 0.0 copy-start.12
  13.6 0.0 copy-start
  13.6 0.0 copy-start.1
  13.6 39.0 %gather_rows.1.x_ref = bf16[2048,1024]{1,0:T(8,128)(2,1)} custom-call(bf16[512,1024]{1,0:T(8,128)(2,1)} %bitcast.32), custom_call_target="tpu_custom_call" | custom-call | flops 40000000000 | bytes 20971520 | tf_op jit(solution)/shard_map/gather_rows/pallas_call | solution.py:648
  52.7 1.5 collective-permute-start.2
  54.2 1.5 collective-permute-start.1
  55.7 0.6 collective-permute-start
  56.2 0.4 copy.28.perm_col_ref
  56.6 0.1 select_reduce_fusion
  56.7 0.0 all-gather.3.cloned.1.call-done.slab_ref
  56.8 1.5 copy-done.2
  58.3 54.0 %attention_forward.1 = (bf16[2048,768]{1,0:T(8,128)(2,1)}, bf16[2048,256]{1,0:T(8,128)(2,1)S(1)}, f32[256,2048]{1,0:T(8,128)S(1)}, f32[8,2048]{1,0:T(8,128)S(1)}...) custom-call(s32[3]{0:T(128)S(1)} %bitcast.30, bf16[2048,1024]{1,0:T(8,128)(2,1)} %gather_rows.1.x_ref, ...), custom_call_target="tpu_custom_call" | custom-call | flops 24000000000 | bytes 16777216 | tf_op jit(solution)/shard_map/attention_forward/pallas_call | solution.py:205
  112.2 1.3 copy-done.6
  113.6 1.0 copy-done.8
  114.5 0.6 slice.21.gain_ref
  115.1 0.0 collective-permute-done.dy1_in
  115.1 8.5 %all-gather.5.cloned.1.call-done.weight_in = bf16[1024,4096]{1,0:T(8,128)(2,1)} async-done(((bf16[128,4096]{1,0:T(8,128)(2,1)}), bf16[1024,4096]{1,0:T(8,128)(2,1)}) %all-gather.5.cloned.1.call-update) | async-done | bytes 8388624 | tf_op jit(solution)/shard_map/all_gather | solution.py:902
  123.7 110.7 %middle.1 = (f32[512,1024]{1,0:T(8,128)}, bf16[4,512,1024]{2,1,0:T(8,128)(2,1)}, bf16[1024,4096]{1,0:T(8,128)(2,1)}, f32[512,1024]{1,0:T(8,128)}, bf16[2048,256]{1,0:T(8,128)(2,1)}, /*index=5*/f32[8,1024]{1,0:T(8,128)}) custom-call(bf16[2048,256]{1,0:T(8,128)(2,1)} %copy-done.8, bf16[512,1024]{1,0:T(8,128)(2,1)} %bitcast.33, ...), custom_call_target="tpu_custom_call" | custom-call | flops 60000002048 | bytes 41943040 | tf_op jit(solution)/shard_map/middle/pallas_call | solution.py:574
  234.4 0.0 reduce-scatter.2.cloned.1.call-update
  234.4 0.0 copy-start.7
  234.4 2.3 slice_bitcast_fusion.2
  236.8 1.5 collective-permute-start.3
  238.3 1.5 collective-permute-start.5
  239.8 0.6 collective-permute-start.4
  240.3 44.5 %attention_backward.1.grad_ref = bf16[2048,768]{1,0:T(8,128)(2,1)} custom-call(s32[3]{0:T(128)S(1)} %bitcast.31, bf16[2048,256]{1,0:T(8,128)(2,1)S(1)} %copy-done.9, bf16[2048,768]{1,0:T(8,128)(2,1)} %get-tuple-element.37.sorted_ref, s32[1,2048]{1,0:T(1,128)S(1)} %copy-done, s32[2048,1]{1,0:T(8,128)S(1)} %copy.28.perm_col_ref, s32[1,2048]{1,0:T(1,128)S(1)} %bitcast.28, ...), custom_call_target="tpu_custom_call" | custom-call | flops 40000000000 | bytes 16777216 | tf_op jit(solution)/shard_map/attention_backward/pallas_call | solution.py:231
  284.9 45.6 %rear.1 = (bf16[512,1024]{1,0:T(8,128)(2,1)S(1)}, f32[8,1024]{1,0:T(8,128)S(1)}, bf16[128,768]{1,0:T(8,128)(2,1)S(1)}) custom-call(bf16[2048,768]{1,0:T(8,128)(2,1)} %attention_backward.1.grad_ref, bf16[2048,1024]{1,0:T(8,128)(2,1)} %get-tuple-element.40.normed_ref, bf16[1024,896]{1,0:T(8,128)(2,1)S(1)} %copy-done.3, ...), custom_call_target="tpu_custom_call" | custom-call | flops 49999998976 | bytes 20971520 | tf_op jit(solution)/shard_map/rear/pallas_call | solution.py:758
  330.6 3.2 fusion.4
  333.8 1.1 reduce-scatter.2.cloned.1.call-done.pieces_ref
  334.9 1.2 copy-done.5
  336.1 50.8 %last.1 = (bf16[128,3072]{1,0:T(8,128)(2,1)S(1)}, f32[128,1024]{1,0:T(8,128)S(1)}, bf16[128,8192]{1,0:T(8,128)(2,1)S(1)}, bf16[128,4096]{1,0:T(8,128)(2,1)S(1)}, f32[8,1024]{1,0:T(8,128)S(1)}) custom-call(bf16[128,4096]{1,0:T(8,128)(2,1)S(1)} %copy-done.5, bf16[128,768]{1,0:T(8,128)(2,1)S(1)} %get-tuple-element.44.qkv_ref, ...), custom_call_target="tpu_custom_call" | custom-call | flops 40000000000 | bytes 20971520 | tf_op jit(solution)/shard_map/last/pallas_call | solution.py:849
  386.9 0.5 slice_bitcast_fusion.3
  387.4 1.3 convert_element_type.37
  388.7 1.5 convert_element_type.39
  390.3 2.4 convert_element_type.38
  392.7 1.0 copy.32
  393.7 0.8 copy.33
  (25 shorter events, 0.1 us)
Async XLA Ops:
  7.2 49.6 %all-gather.3.cloned.1.call-start = ((), (), s32[]{:S(2)}) async-start(), calls=%async_computation.1 | async-start | bytes 2064384 | tf_op jit(solution)/shard_map/all_gather | solution.py:902
  9.8 113.8 %all-gather.5.cloned.1.call-start = ((), (), s32[]{:S(2)}) async-start(), calls=%async_computation.2 | async-start | bytes 9437184 | tf_op jit(solution)/shard_map/all_gather | solution.py:902
  13.5 321.3 %reduce-scatter.2.cloned.1.call-start = ((), (), s32[]{:S(2)}) async-start(), calls=%async_computation.3 | async-start | bytes 9437184 | tf_op jit(solution)/shard_map/reduce_scatter | solution.py:913
  13.6 39.1 %copy-start.12 = (bf16[1,512,1024]{2,1,0:T(8,128)(2,1)S(1)}, bf16[1,512,1024]{2,1,0:T(8,128)(2,1)}, u32[]{:S(2)}) copy-start(bf16[1,512,1024]{2,1,0:T(8,128)(2,1)} %param.18) | copy-start | bytes 3145732
  13.6 42.6 %copy-start = (s32[1,2048]{1,0:T(1,128)S(1)}, s32[1,2048]{1,0:T(1,128)}, u32[]{:S(2)}) copy-start(s32[1,2048]{1,0:T(1,128)} %perm_row_ref.3) | copy-start | bytes 24580
  13.6 43.0 %copy-start.1 = (s32[1,3]{1,0:T(1,128)S(1)}, s32[1,3]{1,0:T(1,128)}, u32[]{:S(2)}) copy-start(s32[1,3]{1,0:T(1,128)} %param.20) | copy-start | bytes 40
  52.7 62.4 %collective-permute-start.2 = (bf16[512,1024]{1,0:T(8,128)(2,1)S(1)}, bf16[512,1024]{1,0:T(8,128)(2,1)}, u32[]{:S(2)}, u32[]{:S(2)}) collective-permute-start(bf16[512,1024]{1,0:T(8,128)(2,1)S(1)} %bitcast.36), channel_id=1, source_target_pairs={{0,24},{8,16},{16,8},{24,0},{1,25},{9,17},{17,9},{25,1},{2,26},{10... | collective-permute-start | bytes 3145736 | tf_op jit(solution)/shard_map/ppermute | solution.py:877
  54.2 60.9 %collective-permute-start.1 = (bf16[512,1024]{1,0:T(8,128)(2,1)S(1)}, bf16[512,1024]{1,0:T(8,128)(2,1)}, u32[]{:S(2)}, u32[]{:S(2)}) collective-permute-start(bf16[512,1024]{1,0:T(8,128)(2,1)S(1)} %bitcast.37), channel_id=1, source_target_pairs={{0,16},{8,24},{16,0},{24,8},{1,17},{9,25},{17,1},{25,9},{2,18},{10... | collective-permute-start | bytes 3145736 | tf_op jit(solution)/shard_map/ppermute | solution.py:877
  55.7 59.5 %collective-permute-start = (bf16[512,1024]{1,0:T(8,128)(2,1)S(1)}, bf16[512,1024]{1,0:T(8,128)(2,1)}, u32[]{:S(2)}, u32[]{:S(2)}) collective-permute-start(bf16[512,1024]{1,0:T(8,128)(2,1)S(1)} %bitcast.38), channel_id=1, source_target_pairs={{0,8},{8,0},{16,24},{24,16},{1,9},{9,1},{17,25},{25,17},{2,10},{10... | collective-permute-start | bytes 3145736 | tf_op jit(solution)/shard_map/ppermute | solution.py:877
  56.8 1.5 copy-start.2
  112.2 1.3 copy-start.6
  113.6 1.0 copy-start.8
  234.4 5.9 %copy-start.7 = (f32[256,2048]{1,0:T(8,128)S(1)}, f32[256,2048]{1,0:T(8,128)}, u32[]{:S(2)}) copy-start(f32[256,2048]{1,0:T(8,128)} %copy-done.6) | copy-start | bytes 6291460
  234.4 5.9 %copy-start.9 = (bf16[2048,256]{1,0:T(8,128)(2,1)S(1)}, bf16[2048,256]{1,0:T(8,128)(2,1)}, u32[]{:S(2)}) copy-start(bf16[2048,256]{1,0:T(8,128)(2,1)} %get-tuple-element.36.grad_ref) | copy-start | bytes 3145732
  236.8 93.8 %collective-permute-start.3 = (bf16[512,1024]{1,0:T(8,128)(2,1)S(1)}, bf16[512,1024]{1,0:T(8,128)(2,1)S(1)}, u32[]{:S(2)}, u32[]{:S(2)}) collective-permute-start(bf16[512,1024]{1,0:T(8,128)(2,1)S(1)} %get-tuple-element.52), channel_id=1, source_target_pairs={{0,8},{8,0},{16,24},{24,16},{1,9},{9,1},{17,25},{25,17},{2,10},{10... | collective-permute-start | bytes 3145736 | tf_op jit(solution)/shard_map/ppermute | solution.py:877
  238.3 92.3 %collective-permute-start.5 = (bf16[512,1024]{1,0:T(8,128)(2,1)S(1)}, bf16[512,1024]{1,0:T(8,128)(2,1)S(1)}, u32[]{:S(2)}, u32[]{:S(2)}) collective-permute-start(bf16[512,1024]{1,0:T(8,128)(2,1)S(1)} %get-tuple-element.53), channel_id=1, source_target_pairs={{0,24},{8,16},{16,8},{24,0},{1,25},{9,17},{17,9},{25,1},{2,26},{10... | collective-permute-start | bytes 3145736 | tf_op jit(solution)/shard_map/ppermute | solution.py:877
  239.8 90.8 %collective-permute-start.4 = (bf16[512,1024]{1,0:T(8,128)(2,1)S(1)}, bf16[512,1024]{1,0:T(8,128)(2,1)S(1)}, u32[]{:S(2)}, u32[]{:S(2)}) collective-permute-start(bf16[512,1024]{1,0:T(8,128)(2,1)S(1)} %get-tuple-element.54), channel_id=1, source_target_pairs={{0,16},{8,24},{16,0},{24,8},{1,17},{9,25},{17,1},{25,9},{2,18},{10... | collective-permute-start | bytes 3145736 | tf_op jit(solution)/shard_map/ppermute | solution.py:877
  240.3 44.5 %copy-start.3 = (bf16[1024,896]{1,0:T(8,128)(2,1)S(1)}, bf16[1024,896]{1,0:T(8,128)(2,1)}, u32[]{:S(2)}) copy-start(bf16[1024,896]{1,0:T(8,128)(2,1)} %all-gather.3.cloned.1.call-done.slab_ref) | copy-start | bytes 5505028
  240.3 44.6 %copy-start.4 = (bf16[1,512,1024]{2,1,0:T(8,128)(2,1)S(1)}, bf16[1,512,1024]{2,1,0:T(8,128)(2,1)}, u32[]{:S(2)}) copy-start(bf16[1,512,1024]{2,1,0:T(8,128)(2,1)} %param.11) | copy-start | bytes 3145732
  284.9 45.7 %copy-start.11 = (f32[512,1024]{1,0:T(8,128)S(1)}, f32[512,1024]{1,0:T(8,128)}, u32[]{:S(2)}) copy-start(f32[512,1024]{1,0:T(8,128)} %get-tuple-element.34) | copy-start | bytes 6291460
  330.6 4.3 %copy-start.10 = (f32[8,1024]{1,0:T(8,128)S(1)}, f32[8,1024]{1,0:T(8,128)}, u32[]{:S(2)}) copy-start(f32[8,1024]{1,0:T(8,128)} %get-tuple-element.46.gain_b_ref) | copy-start | bytes 98308
  334.9 1.2 copy-start.5
Sparse Core Ops, SparseCore 0:
  10.2 29.6 all-gather.2
  42.0 81.5 all-gather.4
  234.5 100.2 reduce-scatter.1
